TPU v7x, 32 devices: a whole 2x2x4 slice. The times are simulated.
32 devices in a mesh: gx: 8 (over y, x, core), gy: 4 (over z).
Axes of the slice: x: 2, y: 2, z: 4, core: 2. Of those that a mesh axis runs over, the one named last changes fastest.
Arguments:
- tracers: float32 [96, 256, 2, 128], P('gx', 'gy'), may hold values from -6 to 6
- weights: float32 [96, 256, 48], P('gx', 'gy'), may hold values from 0 to 0.5
- offsets: int32 [96, 256, 4], P('gx', 'gy'), may hold values from -2 to 1
- owner: int32 [2, 8], replicated, may hold values from 0 to 7, as said below
- codes: int32 [2, 8], replicated, may hold values from 0 to 3
Outputs:
- updated: float32 [96, 256, 2, 128], P('gx', 'gy')
Inputs may be any that keep to these rules, and one draw needn't show every extreme that they name: owner[0, b] names the column block whose first three rows are glued below block b, owner[1, b] the one whose last three rows are glued above it; each row of owner is a permutation of the 8 blocks, so every block's edge rows are glued to exactly one block on each side. `codes`: bit 0 reverses the glued rows along the columns, bit 1 reverses their order.
All inputs are finite; a program needn't handle non-finite values.
Results may differ from a plain program's by a relative error of at most 0.0003.
Values sent between devices are 32-bit elements; how exact they have to be, the bound alone decides.
No kernel may reach another device: no remote copies, remote signals or barrier semaphores. Data moves between devices by JAX's collectives and lax.ppermute only.
A program may use at most 128 MiB of HBM per device.

v0:
```python
import jax
import jax.numpy as jnp
from jax import lax
from jax.sharding import PartitionSpec as P


def padded(cells, sides, width):
    for axis, dim in sides:
        count = lax.axis_size(axis)
        head = lax.slice_in_dim(cells, 0, width, axis=dim)
        tail = lax.slice_in_dim(cells, cells.shape[dim] - width, cells.shape[dim], axis=dim)
        cells = jnp.concatenate(
            [
                lax.ppermute(tail, axis, [(i, (i + 1) % count) for i in range(count)]),
                cells,
                lax.ppermute(head, axis, [((i + 1) % count, i) for i in range(count)]),
            ],
            axis=dim,
        )
    return cells


def moment_list(extended):
    centre = extended[1:-1, 1:-1]
    east_side = extended[2:, 1:-1]
    west_side = extended[:-2, 1:-1]
    north_side = extended[1:-1, 2:]
    south_side = extended[1:-1, :-2]
    slope_east = 0.5 * (east_side - west_side)
    slope_north = 0.5 * (north_side - south_side)
    curve_east = 0.5 * (east_side - 2.0 * centre + west_side)
    curve_north = 0.5 * (north_side - 2.0 * centre + south_side)
    twist_both = 0.25 * (
        extended[2:, 2:] - extended[2:, :-2] - extended[:-2, 2:] + extended[:-2, :-2]
    )
    return [centre, slope_east, slope_north, curve_east, curve_north, twist_both]


def remap_block(extended, weights, offsets):
    cols_out, rows_out = (weights.shape[0], weights.shape[1])
    levels = offsets.shape[2] // 2
    tracer_count = extended.shape[3]
    moments = moment_list(extended)
    results = []
    for level_index in range(levels):
        shift_col = offsets[:, :, 2 * level_index]
        shift_row = offsets[:, :, 2 * level_index + 1]
        summed = jnp.zeros((cols_out, rows_out, tracer_count), jnp.float32)
        for total_col in range(-2, 3):
            for total_row in range(-2, 3):
                combined = jnp.zeros((cols_out, rows_out, 6), jnp.float32)
                for piece_index in range(4):
                    step_col = piece_index // 2
                    step_row = piece_index % 2
                    hit = (shift_col + step_col == total_col) & (shift_row + step_row == total_row)
                    first_weight = level_index * 24 + piece_index * 6
                    piece_weights = weights[:, :, first_weight : first_weight + 6]
                    combined = combined + jnp.where(hit[:, :, None], piece_weights, 0.0)
                col_start = total_col + 2
                row_start = total_row + 2
                for moment_index in range(6):
                    window = moments[moment_index][
                        col_start : col_start + cols_out,
                        row_start : row_start + rows_out,
                        level_index,
                        :,
                    ]
                    summed = summed + combined[:, :, moment_index : moment_index + 1] * window
        results.append(summed)
    return jnp.stack(results, axis=2)


def orient_strip(strips, owner, codes, side_index, column_index):
    chosen = lax.dynamic_index_in_dim(strips, owner[side_index, column_index], 0, keepdims=False)
    code_value = codes[side_index, column_index]
    chosen = jnp.where(code_value % 2 == 1, chosen[::-1], chosen)
    return jnp.where(code_value // 2 % 2 == 1, chosen[:, ::-1], chosen)


def on_device(tracers, weights, offsets, owner, codes):
    rows_local = tracers.shape[1]
    extended = padded(tracers, (("gx", 0), ("gy", 1)), 3)
    column_index = lax.axis_index("gx")
    row_index = lax.axis_index("gy")
    last_row = lax.axis_size("gy") - 1
    lower_rows = extended[:, 3:6]
    upper_rows = extended[:, rows_local : rows_local + 3]
    own_rows = jnp.where(row_index == 0, lower_rows, upper_rows)
    gathered_rows = lax.all_gather(own_rows[None], "gx", axis=0, tiled=True)
    below = orient_strip(gathered_rows, owner, codes, 0, column_index)
    above = orient_strip(gathered_rows, owner, codes, 1, column_index)
    bottom_rows = jnp.where(row_index == 0, below, extended[:, :3])
    top_rows = jnp.where(row_index == last_row, above, extended[:, rows_local + 3 :])
    extended = jnp.concatenate([bottom_rows, extended[:, 3 : rows_local + 3], top_rows], axis=1)
    return remap_block(extended, weights, offsets)


def solution(mesh):
    in_specs = (P("gx", "gy", None, None), P("gx", "gy", None), P("gx", "gy", None), P(), P())
    out_specs = P("gx", "gy", None, None)
    return jax.shard_map(
        on_device, mesh=mesh, in_specs=in_specs, out_specs=out_specs, check_vma=False
    )
```

profile of v0, /device:TPU:0, one launch (start us, length us, event | category | flops | bytes accessed | tf_op | source)
XLA Modules:
  0.0 167.6 jit_solution(11851460443825078328)
XLA Ops:
  0.0 1.3 copy.20
  1.9 2.9 %collective-permute-start.1 = (f32[3,64,2,128]{3,1,0,2:T(8,128)S(1)}, f32[3,64,2,128]{3,1,0,2:T(8,128)S(1)}, u32[]{:S(2)}, u32[]{:S(2)}) collective-permute-start(f32[3,64,2,128]{3,1,0,2:T(8,128)S(1)} %get-tuple-element.153), channel_id=1, source_target_pairs={{4,0},{8,4},{12,8},{16,12},{20,16},{24,20},{28,24},{0,28},{5,1},{9... | collective-permute-start | bytes 589832 | tf_op jit(solution)/shard_map/ppermute | solution.py:16
  4.8 0.7 constant_dynamic-slice_fusion
  16.0 0.7 slice_bitcast_fusion.397
  20.5 0.7 slice_bitcast_fusion.547
  31.7 0.6 slice_bitcast_fusion.360
  33.6 0.6 slice_bitcast_fusion.553
  40.1 0.6 slice_bitcast_fusion.468
  45.3 0.6 slice_bitcast_fusion.517
  47.9 1.4 constant_dynamic-update-slice_fusion.3
  49.4 4.3 %collective-permute-start.3 = (f32[18,3,2,128]{3,1,0,2:T(4,128)S(1)}, f32[18,3,2,128]{3,1,0,2:T(4,128)S(1)}, u32[]{:S(2)}, u32[]{:S(2)}) collective-permute-start(f32[18,3,2,128]{3,1,0,2:T(4,128)S(1)} %get-tuple-element.147), channel_id=1, source_target_pairs={{1,0},{2,1},{3,2},{0,3},{5,4},{6,5},{7,6},{4,7},{9,8},{10,9},{11,1... | collective-permute-start | bytes 165896 | tf_op jit(solution)/shard_map/ppermute | solution.py:16
  53.8 10.1 %all-gather = f32[144,3,2,128]{3,1,0,2:T(4,128)S(1)} all-gather(f32[18,3,2,128]{3,1,0,2:T(4,128)S(1)} %get-tuple-element.146), channel_id=2, replica_groups=mesh['gx'=8,'gy'=4] {'gx'}, dimensions={0}, use_global_device_ids=true | all-gather | bytes 497664 | tf_op jit(solution)/shard_map/all_gather | solution.py:89
  63.9 1.1 fusion.666
  65.3 5.1 %collective-permute-done.2 = f32[18,3,2,128]{3,1,0,2:T(4,128)} collective-permute-done((f32[18,3,2,128]{3,1,0,2:T(4,128)S(1)}, f32[18,3,2,128]{3,1,0,2:T(4,128)}, u32[]{:S(2)}, u32[]{:S(2)}) %collective-permute-start.2) | collective-permute-done | bytes 55328 | tf_op jit(solution)/shard_map/ppermute | solution.py:14
  70.7 0.7 subtract_multiply_fusion.1
  73.7 1.1 fusion.671
  74.9 2.3 %fusion.673 = (f32[12,64,128]{2,1,0:T(8,128)}, f32[12,64,128]{2,1,0:T(8,128)}, f32[12,64,128]{2,1,0:T(8,128)}, f32[12,64,128]{2,1,0:T(8,128)}, f32[12,64,128]{2,...) fusion(f32[16,68,2,128]{3,1,0,2:T(8,128)S(1)} %get-tuple-elemen, ...), kind=kLoop, calls=%fused_computation.1018 | loop fusion | flops 884736 | bytes 7105536 | tf_op jit(solution)/shard_map/mul | solution.py:68
  77.4 2.4 %fusion.674 = (f32[12,64,128]{2,1,0:T(8,128)}, f32[12,64,128]{2,1,0:T(8,128)}, f32[12,64,128]{2,1,0:T(8,128)}, f32[12,64,128]{2,1,0:T(8,128)}, f32[12,64,128]{2,...) fusion(f32[16,68,2,128]{3,1,0,2:T(8,128)S(1)} %get-tuple-elemen, ...), kind=kLoop, calls=%fused_computation.1020 | loop fusion | flops 884736 | bytes 7105536 | tf_op jit(solution)/shard_map/mul | solution.py:68
  80.0 2.4 %fusion.675 = (f32[12,64,128]{2,1,0:T(8,128)}, f32[12,64,128]{2,1,0:T(8,128)}, f32[12,64,128]{2,1,0:T(8,128)}, f32[12,64,128]{2,1,0:T(8,128)}, f32[12,64,128]{2,...) fusion(f32[16,68,2,128]{3,1,0,2:T(8,128)S(1)} %get-tuple-elemen, ...), kind=kLoop, calls=%fused_computation.1022 | loop fusion | flops 884736 | bytes 7105536 | tf_op jit(solution)/shard_map/mul | solution.py:68
  82.5 2.5 %fusion.676 = (f32[12,64,128]{2,1,0:T(8,128)}, f32[12,64,128]{2,1,0:T(8,128)}, f32[12,64,128]{2,1,0:T(8,128)}, f32[12,64,128]{2,1,0:T(8,128)}, f32[12,64,128]{2,...) fusion(f32[16,68,2,128]{3,1,0,2:T(8,128)S(1)} %get-tuple-elemen, ...), kind=kLoop, calls=%fused_computation.1024 | loop fusion | flops 884736 | bytes 7105536 | tf_op jit(solution)/shard_map/mul | solution.py:68
  85.3 3.2 %fusion.672 = (f32[12,64,128]{2,1,0:T(8,128)}, f32[12,64,128]{2,1,0:T(8,128)}, f32[12,64,128]{2,1,0:T(8,128)}, f32[12,64,128]{2,1,0:T(8,128)}, f32[12,64,128]{2,...) fusion(f32[16,68,2,128]{3,1,0,2:T(8,128)S(1)} %get-tuple-elemen, ...), kind=kLoop, calls=%fused_computation.1016 | loop fusion | flops 884736 | bytes 7105536 | tf_op jit(solution)/shard_map/mul | solution.py:68
  88.9 38.3 %fusion.15 = f32[12,64,128]{2,1,0:T(8,128)} fusion(f32[18,64,2,128]{3,1,0,2:T(8,128)S(1)} %get-tuple-element.216, f32[18,3,2,128]{3,1,0,2:T(4,128)S(1)} %select_select_fusion, f32[16,68,2,128]{3,1,0,2:T(8,128)S(1)} %get-tuple-element.84, f32[16,68,2,128]{3,1,0,2:T(8,128)S(1)} %get-tuple-element.86, f32[16,68,2,128]{3,1,0,2:T(8,128)S(1)} %get-tuple-element.87, ...), kind=kLoop, calls=%fused_computation.101 | loop fusion | flops 28409856 | bytes 53170176 | tf_op jit(solution)/shard_map/add | solution.py:68
  127.2 37.7 %fusion.130 = f32[12,64,128]{2,1,0:T(8,128)} fusion(f32[18,64,2,128]{3,1,0,2:T(8,128)S(1)} %get-tuple-element.216, f32[18,3,2,128]{3,1,0,2:T(4,128)S(1)} %select_select_fusion, f32[16,68,2,128]{3,1,0,2:T(8,128)S(1)} %get-tuple-element.84, f32[16,68,2,128]{3,1,0,2:T(8,128)S(1)} %get-tuple-element.86, f32[16,68,2,128]{3,1,0,2:T(8,128)S(1)} %get-tuple-element.87, ...), kind=kLoop, calls=%fused_computation.216 | loop fusion | flops 28508160 | bytes 53173248 | tf_op jit(solution)/shard_map/add | solution.py:68
  164.9 2.7 %pad_maximum_fusion.1 = f32[12,64,2,128]{3,2,1,0:T(2,128)} fusion(f32[12,64,1,128]{3,2,1,0:T(1,128)} %bitcast.3355, f32[12,64,1,128]{3,2,1,0:T(1,128)} %bitcast.3356), kind=kLoop, calls=%fused_computation.86 | loop fusion | flops 196608 | bytes 1572864 | tf_op jit(solution)/shard_map/stack | solution.py:70
  (280 shorter events, 32.8 us)
Async XLA Ops:
  0.0 4.8 %copy-start.93 = (s32[2,8]{1,0:T(2,128)S(1)}, s32[2,8]{1,0:T(2,128)}, u32[]{:S(2)}) copy-start(s32[2,8]{1,0:T(2,128)} %param.8) | copy-start | bytes 196
  0.0 4.8 %copy-start.94 = (s32[2,8]{1,0:T(2,128)S(1)}, s32[2,8]{1,0:T(2,128)}, u32[]{:S(2)}) copy-start(s32[2,8]{1,0:T(2,128)} %param.9) | copy-start | bytes 196
  0.0 13.3 %copy-start.92 = (s32[12,64,4]{1,2,0:T(4,128)S(1)}, s32[12,64,4]{1,2,0:T(4,128)}, u32[]{:S(2)}) copy-start(s32[12,64,4]{1,2,0:T(4,128)} %param.7) | copy-start | bytes 36868
  0.0 13.4 %copy-start.2 = (f32[12,64,48]{1,2,0:T(8,128)S(1)}, f32[12,64,48]{1,2,0:T(8,128)}, u32[]{:S(2)}) copy-start(f32[12,64,48]{1,2,0:T(8,128)} %param.6) | copy-start | bytes 442372
  1.3 46.5 %collective-permute-start = (f32[3,64,2,128]{3,1,0,2:T(8,128)S(1)}, f32[3,64,2,128]{3,1,0,2:T(8,128)S(1)}, u32[]{:S(2)}, u32[]{:S(2)}) collective-permute-start(f32[3,64,2,128]{3,1,0,2:T(8,128)S(1)} %get-tuple-element.154), channel_id=1, source_target_pairs={{0,4},{4,8},{8,12},{12,16},{16,20},{20,24},{24,28},{28,0},{1,5},{5... | collective-permute-start | bytes 589832 | tf_op jit(solution)/shard_map/ppermute | solution.py:14
  1.9 47.4 %collective-permute-start.1 = (f32[3,64,2,128]{3,1,0,2:T(8,128)S(1)}, f32[3,64,2,128]{3,1,0,2:T(8,128)S(1)}, u32[]{:S(2)}, u32[]{:S(2)}) collective-permute-start(f32[3,64,2,128]{3,1,0,2:T(8,128)S(1)} %get-tuple-element.153), channel_id=1, source_target_pairs={{4,0},{8,4},{12,8},{16,12},{20,16},{24,20},{28,24},{0,28},{5,1},{9... | collective-permute-start | bytes 589832 | tf_op jit(solution)/shard_map/ppermute | solution.py:16
  49.3 15.8 %copy-start = (f32[15,64,2,128]{3,1,0,2:T(8,128)}, f32[15,64,2,128]{3,1,0,2:T(8,128)S(1)}, u32[]{:S(2)}) copy-start(f32[15,64,2,128]{3,1,0,2:T(8,128)S(1)} %get-tuple-element.150) | copy-start | bytes 2949124
  49.3 14.6 %copy-start.42 = (f32[12,64]{1,0:T(8,128)S(1)}, f32[12,64]{1,0:T(8,128)}, u32[]{:S(2)}) copy-start(f32[12,64]{1,0:T(8,128)} %get-tuple-element.379) | copy-start | bytes 9220
  49.3 14.6 %copy-start.51 = (f32[12,64]{1,0:T(8,128)S(1)}, f32[12,64]{1,0:T(8,128)}, u32[]{:S(2)}) copy-start(f32[12,64]{1,0:T(8,128)} %get-tuple-element.229) | copy-start | bytes 9220
  49.4 21.0 %collective-permute-start.3 = (f32[18,3,2,128]{3,1,0,2:T(4,128)S(1)}, f32[18,3,2,128]{3,1,0,2:T(4,128)S(1)}, u32[]{:S(2)}, u32[]{:S(2)}) collective-permute-start(f32[18,3,2,128]{3,1,0,2:T(4,128)S(1)} %get-tuple-element.147), channel_id=1, source_target_pairs={{1,0},{2,1},{3,2},{0,3},{5,4},{6,5},{7,6},{4,7},{9,8},{10,9},{11,1... | collective-permute-start | bytes 165896 | tf_op jit(solution)/shard_map/ppermute | solution.py:16
  63.9 6.5 %collective-permute-start.2 = (f32[18,3,2,128]{3,1,0,2:T(4,128)S(1)}, f32[18,3,2,128]{3,1,0,2:T(4,128)}, u32[]{:S(2)}, u32[]{:S(2)}) collective-permute-start(f32[18,3,2,128]{3,1,0,2:T(4,128)S(1)} %get-tuple-element.145), channel_id=1, source_target_pairs={{0,1},{1,2},{2,3},{3,0},{4,5},{5,6},{6,7},{7,4},{8,9},{9,10},{10,1... | collective-permute-start | bytes 165896 | tf_op jit(solution)/shard_map/ppermute | solution.py:14
  84.9 3.6 %copy-start.4 = (f32[12,64]{1,0:T(8,128)S(1)}, f32[12,64]{1,0:T(8,128)}, u32[]{:S(2)}) copy-start(f32[12,64]{1,0:T(8,128)} %get-tuple-element.367) | copy-start | bytes 9220
  84.9 3.6 %copy-start.5 = (f32[12,64]{1,0:T(8,128)S(1)}, f32[12,64]{1,0:T(8,128)}, u32[]{:S(2)}) copy-start(f32[12,64]{1,0:T(8,128)} %get-tuple-element.397) | copy-start | bytes 9220
  85.0 3.6 %copy-start.6 = (f32[12,64]{1,0:T(8,128)S(1)}, f32[12,64]{1,0:T(8,128)}, u32[]{:S(2)}) copy-start(f32[12,64]{1,0:T(8,128)} %get-tuple-element.398) | copy-start | bytes 9220
  85.0 3.6 %copy-start.7 = (f32[12,64]{1,0:T(8,128)S(1)}, f32[12,64]{1,0:T(8,128)}, u32[]{:S(2)}) copy-start(f32[12,64]{1,0:T(8,128)} %get-tuple-element.511) | copy-start | bytes 9220
  85.0 3.6 %copy-start.8 = (f32[12,64]{1,0:T(8,128)S(1)}, f32[12,64]{1,0:T(8,128)}, u32[]{:S(2)}) copy-start(f32[12,64]{1,0:T(8,128)} %get-tuple-element.512) | copy-start | bytes 9220
  85.0 3.6 %copy-start.9 = (f32[12,64]{1,0:T(8,128)S(1)}, f32[12,64]{1,0:T(8,128)}, u32[]{:S(2)}) copy-start(f32[12,64]{1,0:T(8,128)} %get-tuple-element.513) | copy-start | bytes 9220
  85.0 3.6 %copy-start.10 = (f32[12,64]{1,0:T(8,128)S(1)}, f32[12,64]{1,0:T(8,128)}, u32[]{:S(2)}) copy-start(f32[12,64]{1,0:T(8,128)} %get-tuple-element.514) | copy-start | bytes 9220
  85.0 3.6 %copy-start.11 = (f32[12,64]{1,0:T(8,128)S(1)}, f32[12,64]{1,0:T(8,128)}, u32[]{:S(2)}) copy-start(f32[12,64]{1,0:T(8,128)} %get-tuple-element.515) | copy-start | bytes 9220
  85.0 3.6 %copy-start.12 = (f32[12,64]{1,0:T(8,128)S(1)}, f32[12,64]{1,0:T(8,128)}, u32[]{:S(2)}) copy-start(f32[12,64]{1,0:T(8,128)} %get-tuple-element.516) | copy-start | bytes 9220
  85.0 3.6 %copy-start.13 = (f32[12,64]{1,0:T(8,128)S(1)}, f32[12,64]{1,0:T(8,128)}, u32[]{:S(2)}) copy-start(f32[12,64]{1,0:T(8,128)} %get-tuple-element.505) | copy-start | bytes 9220
  85.0 3.6 %copy-start.14 = (f32[12,64]{1,0:T(8,128)S(1)}, f32[12,64]{1,0:T(8,128)}, u32[]{:S(2)}) copy-start(f32[12,64]{1,0:T(8,128)} %get-tuple-element.506) | copy-start | bytes 9220
  85.0 3.6 %copy-start.15 = (f32[12,64]{1,0:T(8,128)S(1)}, f32[12,64]{1,0:T(8,128)}, u32[]{:S(2)}) copy-start(f32[12,64]{1,0:T(8,128)} %get-tuple-element.507) | copy-start | bytes 9220
  85.1 3.6 %copy-start.16 = (f32[12,64]{1,0:T(8,128)S(1)}, f32[12,64]{1,0:T(8,128)}, u32[]{:S(2)}) copy-start(f32[12,64]{1,0:T(8,128)} %get-tuple-element.508) | copy-start | bytes 9220
  (75 other events, 183.3 us)
where the time goes:
time: 168 us
  other arithmetic  97.2 us (58%)
  local copies, waits for them, and re-layouts  36.7 us (22%)
  between operations  10.6 us (6%)
  blocking collectives  10.1 us (6%)
  starting transfers between devices  7.84 us (5%)
  waiting for transfers between devices  5.1 us (3%)
    add x2, other arithmetic, remap_block(): summed = summed + combined[:, :, moment_index:moment_index + 1] * window  76 us
    mul x50, local copies, waits for them, and re-layouts, remap_block(): summed = summed + combined[:, :, moment_index:moment_index + 1] * window  31.7 us
    mul x10, other arithmetic, remap_block(): summed = summed + combined[:, :, moment_index:moment_index + 1] * window  16.1 us
    all_gather x1, blocking collectives, on_device(): gathered_rows = lax.all_gather(own_rows[None], 'gx', axis=0, tiled=True)  10.1 us
    ppermute x2, starting transfers between devices, padded(): lax.ppermute(head, axis, [((i + 1) % count, i) for i in range(count)])  7.28 us
    ppermute x2, waiting for transfers between devices, padded(): lax.ppermute(tail, axis, [(i, (i + 1) % count) for i in range(count)])  5.1 us
  transfers between devices with their start and end apart: 4, of which 1 were waited for; matrix products, arithmetic and copies ran while one was open for 22% of the time, Pallas kernels for 0%

commit v1 on v0

v1 whole, which is shorter than its diff:
```python
import functools

import jax
import jax.numpy as jnp
import numpy as np
from jax import lax
from jax.experimental import pallas as pl
from jax.experimental.pallas import tpu as pltpu
from jax.sharding import PartitionSpec as P

HALO = 3
BLOCK_X = 4
BLOCK_Y = 16
PITCH = 24
LANES = 128
LEAD = 4
BF16 = jnp.bfloat16
F32 = jnp.float32

STENCILS = [
    {(0, 0): 1.0},
    {(1, 0): 0.5, (-1, 0): -0.5},
    {(0, 1): 0.5, (0, -1): -0.5},
    {(1, 0): 0.5, (0, 0): -1.0, (-1, 0): 0.5},
    {(0, 1): 0.5, (0, 0): -1.0, (0, -1): 0.5},
    {(1, 1): 0.25, (1, -1): -0.25, (-1, 1): -0.25, (-1, -1): 0.25},
]


def spread_matrix(levels):
    terms = 24 * levels
    rows = 2 * terms + 8 * pl.cdiv(2 * levels, 8)
    matrix = np.zeros((rows, 2 * levels * LANES), np.float32)
    for level in range(levels):
        for piece in range(4):
            for moment, stencil in enumerate(STENCILS):
                for (east, north), value in stencil.items():
                    lane = (piece // 2 + 1 + east) * PITCH + piece % 2 + 1 + north
                    row = 24 * level + 6 * piece + moment
                    matrix[row, level * LANES + lane] += value
                    matrix[terms + row, level * LANES + lane] += value
        first = (levels + level) * LANES
        matrix[2 * terms + 2 * level, first : first + LANES] = PITCH
        matrix[2 * terms + 2 * level + 1, first : first + LANES] = 1
    return matrix


def band_kernel(levels, rows, weights_ref, offsets_ref, matrix_ref, band_ref):
    y_blocks = rows // BLOCK_Y
    lane = lax.broadcasted_iota(jnp.int32, (rows, LANES), 1)
    row_in = lax.broadcasted_iota(jnp.int32, (rows, LANES), 0) % BLOCK_Y
    base = lane - row_in - 2 * PITCH - 2
    pad = matrix_ref.shape[0] - 2 * weights_ref.shape[1] - offsets_ref.shape[1]

    def column(x, carry):
        weights = weights_ref[x]
        high = weights.astype(BF16).astype(F32)
        stacked = jnp.concatenate(
            [high, weights - high, offsets_ref[x].astype(F32), jnp.zeros((pad, rows), F32)], axis=0
        ).astype(BF16)
        spread = lax.dot_general(
            stacked, matrix_ref[...], (((0,), (0,)), ((), ())), preferred_element_type=F32
        )
        block, inner = x // BLOCK_X, x % BLOCK_X
        for level in range(levels):
            points = spread[:, level * LANES : (level + 1) * LANES]
            first = (levels + level) * LANES
            shift = spread[:, first : first + LANES].astype(jnp.int32)
            index = base - shift - inner * PITCH
            for part in range(2):
                here = index + part * LANES
                picked = jnp.take_along_axis(
                    points, here & (LANES - 1), axis=1, mode="promise_in_bounds"
                )
                band = jnp.where((here & ~(LANES - 1)) == 0, picked, 0.0)
                top = band.astype(BF16)
                rest = (band - top.astype(F32)).astype(BF16)
                for y in range(y_blocks):
                    slot = (block * y_blocks + y) * levels + level
                    at = pl.multiple_of(inner * BLOCK_Y, BLOCK_Y)
                    lanes = slice(part * LANES, (part + 1) * LANES)
                    mine = slice(y * BLOCK_Y, (y + 1) * BLOCK_Y)
                    band_ref[slot, pl.ds(at, BLOCK_Y), lanes] = top[mine]
                    low = pl.multiple_of(at + BLOCK_X * BLOCK_Y, BLOCK_Y)
                    band_ref[slot, pl.ds(low, BLOCK_Y), lanes] = rest[mine]
        return carry

    lax.fori_loop(0, weights_ref.shape[0], column, 0)


def pack_kernel(cells_ref, edges_ref, inner_ref, outer_ref):
    cols, rows, _ = cells_ref.shape
    width = edges_ref.shape[0] // cols // 2
    even = lax.axis_index("gx") % 2 == 0
    for col in range(cols):
        at = 2 * width * col
        edges_ref[at : at + width] = cells_ref[col, :width]
        edges_ref[at + width : at + 2 * width] = cells_ref[col, rows - width :]
    last = cols - HALO
    for col in range(HALO):
        to = slice(col * rows, (col + 1) * rows)
        inner_ref[to] = cells_ref[jnp.where(even, last + col, col)]
        outer_ref[to] = cells_ref[jnp.where(even, col, last + col)]


def strip_kernel(cols, width, edges_ref, other_ref, message_ref):
    even = lax.axis_index("gx") % 2 == 0
    low = lax.axis_index("gy") == 0
    for col in range(cols):
        at = 2 * width * col
        mine = jnp.where(low, edges_ref[at : at + width], edges_ref[at + width : at + 2 * width])
        theirs = jnp.where(low, other_ref[at : at + width], other_ref[at + width : at + 2 * width])
        message_ref[width * col : width * (col + 1)] = jnp.where(even, mine, theirs)
        to = width * (cols + col)
        message_ref[to : to + width] = jnp.where(even, theirs, mine)
    corner = 2 * width * HALO
    first, last = edges_ref[:corner], edges_ref[2 * width * cols - corner :]
    at = 2 * width * cols
    message_ref[at : at + corner] = jnp.where(even, first, last)
    end = message_ref.shape[0]
    if end > at + corner:
        message_ref[at + corner :] = jnp.zeros((end - at - corner, LANES), F32)


class Window:
    def __init__(self, cols, width, count, run, based, own, got):
        self.cols, self.width, self.total, self.run = cols, width, count * cols, run
        self.count, self.own, self.got = count, own, got
        index = lax.axis_index("gx")
        even = index % 2 == 0
        self.half = run * cols // 2
        self.own_low = jnp.logical_not(even) if based else None
        self.first = jnp.where(even, index - 2, index - 1)

    def start(self, owner):
        return lax.rem((owner - self.first) * self.cols - HALO + 2 * self.total, self.total)

    def column(self, start, step):
        at = start + step
        at = jnp.where(at >= self.total, at - self.total, at)
        held = at < self.run * self.cols
        at = jnp.minimum(at, self.run * self.cols - 1)
        low = at < self.half
        row = jnp.where(low, at, at - self.half) * self.width
        own, got = self.own[pl.ds(row, self.width)], self.got[pl.ds(row, self.width)]
        from_own = low if self.own_low is None else low == self.own_low
        return held, jnp.where(from_own, own, got)


def rows_kernel(cols, width, count, ends, run, based, owner_ref, edges_ref, other_ref, got_ref,
                own_run_ref, got_run_ref, first_ref, second_ref):
    index, place = lax.axis_index("gx"), lax.axis_index("gy")
    even = index % 2 == 0
    flat_place = place % 2 == 0
    corner = 2 * width * cols

    def rows(ref, at, top):
        return jnp.where(top, ref[at + width : at + 2 * width], ref[at : at + width])

    def column(u, top):
        if u < HALO:
            near = rows(other_ref, 2 * width * (cols - HALO + u), top)
            far = rows(got_ref, corner + 2 * width * u, top)
            return jnp.where(even, far, near)
        if u < HALO + cols:
            return rows(edges_ref, 2 * width * (u - HALO), top)
        near = rows(other_ref, 2 * width * (u - HALO - cols), top)
        far = rows(got_ref, corner + 2 * width * (u - HALO - cols), top)
        return jnp.where(even, near, far)

    wide = cols + 2 * HALO
    window = Window(cols, width, count, run, based, own_run_ref, got_run_ref)
    side = jnp.where(place == 0, 0, 1)
    target = lax.rem(index + count // 2, count)
    start = window.start(owner_ref[side, target])
    is_end = jnp.logical_or(place == 0, place == ends - 1)
    for u in range(wide):
        to = slice(u * width, (u + 1) * width)
        first_ref[to] = column(u, flat_place)
        _, glued = window.column(start, u)
        second_ref[to] = jnp.where(is_end, glued, column(u, jnp.logical_not(flat_place)))
    end = first_ref.shape[0]
    if end > wide * width:
        first_ref[wide * width :] = jnp.zeros((end - wide * width, LANES), F32)
        second_ref[wide * width :] = jnp.zeros((end - wide * width, LANES), F32)


def remap_kernel(levels, count, ends, run, based, owner_ref, codes_ref, cells_ref, inner_ref,
                 outer_ref, first_ref, second_ref, own_run_ref, got_run_ref, band_ref, out_ref,
                 field_ref):
    cols, rows, _ = cells_ref.shape
    width = HALO * levels
    lead = LEAD * levels
    index, place = lax.axis_index("gx"), lax.axis_index("gy")
    even = index % 2 == 0
    flat_place = place % 2 == 0
    wide = cols + 2 * HALO

    for col in range(cols):
        field_ref[HALO + col, lead : lead + rows] = cells_ref[col]
    for col in range(HALO):
        inner = inner_ref[col * rows : (col + 1) * rows]
        outer = outer_ref[col * rows : (col + 1) * rows]
        field_ref[col, lead : lead + rows] = jnp.where(even, outer, inner)
        field_ref[HALO + cols + col, lead : lead + rows] = jnp.where(even, inner, outer)

    window = Window(cols, width, count, run, based, own_run_ref, got_run_ref)
    side = jnp.where(place == 0, 0, 1)
    code = codes_ref[side, index]
    start = window.start(owner_ref[side, index])
    is_end = jnp.logical_or(place == 0, place == ends - 1)
    mirrored = jnp.logical_and(is_end, code % 2 == 1)
    flipped = jnp.logical_and(is_end, code // 2 % 2 == 1)
    tail = field_ref.shape[1] - lead - rows - width
    for u in range(wide):
        plain = first_ref[u * width : (u + 1) * width]
        step = jnp.where(mirrored, wide - 1 - u, u)
        held, glued = window.column(start, step)
        come = second_ref[pl.ds(step * width, width)]
        strip = jnp.where(jnp.logical_and(is_end, held), glued, come)
        turned = jnp.concatenate(
            [strip[levels * r : levels * (r + 1)] for r in reversed(range(HALO))], axis=0
        )
        strip = jnp.where(flipped, turned, strip)
        field_ref[u, lead - width : lead] = jnp.where(flat_place, strip, plain)
        field_ref[u, lead + rows : lead + rows + width] = jnp.where(flat_place, plain, strip)
        field_ref[u, lead + rows + width :] = jnp.zeros((tail, LANES), F32)

    x_blocks, y_blocks = cols // BLOCK_X, rows // levels // BLOCK_Y
    size = BLOCK_X * BLOCK_Y
    reach = BLOCK_X + 2 * HALO
    spare = jnp.zeros((2 * LANES - reach * PITCH, LANES), F32)

    def block_row(step, carry):
        y, level = step // levels, step % levels
        begin = (y * BLOCK_Y + LEAD - HALO) * levels + level
        for x in range(x_blocks):
            points = jnp.concatenate(
                [
                    field_ref[x * BLOCK_X + c, pl.ds(begin, PITCH, stride=levels), :]
                    for c in range(reach)
                ]
                + [spare],
                axis=0,
            )
            top = points.astype(BF16)
            rest = (points - top.astype(F32)).astype(BF16)
            band = band_ref[(x * y_blocks + y) * levels + level]
            product = jnp.dot(
                band, jnp.concatenate([top, rest], axis=1), preferred_element_type=F32
            )
            total = product[:size, :LANES] + (product[:size, LANES:] + product[size:, :LANES])
            for c in range(BLOCK_X):
                out_ref[
                    x * BLOCK_X + c, pl.ds(y * BLOCK_Y * levels + level, BLOCK_Y, stride=levels), :
                ] = total[c * BLOCK_Y : (c + 1) * BLOCK_Y]
        return carry

    lax.fori_loop(0, y_blocks * levels, block_row, 0)


VMEM = pl.BlockSpec(memory_space=pltpu.VMEM)
SMEM = pl.BlockSpec(memory_space=pltpu.SMEM)


def shaped(*shape, dtype=F32):
    return jax.ShapeDtypeStruct(shape, dtype)


def eights(rows):
    return 8 * pl.cdiv(rows, 8)


def on_device(tracers, weights, offsets, owner, codes, matrix):
    cols, rows, levels, lanes = tracers.shape
    width = HALO * levels
    count, ends = lax.axis_size("gx"), lax.axis_size("gy")
    axes = ("gx", "gy")
    cells = tracers.reshape(cols, rows * levels, lanes)
    partner = [(i, i ^ 1) for i in range(count)]
    across = [(i, (i + 1) % count if i % 2 else (i - 1) % count) for i in range(count)]
    first_swap = [(i * ends + j, i * ends + (j ^ 1)) for i in range(count) for j in range(ends)]
    second_swap = []
    for i in range(count):
        for j in range(ends):
            if j in (0, ends - 1):
                second_swap.append((i * ends + j, (i + count // 2) % count * ends + j))
            else:
                second_swap.append((i * ends + j, i * ends + (j + 1 if j % 2 else j - 1)))

    edges, inner, outer = pl.pallas_call(
        pack_kernel,
        out_shape=(
            shaped(2 * width * cols, lanes),
            shaped(HALO * rows * levels, lanes),
            shaped(HALO * rows * levels, lanes),
        ),
        in_specs=[VMEM],
        out_specs=(VMEM, VMEM, VMEM),
        name="pack",
    )(cells)
    other = lax.ppermute(edges, "gx", partner)
    inner_got = lax.ppermute(inner, "gx", partner)

    strip_rows = 2 * width * cols
    message = pl.pallas_call(
        functools.partial(strip_kernel, cols, width),
        out_shape=shaped(eights(strip_rows + 2 * width * HALO), lanes),
        in_specs=[VMEM, VMEM],
        out_specs=VMEM,
        name="strip",
    )(edges, other)
    got = lax.ppermute(message, "gx", across)
    outer_got = lax.ppermute(outer, "gx", across)

    run, based = 4, True
    own_run, got_run = message, got
    if count // 2 > run:
        mine, theirs = message[:strip_rows], got[:strip_rows]
        own_run = jnp.where(
            lax.axis_index("gx") % 2 == 0,
            jnp.concatenate([theirs, mine]),
            jnp.concatenate([mine, theirs]),
        )
        based = False
        while True:
            shift = run
            got_run = lax.ppermute(
                own_run, "gx", [((i + shift) % count, i) for i in range(count)]
            )
            run *= 2
            if run >= count // 2:
                break
            own_run = jnp.concatenate([own_run, got_run])

    z_rows = eights(width * (cols + 2 * HALO))
    first, second = pl.pallas_call(
        functools.partial(rows_kernel, cols, width, count, ends, run, based),
        out_shape=(shaped(z_rows, lanes), shaped(z_rows, lanes)),
        in_specs=[SMEM] + [VMEM] * 5,
        out_specs=(VMEM, VMEM),
        name="rows",
    )(owner, edges, other, got, own_run, got_run)
    first_got = lax.ppermute(first, axes, first_swap)
    second_got = lax.ppermute(second, axes, second_swap)

    slots = cols // BLOCK_X * (rows // BLOCK_Y) * levels
    band = pl.pallas_call(
        functools.partial(band_kernel, levels, rows),
        out_shape=shaped(slots, 2 * BLOCK_X * BLOCK_Y, 2 * LANES, dtype=BF16),
        in_specs=[VMEM] * 3,
        out_specs=VMEM,
        name="band",
        cost_estimate=pl.CostEstimate(
            flops=4 * 10**8, bytes_accessed=3 * 10**6, transcendentals=0
        ),
    )(jnp.swapaxes(weights, 1, 2), jnp.swapaxes(offsets, 1, 2), matrix)

    field_rows = eights((LEAD + rows + HALO + PITCH - BLOCK_Y - 2 * HALO) * levels)
    updated = pl.pallas_call(
        functools.partial(remap_kernel, levels, count, ends, run, based),
        out_shape=shaped(cols, rows * levels, lanes),
        in_specs=[SMEM, SMEM] + [VMEM] * 8,
        out_specs=VMEM,
        scratch_shapes=[pltpu.VMEM((cols + 2 * HALO, field_rows, lanes), F32)],
        name="remap",
    )(owner, codes, cells, inner_got, outer_got, first_got, second_got, own_run, got_run, band)
    return updated.reshape(cols, rows, levels, lanes)


def solution(mesh):
    split = P("gx", "gy", None, None)
    in_specs = (split, P("gx", "gy", None), P("gx", "gy", None), P(), P(), P())

    def run(tracers, weights, offsets, owner, codes):
        matrix = jnp.asarray(spread_matrix(tracers.shape[2]), BF16)
        body = jax.shard_map(
            on_device, mesh=mesh, in_specs=in_specs, out_specs=split, check_vma=False
        )
        return body(tracers, weights, offsets, owner, codes, matrix)

    return run
```

time: 168 us -> 31.9 us (0.19)
  other arithmetic: 97.2 us -> 0 us
  local copies, waits for them, and re-layouts: 36.7 us -> 2.59 us
  Pallas kernels: 0 us -> 16.6 us
  between operations: 10.6 us -> 0.05 us
  blocking collectives: 10.1 us -> 0 us
    add x20 -> x0, other arithmetic: 76.9 us -> none  [the longest x2 76 us: remap_block(): summed = summed + combined[:, :, moment_index:moment_index + 1] * window]
    mul x50 -> x0, local copies, waits for them, and re-layouts: 31.7 us -> none  [remap_block(): summed = summed + combined[:, :, moment_index:moment_index + 1] * window]
    mul x11 -> x0, other arithmetic: 16.9 us -> none  [the longest x10 16.1 us: remap_block(): summed = summed + combined[:, :, moment_index:moment_index + 1] * window]
    pallas_call x0 -> x5, Pallas kernels: none -> 16.6 us  [the longest x1 6.41 us: on_device(): pl.pallas_call(functools.partial(band_kernel, levels, rows), out_shape=sh...]
    all_gather x1 -> x0, blocking collectives: 10.1 us -> none  [on_device(): gathered_rows = lax.all_gather(own_rows[None], 'gx', axis=0, tiled=True)]
    another operation x1 -> x0, other arithmetic: 2.69 us -> none  [remap_block(): return jnp.stack(results, axis=2)]
    ppermute x4 -> x6, waiting for transfers between devices: 5.1 us -> 4.8 us  [the longest x1 4.79 us: on_device(): got = lax.ppermute(message, 'gx', across)]
    ppermute x4 -> x6, starting transfers between devices: 7.84 us -> 7.64 us  [the longest x1 3.53 us: on_device(): outer_got = lax.ppermute(outer, 'gx', across)]
  transfers between devices with their start and end apart: 4 -> 6, of which waited for: 1 -> 1; matrix products, arithmetic and copies ran while one was open for 22% -> 0% of each run, Pallas kernels for 0% -> 31%
where the time goes in v1:
time: 31.9 us; the launch traced here: 31.6 us
  Pallas kernels  16.6 us (52%)
  starting transfers between devices  7.64 us (24%)
  waiting for transfers between devices  4.8 us (15%)
  local copies, waits for them, and re-layouts  2.59 us (8%)
    pallas_call x1, Pallas kernels, on_device(): pl.pallas_call(functools.partial(band_kernel, levels, rows), out_shape=sh...  6.41 us
    pallas_call x1, Pallas kernels, on_device(): pl.pallas_call(functools.partial(remap_kernel, levels, count, ends, run,...  4.82 us
    ppermute x1, waiting for transfers between devices, on_device(): got = lax.ppermute(message, 'gx', across)  4.79 us
    ppermute x1, starting transfers between devices, on_device(): outer_got = lax.ppermute(outer, 'gx', across)  3.53 us
    unnamed x12, local copies, waits for them, and re-layouts  2.59 us
    pallas_call x1, Pallas kernels, on_device(): pl.pallas_call(pack_kernel, out_shape=(shaped(2 * width * cols, lanes), s...  1.9 us
    pallas_call x1, Pallas kernels, on_device(): pl.pallas_call(functools.partial(rows_kernel, cols, width, count, ends, r...  1.85 us
    ppermute x1, starting transfers between devices, on_device(): first_got = lax.ppermute(first, axes, first_swap)  1.74 us
  transfers between devices with their start and end apart: 6, of which 1 were waited for; matrix products, arithmetic and copies ran while one was open for 0% of the time, Pallas kernels for 31%

profile of v1, /device:TPU:0, one launch (start us, length us, event | category | flops | bytes accessed | tf_op | source)
XLA Modules:
  0.0 31.6 jit_solution(9264146078591961187)
XLA Ops:
  0.0 1.9 %pack.1 = (f32[144,128]{1,0:T(8,128)}, f32[384,128]{1,0:T(8,128)}, f32[384,128]{1,0:T(8,128)}) custom-call(f32[12,128,128]{2,1,0:T(8,128)} %bitcast.4), custom_call_target="tpu_custom_call" | custom-call | tf_op jit(solution)/shard_map/pack/pallas_call | solution.py:291
  1.9 0.5 %collective-permute-start.2 = (f32[144,128]{1,0:T(8,128)}, f32[144,128]{1,0:T(8,128)S(1)}, u32[]{:S(2)}, u32[]{:S(2)}) collective-permute-start(f32[144,128]{1,0:T(8,128)} %get-tuple-element.12.edges_ref), channel_id=1, source_target_pairs={{0,4},{4,0},{8,12},{12,8},{16,20},{20,16},{24,28},{28,24},{1,5},{5... | collective-permute-start | bytes 221192 | tf_op jit(solution)/shard_map/ppermute | solution.py:302
  2.4 0.0 collective-permute-start
  2.4 3.5 %collective-permute-start.1 = (f32[384,128]{1,0:T(8,128)}, f32[384,128]{1,0:T(8,128)S(1)}, u32[]{:S(2)}, u32[]{:S(2)}) collective-permute-start(f32[384,128]{1,0:T(8,128)} %get-tuple-element.11), channel_id=1, source_target_pairs={{0,28},{4,8},{8,4},{12,16},{16,12},{20,24},{24,20},{28,0},{1,29},{... | collective-permute-start | bytes 589832 | tf_op jit(solution)/shard_map/ppermute | solution.py:314
  5.9 0.0 collective-permute-done.2.other_ref
  6.0 0.6 %copy-done.1 = f32[144,128]{1,0:T(8,128)} copy-done((f32[144,128]{1,0:T(8,128)}, f32[144,128]{1,0:T(8,128)S(1)}, u32[]{:S(2)}) %copy-start.1) | copy-done | bytes 73752
  6.6 1.6 %strip.1.own_run_ref = f32[184,128]{1,0:T(8,128)} custom-call(f32[144,128]{1,0:T(8,128)} %get-tuple-element.12.edges_ref, f32[144,128]{1,0:T(8,128)} %copy-done.1), custom_call_target="tpu_custom_call" | custom-call | tf_op jit(solution)/shard_map/strip/pallas_call | solution.py:306
  8.2 1.1 %collective-permute-start.3 = (f32[184,128]{1,0:T(8,128)}, f32[184,128]{1,0:T(8,128)S(1)}, u32[]{:S(2)}, u32[]{:S(2)}) collective-permute-start(f32[184,128]{1,0:T(8,128)} %strip.1.own_run_ref), channel_id=1, source_target_pairs={{0,28},{4,8},{8,4},{12,16},{16,12},{20,24},{24,20},{28,0},{1,29},{... | collective-permute-start | bytes 282632 | tf_op jit(solution)/shard_map/ppermute | solution.py:313
  9.3 4.8 %collective-permute-done.3.got_ref.got_run_ref = f32[184,128]{1,0:T(8,128)S(1)} collective-permute-done((f32[184,128]{1,0:T(8,128)}, f32[184,128]{1,0:T(8,128)S(1)}, u32[]{:S(2)}, u32[]{:S(2)}) %collective-permute-start.3) | collective-permute-done | bytes 94240 | tf_op jit(solution)/shard_map/ppermute | solution.py:313
  14.1 0.6 %copy-done = f32[184,128]{1,0:T(8,128)} copy-done((f32[184,128]{1,0:T(8,128)}, f32[184,128]{1,0:T(8,128)S(1)}, u32[]{:S(2)}) %copy-start) | copy-done | bytes 94232
  14.7 1.8 %rows.1 = (f32[112,128]{1,0:T(8,128)}, f32[112,128]{1,0:T(8,128)}) custom-call(s32[2,8]{1,0:T(2,128)} %owner_ref.3, f32[144,128]{1,0:T(8,128)} %get-tuple-element.12.edges_ref, f32[144,128]{1,0:T(8,128)} %copy-done.1, f32[184,128]{1,0:T(8,128)} %copy-done, f32[184,128]{1,0:T(8,128)} %strip.1.own_run_ref, f32[184,128]{1,0:T(8,128)} %copy-done), custom_call_target="tpu_custom_call" | custom-call | tf_op jit(solution)/shard_map/rows/pallas_call | solution.py:337
  16.5 1.7 %collective-permute-start.4 = (f32[112,128]{1,0:T(8,128)}, f32[112,128]{1,0:T(8,128)S(1)}, u32[]{:S(2)}, u32[]{:S(2)}) collective-permute-start(f32[112,128]{1,0:T(8,128)} %get-tuple-element.13), channel_id=1, source_target_pairs={{0,1},{1,0},{2,3},{3,2},{4,5},{5,4},{6,7},{7,6},{8,9},{9,8},{10,11... | collective-permute-start | bytes 172040 | tf_op jit(solution)/shard_map/ppermute | solution.py:344
  18.3 0.7 %collective-permute-start.5 = (f32[112,128]{1,0:T(8,128)}, f32[112,128]{1,0:T(8,128)S(1)}, u32[]{:S(2)}, u32[]{:S(2)}) collective-permute-start(f32[112,128]{1,0:T(8,128)} %get-tuple-element.14), channel_id=1, source_target_pairs={{0,16},{1,2},{2,1},{3,19},{4,20},{5,6},{6,5},{7,23},{8,24},{9,10},... | collective-permute-start | bytes 172040 | tf_op jit(solution)/shard_map/ppermute | solution.py:345
  19.0 6.4 %band.1.band_ref = bf16[24,128,256]{2,1,0:T(8,128)(2,1)} custom-call(f32[12,48,64]{2,1,0:T(8,128)} %bitcast.6, s32[12,4,64]{2,1,0:T(4,128)} %bitcast.7, bf16[104,512]{1,0:T(8,128)(2,1)} %constant.2.clone.matrix_ref), custom_call_target="tpu_custom_call" | custom-call | flops 400000000 | bytes 3000000 | tf_op jit(solution)/shard_map/band/pallas_call | solution.py:348
  25.4 0.0 collective-permute-done.inner_ref
  25.4 0.0 collective-permute-done.1.outer_ref
  25.5 0.0 collective-permute-done.4.first_ref
  25.5 0.0 copy-start.4
  25.5 0.0 collective-permute-done.5.second_ref
  25.5 0.6 %copy-done.2 = f32[384,128]{1,0:T(8,128)} copy-done((f32[384,128]{1,0:T(8,128)}, f32[384,128]{1,0:T(8,128)S(1)}, u32[]{:S(2)}) %copy-start.2) | copy-done | bytes 196632
  26.1 0.1 copy-done.3
  26.2 0.0 copy-done.4
  26.2 0.6 %copy-done.5 = f32[112,128]{1,0:T(8,128)} copy-done((f32[112,128]{1,0:T(8,128)}, f32[112,128]{1,0:T(8,128)S(1)}, u32[]{:S(2)}) %copy-start.5) | copy-done | bytes 57368
  26.8 4.8 %remap.1 = f32[12,128,128]{2,1,0:T(8,128)} custom-call(s32[2,8]{1,0:T(2,128)} %owner_ref.3, s32[2,8]{1,0:T(2,128)} %codes_ref.1, f32[12,128,128]{2,1,0:T(8,128)} %bitcast.5, f32[384,128]{1,0:T(8,128)} %copy-done.2, f32[384,128]{1,0:T(8,128)} %copy-done.3, f32[112,128]{1,0:T(8,128)} %copy-done.4, f32[112,128]{1,0:T(8,128)} %copy-done.5, ...), custom_call_target="tpu_custom_call" | custom-call | tf_op jit(solution)/shard_map/remap/pallas_call | solution.py:360
  (5 shorter events, 0.0 us)
Async XLA Ops:
  1.9 4.0 %collective-permute-start.2 = (f32[144,128]{1,0:T(8,128)}, f32[144,128]{1,0:T(8,128)S(1)}, u32[]{:S(2)}, u32[]{:S(2)}) collective-permute-start(f32[144,128]{1,0:T(8,128)} %get-tuple-element.12.edges_ref), channel_id=1, source_target_pairs={{0,4},{4,0},{8,12},{12,8},{16,20},{20,16},{24,28},{28,24},{1,5},{5... | collective-permute-start | bytes 221192 | tf_op jit(solution)/shard_map/ppermute | solution.py:302
  2.4 23.0 %collective-permute-start = (f32[384,128]{1,0:T(8,128)}, f32[384,128]{1,0:T(8,128)S(1)}, u32[]{:S(2)}, u32[]{:S(2)}) collective-permute-start(f32[384,128]{1,0:T(8,128)} %get-tuple-element.10), channel_id=1, source_target_pairs={{0,4},{4,0},{8,12},{12,8},{16,20},{20,16},{24,28},{28,24},{1,5},{5... | collective-permute-start | bytes 589832 | tf_op jit(solution)/shard_map/ppermute | solution.py:303
  2.4 23.0 %collective-permute-start.1 = (f32[384,128]{1,0:T(8,128)}, f32[384,128]{1,0:T(8,128)S(1)}, u32[]{:S(2)}, u32[]{:S(2)}) collective-permute-start(f32[384,128]{1,0:T(8,128)} %get-tuple-element.11), channel_id=1, source_target_pairs={{0,28},{4,8},{8,4},{12,16},{16,12},{20,24},{24,20},{28,0},{1,29},{... | collective-permute-start | bytes 589832 | tf_op jit(solution)/shard_map/ppermute | solution.py:314
  5.9 0.6 %copy-start.1 = (f32[144,128]{1,0:T(8,128)}, f32[144,128]{1,0:T(8,128)S(1)}, u32[]{:S(2)}) copy-start(f32[144,128]{1,0:T(8,128)S(1)} %collective-permute-done.2.other_ref) | copy-start | bytes 221188
  8.2 5.9 %collective-permute-start.3 = (f32[184,128]{1,0:T(8,128)}, f32[184,128]{1,0:T(8,128)S(1)}, u32[]{:S(2)}, u32[]{:S(2)}) collective-permute-start(f32[184,128]{1,0:T(8,128)} %strip.1.own_run_ref), channel_id=1, source_target_pairs={{0,28},{4,8},{8,4},{12,16},{16,12},{20,24},{24,20},{28,0},{1,29},{... | collective-permute-start | bytes 282632 | tf_op jit(solution)/shard_map/ppermute | solution.py:313
  14.1 0.6 %copy-start = (f32[184,128]{1,0:T(8,128)}, f32[184,128]{1,0:T(8,128)S(1)}, u32[]{:S(2)}) copy-start(f32[184,128]{1,0:T(8,128)S(1)} %collective-permute-done.3.got_ref.got_run_ref) | copy-start | bytes 282628
  16.5 8.9 %collective-permute-start.4 = (f32[112,128]{1,0:T(8,128)}, f32[112,128]{1,0:T(8,128)S(1)}, u32[]{:S(2)}, u32[]{:S(2)}) collective-permute-start(f32[112,128]{1,0:T(8,128)} %get-tuple-element.13), channel_id=1, source_target_pairs={{0,1},{1,0},{2,3},{3,2},{4,5},{5,4},{6,7},{7,6},{8,9},{9,8},{10,11... | collective-permute-start | bytes 172040 | tf_op jit(solution)/shard_map/ppermute | solution.py:344
  18.3 7.2 %collective-permute-start.5 = (f32[112,128]{1,0:T(8,128)}, f32[112,128]{1,0:T(8,128)S(1)}, u32[]{:S(2)}, u32[]{:S(2)}) collective-permute-start(f32[112,128]{1,0:T(8,128)} %get-tuple-element.14), channel_id=1, source_target_pairs={{0,16},{1,2},{2,1},{3,19},{4,20},{5,6},{6,5},{7,23},{8,24},{9,10},... | collective-permute-start | bytes 172040 | tf_op jit(solution)/shard_map/ppermute | solution.py:345
  25.4 0.7 %copy-start.2 = (f32[384,128]{1,0:T(8,128)}, f32[384,128]{1,0:T(8,128)S(1)}, u32[]{:S(2)}) copy-start(f32[384,128]{1,0:T(8,128)S(1)} %collective-permute-done.inner_ref) | copy-start | bytes 589828
  25.4 0.7 %copy-start.3 = (f32[384,128]{1,0:T(8,128)}, f32[384,128]{1,0:T(8,128)S(1)}, u32[]{:S(2)}) copy-start(f32[384,128]{1,0:T(8,128)S(1)} %collective-permute-done.1.outer_ref) | copy-start | bytes 589828
  25.5 0.7 %copy-start.4 = (f32[112,128]{1,0:T(8,128)}, f32[112,128]{1,0:T(8,128)S(1)}, u32[]{:S(2)}) copy-start(f32[112,128]{1,0:T(8,128)S(1)} %collective-permute-done.4.first_ref) | copy-start | bytes 172036
  26.2 0.6 %copy-start.5 = (f32[112,128]{1,0:T(8,128)}, f32[112,128]{1,0:T(8,128)S(1)}, u32[]{:S(2)}) copy-start(f32[112,128]{1,0:T(8,128)S(1)} %collective-permute-done.5.second_ref) | copy-start | bytes 172036

commit v2 on v1

--- a/solution.py
+++ b/solution.py
@@ -14,6 +14,7 @@
 PITCH = 24
 LANES = 128
 LEAD = 4
+UNROLL = 4
 BF16 = jnp.bfloat16
 F32 = jnp.float32
 
@@ -45,14 +46,63 @@
     return matrix
 
 
-def band_kernel(levels, rows, weights_ref, offsets_ref, matrix_ref, band_ref):
+def columns_kernel(cells_ref, after_ref, inner_ref, outer_ref, sems):
+    del after_ref
+    even = lax.axis_index("gx") % 2 == 0
+    last = cells_ref.shape[0] - HALO
+    copies = [
+        pltpu.make_async_copy(
+            cells_ref.at[pl.ds(jnp.where(even, last, 0), HALO)], inner_ref, sems.at[0]
+        ),
+        pltpu.make_async_copy(
+            cells_ref.at[pl.ds(jnp.where(even, 0, last), HALO)], outer_ref, sems.at[1]
+        ),
+    ]
+    for copy in copies:
+        copy.start()
+    for copy in copies:
+        copy.wait()
+
+
+def band_kernel(levels, rows, count, ends, run, based, owner_ref, codes_ref, weights_hbm, offsets_hbm,
+                matrix_hbm, after_ref, band_ref, table_ref, weights_ref, offsets_ref, matrix_ref, sems):
+    del after_ref
+    cols = weights_ref.shape[0]
+    groups = cols // UNROLL
+
+    def fetch(group):
+        part = pl.ds(group * UNROLL, UNROLL)
+        return pltpu.make_async_copy(weights_hbm.at[part], weights_ref.at[part], sems.at[group])
+
+    others = [
+        pltpu.make_async_copy(offsets_hbm, offsets_ref, sems.at[groups]),
+        pltpu.make_async_copy(matrix_hbm, matrix_ref, sems.at[groups + 1]),
+    ]
+    fetch(0).start()
+    for copy in others:
+        copy.start()
+    for group in range(1, groups):
+        fetch(group).start()
+
+    index, place = lax.axis_index("gx"), lax.axis_index("gy")
+    side = jnp.where(place == 0, 0, 1)
+    window = Window(cols, 0, count, run, based, None, None)
+    target = lax.rem(index + count // 2, count)
+    is_end = jnp.logical_or(place == 0, place == ends - 1)
+    code = jnp.where(is_end, codes_ref[side, index], 0)
+    lines = [window.start(owner_ref[side, target]), window.start(owner_ref[side, index]), code]
+    for at, line in enumerate(lines):
+        table_ref[at : at + 1] = jnp.full((1, LANES), line, jnp.int32)
+    for copy in others:
+        copy.wait()
+
     y_blocks = rows // BLOCK_Y
     lane = lax.broadcasted_iota(jnp.int32, (rows, LANES), 1)
     row_in = lax.broadcasted_iota(jnp.int32, (rows, LANES), 0) % BLOCK_Y
     base = lane - row_in - 2 * PITCH - 2
     pad = matrix_ref.shape[0] - 2 * weights_ref.shape[1] - offsets_ref.shape[1]
 
-    def column(x, carry):
+    def column(x):
         weights = weights_ref[x]
         high = weights.astype(BF16).astype(F32)
         stacked = jnp.concatenate(
@@ -62,48 +112,57 @@
             stacked, matrix_ref[...], (((0,), (0,)), ((), ())), preferred_element_type=F32
         )
         block, inner = x // BLOCK_X, x % BLOCK_X
+        at = pl.multiple_of(inner * BLOCK_Y, BLOCK_Y)
+        low = pl.multiple_of(at + BLOCK_X * BLOCK_Y, BLOCK_Y)
         for level in range(levels):
             points = spread[:, level * LANES : (level + 1) * LANES]
             first = (levels + level) * LANES
             shift = spread[:, first : first + LANES].astype(jnp.int32)
-            index = base - shift - inner * PITCH
-            for part in range(2):
-                here = index + part * LANES
+            for y in range(y_blocks):
+                mine = slice(y * BLOCK_Y, (y + 1) * BLOCK_Y)
+                index = base[mine] - shift[mine] - inner * PITCH
                 picked = jnp.take_along_axis(
-                    points, here & (LANES - 1), axis=1, mode="promise_in_bounds"
+                    points[mine], index & (LANES - 1), axis=1, mode="promise_in_bounds"
                 )
-                band = jnp.where((here & ~(LANES - 1)) == 0, picked, 0.0)
-                top = band.astype(BF16)
-                rest = (band - top.astype(F32)).astype(BF16)
-                for y in range(y_blocks):
-                    slot = (block * y_blocks + y) * levels + level
-                    at = pl.multiple_of(inner * BLOCK_Y, BLOCK_Y)
+                top = picked.astype(BF16).astype(F32)
+                rest = picked - top
+                here = index >= 0
+                slot = (block * y_blocks + y) * levels + level
+                for part in range(2):
                     lanes = slice(part * LANES, (part + 1) * LANES)
-                    mine = slice(y * BLOCK_Y, (y + 1) * BLOCK_Y)
-                    band_ref[slot, pl.ds(at, BLOCK_Y), lanes] = top[mine]
-                    low = pl.multiple_of(at + BLOCK_X * BLOCK_Y, BLOCK_Y)
-                    band_ref[slot, pl.ds(low, BLOCK_Y), lanes] = rest[mine]
+                    keep = here if part == 0 else jnp.logical_not(here)
+                    band_ref[slot, pl.ds(at, BLOCK_Y), lanes] = jnp.where(keep, top, 0.0).astype(BF16)
+                    band_ref[slot, pl.ds(low, BLOCK_Y), lanes] = jnp.where(keep, rest, 0.0).astype(BF16)
+
+    def group_of(group, carry):
+        fetch(group).wait()
+        for step in range(UNROLL):
+            column(group * UNROLL + step)
         return carry
 
-    lax.fori_loop(0, weights_ref.shape[0], column, 0)
-
-
-def pack_kernel(cells_ref, edges_ref, inner_ref, outer_ref):
+    lax.fori_loop(0, groups, group_of, 0)
+
+
+def pack_kernel(cells_ref, edges_ref, low_ref, high_ref, sems):
     cols, rows, _ = cells_ref.shape
     width = edges_ref.shape[0] // cols // 2
-    even = lax.axis_index("gx") % 2 == 0
+    deep = low_ref.shape[1]
+    copies = [
+        pltpu.make_async_copy(cells_ref.at[:, pl.ds(0, deep)], low_ref, sems.at[0]),
+        pltpu.make_async_copy(cells_ref.at[:, pl.ds(rows - deep, deep)], high_ref, sems.at[1]),
+    ]
+    for copy in copies:
+        copy.start()
+    for copy in copies:
+        copy.wait()
     for col in range(cols):
         at = 2 * width * col
-        edges_ref[at : at + width] = cells_ref[col, :width]
-        edges_ref[at + width : at + 2 * width] = cells_ref[col, rows - width :]
-    last = cols - HALO
-    for col in range(HALO):
-        to = slice(col * rows, (col + 1) * rows)
-        inner_ref[to] = cells_ref[jnp.where(even, last + col, col)]
-        outer_ref[to] = cells_ref[jnp.where(even, col, last + col)]
-
-
-def strip_kernel(cols, width, edges_ref, other_ref, message_ref):
+        edges_ref[at : at + width] = low_ref[col, :width]
+        edges_ref[at + width : at + 2 * width] = high_ref[col, deep - width :]
+
+
+def strip_kernel(cols, width, edges_ref, other_ref, after_ref, message_ref):
+    del after_ref
     even = lax.axis_index("gx") % 2 == 0
     low = lax.axis_index("gy") == 0
     for col in range(cols):
@@ -147,10 +206,10 @@
         return held, jnp.where(from_own, own, got)
 
 
-def rows_kernel(cols, width, count, ends, run, based, owner_ref, edges_ref, other_ref, got_ref,
-                own_run_ref, got_run_ref, first_ref, second_ref):
-    index, place = lax.axis_index("gx"), lax.axis_index("gy")
-    even = index % 2 == 0
+def rows_kernel(cols, width, count, ends, run, based, table_ref, edges_ref, other_ref, got_ref,
+                own_run_ref, got_run_ref, after_ref, first_ref, second_ref):
+    del after_ref
+    even, place = lax.axis_index("gx") % 2 == 0, lax.axis_index("gy")
     flat_place = place % 2 == 0
     corner = 2 * width * cols
 
@@ -170,9 +229,7 @@
 
     wide = cols + 2 * HALO
     window = Window(cols, width, count, run, based, own_run_ref, got_run_ref)
-    side = jnp.where(place == 0, 0, 1)
-    target = lax.rem(index + count // 2, count)
-    start = window.start(owner_ref[side, target])
+    start = table_ref[0:1, 0:1][0, 0]
     is_end = jnp.logical_or(place == 0, place == ends - 1)
     for u in range(wide):
         to = slice(u * width, (u + 1) * width)
@@ -185,32 +242,79 @@
         second_ref[wide * width :] = jnp.zeros((end - wide * width, LANES), F32)
 
 
-def remap_kernel(levels, count, ends, run, based, owner_ref, codes_ref, cells_ref, inner_ref,
-                 outer_ref, first_ref, second_ref, own_run_ref, got_run_ref, band_ref, out_ref,
-                 field_ref):
+def block_sum(field_ref, band_ref, x, y, y_blocks, levels, level):
+    size = BLOCK_X * BLOCK_Y
+    reach = BLOCK_X + 2 * HALO
+    begin = (y * BLOCK_Y + LEAD - HALO) * levels + level
+    points = jnp.concatenate(
+        [
+            field_ref[x * BLOCK_X + c, pl.ds(begin, PITCH, stride=levels), :]
+            for c in range(reach)
+        ]
+        + [jnp.zeros((2 * LANES - reach * PITCH, LANES), F32)],
+        axis=0,
+    )
+    top = points.astype(BF16)
+    rest = (points - top.astype(F32)).astype(BF16)
+    band = band_ref[(x * y_blocks + y) * levels + level]
+    product = jnp.dot(band, jnp.concatenate([top, rest], axis=1), preferred_element_type=F32)
+    return product[:size, :LANES] + (product[:size, LANES:] + product[size:, :LANES])
+
+
+def remap_rows(field_ref, band_ref, stage_ref, out_ref, sems, levels, y_blocks, which):
+    x_blocks = stage_ref.shape[1] // BLOCK_X
+    deep = BLOCK_Y * levels
+    copies = []
+    for at, y in enumerate(which):
+        for level in range(levels):
+            for x in range(x_blocks):
+                total = block_sum(field_ref, band_ref, x, y, y_blocks, levels, level)
+                for c in range(BLOCK_X):
+                    stage_ref[at, x * BLOCK_X + c, pl.ds(level, BLOCK_Y, stride=levels), :] = total[
+                        c * BLOCK_Y : (c + 1) * BLOCK_Y
+                    ]
+        copies.append(
+            pltpu.make_async_copy(
+                stage_ref.at[at], out_ref.at[:, pl.ds(y * deep, deep)], sems.at[at]
+            )
+        )
+        copies[-1].start()
+    for copy in copies:
+        copy.wait()
+
+
+def middle_kernel(levels, cells_ref, inner_ref, outer_ref, band_ref, after_ref, out_ref, field_ref,
+                  stage_ref, sems):
+    del after_ref
     cols, rows, _ = cells_ref.shape
-    width = HALO * levels
     lead = LEAD * levels
-    index, place = lax.axis_index("gx"), lax.axis_index("gy")
-    even = index % 2 == 0
-    flat_place = place % 2 == 0
-    wide = cols + 2 * HALO
-
+    even = lax.axis_index("gx") % 2 == 0
     for col in range(cols):
         field_ref[HALO + col, lead : lead + rows] = cells_ref[col]
     for col in range(HALO):
-        inner = inner_ref[col * rows : (col + 1) * rows]
-        outer = outer_ref[col * rows : (col + 1) * rows]
+        inner, outer = inner_ref[col], outer_ref[col]
         field_ref[col, lead : lead + rows] = jnp.where(even, outer, inner)
         field_ref[HALO + cols + col, lead : lead + rows] = jnp.where(even, inner, outer)
-
+    y_blocks = rows // levels // BLOCK_Y
+    remap_rows(
+        field_ref, band_ref, stage_ref, out_ref, sems, levels, y_blocks, range(1, y_blocks - 1)
+    )
+
+
+def edge_kernel(levels, cols, rows, count, ends, run, based, table_ref, first_ref, second_ref,
+                own_run_ref, got_run_ref, band_ref, field_in, out_in, field_ref, out_ref,
+                stage_ref, sems):
+    del field_in, out_in
+    width = HALO * levels
+    lead = LEAD * levels
+    place = lax.axis_index("gy")
+    flat_place = place % 2 == 0
+    wide = cols + 2 * HALO
     window = Window(cols, width, count, run, based, own_run_ref, got_run_ref)
-    side = jnp.where(place == 0, 0, 1)
-    code = codes_ref[side, index]
-    start = window.start(owner_ref[side, index])
+    start, code = table_ref[1:2, 0:1][0, 0], table_ref[2:3, 0:1][0, 0]
     is_end = jnp.logical_or(place == 0, place == ends - 1)
-    mirrored = jnp.logical_and(is_end, code % 2 == 1)
-    flipped = jnp.logical_and(is_end, code // 2 % 2 == 1)
+    mirrored = code % 2 == 1
+    flipped = code // 2 % 2 == 1
     tail = field_ref.shape[1] - lead - rows - width
     for u in range(wide):
         plain = first_ref[u * width : (u + 1) * width]
@@ -225,41 +329,29 @@
         field_ref[u, lead - width : lead] = jnp.where(flat_place, strip, plain)
         field_ref[u, lead + rows : lead + rows + width] = jnp.where(flat_place, plain, strip)
         field_ref[u, lead + rows + width :] = jnp.zeros((tail, LANES), F32)
-
-    x_blocks, y_blocks = cols // BLOCK_X, rows // levels // BLOCK_Y
-    size = BLOCK_X * BLOCK_Y
-    reach = BLOCK_X + 2 * HALO
-    spare = jnp.zeros((2 * LANES - reach * PITCH, LANES), F32)
-
-    def block_row(step, carry):
-        y, level = step // levels, step % levels
-        begin = (y * BLOCK_Y + LEAD - HALO) * levels + level
-        for x in range(x_blocks):
-            points = jnp.concatenate(
-                [
-                    field_ref[x * BLOCK_X + c, pl.ds(begin, PITCH, stride=levels), :]
-                    for c in range(reach)
-                ]
-                + [spare],
-                axis=0,
-            )
-            top = points.astype(BF16)
-            rest = (points - top.astype(F32)).astype(BF16)
-            band = band_ref[(x * y_blocks + y) * levels + level]
-            product = jnp.dot(
-                band, jnp.concatenate([top, rest], axis=1), preferred_element_type=F32
-            )
-            total = product[:size, :LANES] + (product[:size, LANES:] + product[size:, :LANES])
-            for c in range(BLOCK_X):
-                out_ref[
-                    x * BLOCK_X + c, pl.ds(y * BLOCK_Y * levels + level, BLOCK_Y, stride=levels), :
-                ] = total[c * BLOCK_Y : (c + 1) * BLOCK_Y]
-        return carry
-
-    lax.fori_loop(0, y_blocks * levels, block_row, 0)
+    y_blocks = rows // levels // BLOCK_Y
+    remap_rows(
+        field_ref, band_ref, stage_ref, out_ref, sems, levels, y_blocks, (0, y_blocks - 1)
+    )
+
+
+def grant(mebibytes):
+    return pltpu.CompilerParams(vmem_limit_bytes=mebibytes << 20)
+
+
+def takes(microseconds):
+    return pl.CostEstimate(
+        flops=0, bytes_accessed=int(microseconds * 3_000_000), transcendentals=0
+    )
+
+
+def in_hbm(array):
+    return pltpu.with_memory_space_constraint(array, pltpu.HBM)
 
 
 VMEM = pl.BlockSpec(memory_space=pltpu.VMEM)
+HBM = pl.BlockSpec(memory_space=pltpu.HBM)
+ANY = pl.BlockSpec(memory_space=pl.ANY)
 SMEM = pl.BlockSpec(memory_space=pltpu.SMEM)
 
 
@@ -288,30 +380,48 @@
             else:
                 second_swap.append((i * ends + j, i * ends + (j + 1 if j % 2 else j - 1)))
 
-    edges, inner, outer = pl.pallas_call(
+    deep = eights(width)
+    edges = pl.pallas_call(
         pack_kernel,
-        out_shape=(
-            shaped(2 * width * cols, lanes),
-            shaped(HALO * rows * levels, lanes),
-            shaped(HALO * rows * levels, lanes),
-        ),
-        in_specs=[VMEM],
-        out_specs=(VMEM, VMEM, VMEM),
+        out_shape=shaped(2 * width * cols, lanes),
+        in_specs=[HBM],
+        out_specs=VMEM,
+        scratch_shapes=[
+            pltpu.VMEM((cols, deep, lanes), F32),
+            pltpu.VMEM((cols, deep, lanes), F32),
+            pltpu.SemaphoreType.DMA((2,)),
+        ],
         name="pack",
-    )(cells)
+        compiler_params=grant(4),
+        cost_estimate=takes(1.0),
+    )(in_hbm(cells))
     other = lax.ppermute(edges, "gx", partner)
-    inner_got = lax.ppermute(inner, "gx", partner)
+
+    columns = shaped(HALO, rows * levels, lanes)
+    inner, outer = pl.pallas_call(
+        columns_kernel,
+        out_shape=(columns, columns),
+        in_specs=[HBM, ANY],
+        out_specs=(VMEM, VMEM),
+        scratch_shapes=[pltpu.SemaphoreType.DMA((2,))],
+        name="columns",
+        compiler_params=grant(4),
+        cost_estimate=takes(0.5),
+    )(in_hbm(cells), edges)
 
     strip_rows = 2 * width * cols
     message = pl.pallas_call(
         functools.partial(strip_kernel, cols, width),
         out_shape=shaped(eights(strip_rows + 2 * width * HALO), lanes),
-        in_specs=[VMEM, VMEM],
+        in_specs=[VMEM, VMEM, ANY],
         out_specs=VMEM,
         name="strip",
-    )(edges, other)
+        cost_estimate=takes(1.0),
+        compiler_params=grant(4),
+    )(edges, other, inner)
     got = lax.ppermute(message, "gx", across)
     outer_got = lax.ppermute(outer, "gx", across)
+    inner_got = lax.ppermute(inner, "gx", partner)
 
     run, based = 4, True
     own_run, got_run = message, got
@@ -333,44 +443,77 @@
                 break
             own_run = jnp.concatenate([own_run, got_run])
 
+    weights = jnp.swapaxes(weights, 1, 2)
+    offsets = jnp.swapaxes(offsets, 1, 2)
+    y_blocks = rows // BLOCK_Y
+    slots = cols // BLOCK_X * y_blocks * levels
+    band, table = pl.pallas_call(
+        functools.partial(band_kernel, levels, rows, count, ends, run, based),
+        out_shape=(
+            shaped(slots, 2 * BLOCK_X * BLOCK_Y, 2 * LANES, dtype=BF16),
+            shaped(8, lanes, dtype=jnp.int32),
+        ),
+        in_specs=[SMEM, SMEM] + [HBM] * 3 + [ANY],
+        out_specs=(VMEM, VMEM),
+        scratch_shapes=[
+            pltpu.VMEM(weights.shape, F32),
+            pltpu.VMEM(offsets.shape, jnp.int32),
+            pltpu.VMEM(matrix.shape, BF16),
+            pltpu.SemaphoreType.DMA((cols // UNROLL + 2,)),
+        ],
+        name="band",
+        compiler_params=grant(6),
+        cost_estimate=takes(3.0),
+    )(*[in_hbm(a) for a in (owner, codes, weights, offsets, matrix)], message)
+
     z_rows = eights(width * (cols + 2 * HALO))
     first, second = pl.pallas_call(
         functools.partial(rows_kernel, cols, width, count, ends, run, based),
         out_shape=(shaped(z_rows, lanes), shaped(z_rows, lanes)),
-        in_specs=[SMEM] + [VMEM] * 5,
+        in_specs=[VMEM] * 6 + [ANY],
         out_specs=(VMEM, VMEM),
         name="rows",
-    )(owner, edges, other, got, own_run, got_run)
+        cost_estimate=takes(1.0),
+        compiler_params=grant(2),
+    )(table, edges, other, got, own_run, got_run, band)
     first_got = lax.ppermute(first, axes, first_swap)
     second_got = lax.ppermute(second, axes, second_swap)
 
-    slots = cols // BLOCK_X * (rows // BLOCK_Y) * levels
-    band = pl.pallas_call(
-        functools.partial(band_kernel, levels, rows),
-        out_shape=shaped(slots, 2 * BLOCK_X * BLOCK_Y, 2 * LANES, dtype=BF16),
-        in_specs=[VMEM] * 3,
-        out_specs=VMEM,
-        name="band",
-        cost_estimate=pl.CostEstimate(
-            flops=4 * 10**8, bytes_accessed=3 * 10**6, transcendentals=0
-        ),
-    )(jnp.swapaxes(weights, 1, 2), jnp.swapaxes(offsets, 1, 2), matrix)
-
     field_rows = eights((LEAD + rows + HALO + PITCH - BLOCK_Y - 2 * HALO) * levels)
-    updated = pl.pallas_call(
-        functools.partial(remap_kernel, levels, count, ends, run, based),
-        out_shape=shaped(cols, rows * levels, lanes),
-        in_specs=[SMEM, SMEM] + [VMEM] * 8,
-        out_specs=VMEM,
-        scratch_shapes=[pltpu.VMEM((cols + 2 * HALO, field_rows, lanes), F32)],
-        name="remap",
-    )(owner, codes, cells, inner_got, outer_got, first_got, second_got, own_run, got_run, band)
+    field_shape = shaped(cols + 2 * HALO, field_rows, lanes)
+    out_shape = shaped(cols, rows * levels, lanes)
+    stage = (cols, BLOCK_Y * levels, lanes)
+    partial, field = pl.pallas_call(
+        functools.partial(middle_kernel, levels),
+        out_shape=(out_shape, field_shape),
+        in_specs=[VMEM] * 4 + [ANY],
+        out_specs=(HBM, VMEM),
+        scratch_shapes=[
+            pltpu.VMEM((y_blocks - 2, *stage), F32),
+            pltpu.SemaphoreType.DMA((y_blocks - 2,)),
+        ],
+        name="middle",
+        cost_estimate=takes(2.0),
+        compiler_params=grant(6),
+    )(cells, inner_got, outer_got, band, first)
+    _, updated = pl.pallas_call(
+        functools.partial(edge_kernel, levels, cols, rows * levels, count, ends, run, based),
+        out_shape=(field_shape, out_shape),
+        in_specs=[VMEM] * 7 + [HBM],
+        out_specs=(VMEM, HBM),
+        scratch_shapes=[pltpu.VMEM((2, *stage), F32), pltpu.SemaphoreType.DMA((2,))],
+        input_output_aliases={6: 0, 7: 1},
+        name="edge",
+        cost_estimate=takes(2.0),
+        compiler_params=grant(6),
+    )(table, first_got, second_got, own_run, got_run, band, field, partial)
     return updated.reshape(cols, rows, levels, lanes)
 
 
 def solution(mesh):
     split = P("gx", "gy", None, None)
     in_specs = (split, P("gx", "gy", None), P("gx", "gy", None), P(), P(), P())
+
 
     def run(tracers, weights, offsets, owner, codes):
         matrix = jnp.asarray(spread_matrix(tracers.shape[2]), BF16)

time: 31.9 us -> 20.1 us (0.63)
  Pallas kernels: 16.6 us -> 7.49 us
  local copies, waits for them, and re-layouts: 2.59 us -> 0.01 us
  waiting for transfers between devices: 4.8 us -> 4.01 us
  starting transfers between devices: 7.64 us -> 8.31 us
    pallas_call x3 -> x5, Pallas kernels: 13.1 us -> 7.32 us  [the longest x1 3.07 us: on_device(): pl.pallas_call(functools.partial(band_kernel, levels, rows, count, ends,...]
    unnamed x12 -> x2, local copies, waits for them, and re-layouts: 2.59 us -> 0.01 us
    ppermute x1, waiting for transfers between devices: 4.79 us -> 2.82 us  [on_device(): got = lax.ppermute(message, 'gx', across)]
    pallas_call x1, Pallas kernels: 1.85 us -> 0.14 us  [on_device(): pl.pallas_call(functools.partial(rows_kernel, cols, width, count, ends, r...]
    pallas_call x1, Pallas kernels: 1.58 us -> 0.03 us  [on_device(): pl.pallas_call(functools.partial(strip_kernel, cols, width), out_shape=sh...]
    ppermute x1, waiting for transfers between devices: 0.01 us -> 1.18 us  [on_device(): first_got = lax.ppermute(first, axes, first_swap)]
    ppermute x1, starting transfers between devices: 0.75 us -> 1.61 us  [on_device(): second_got = lax.ppermute(second, axes, second_swap)]
    ppermute x1, starting transfers between devices: 1.12 us -> 0.71 us  [on_device(): got = lax.ppermute(message, 'gx', across)]
  transfers between devices with their start and end apart: 6 -> 6, of which waited for: 1 -> 2; matrix products, arithmetic and copies ran while one was open for 0% -> 0% of each run, Pallas kernels for 31% -> 27%
where the time goes in v2:
time: 20.1 us; the launch traced here: 19.9 us
  starting transfers between devices  8.31 us (41%)
  Pallas kernels  7.49 us (37%)
  waiting for transfers between devices  4.01 us (20%)
    ppermute x1, starting transfers between devices, on_device(): outer_got = lax.ppermute(outer, 'gx', across)  3.61 us
    pallas_call x1, Pallas kernels, on_device(): pl.pallas_call(functools.partial(band_kernel, levels, rows, count, ends,...  3.07 us
    ppermute x1, waiting for transfers between devices, on_device(): got = lax.ppermute(message, 'gx', across)  2.82 us
    ppermute x1, starting transfers between devices, on_device(): first_got = lax.ppermute(first, axes, first_swap)  1.82 us
    ppermute x1, starting transfers between devices, on_device(): second_got = lax.ppermute(second, axes, second_swap)  1.61 us
    pallas_call x1, Pallas kernels, on_device(): pl.pallas_call(functools.partial(edge_kernel, levels, cols, rows * levels...  1.22 us
    ppermute x1, waiting for transfers between devices, on_device(): first_got = lax.ppermute(first, axes, first_swap)  1.18 us
    pallas_call x1, Pallas kernels, on_device(): pl.pallas_call(functools.partial(middle_kernel, levels), out_shape=(out_s...  1.14 us
  transfers between devices with their start and end apart: 6, of which 2 were waited for; matrix products, arithmetic and copies ran while one was open for 0% of the time, Pallas kernels for 27%

profile of v2, /device:TPU:0, one launch (start us, length us, event | category | flops | bytes accessed | tf_op | source)
XLA Modules:
  0.0 19.9 jit_solution(11364699476868546797)
XLA Ops:
  0.0 0.8 %pack.1.after_ref.edges_ref = f32[144,128]{1,0:T(8,128)S(1)} custom-call(f32[12,128,128]{2,1,0:T(8,128)} %bitcast.4), custom_call_target="tpu_custom_call" | custom-call | bytes 3000000 | tf_op jit(solution)/shard_map/pack/pallas_call | solution.py:384
  0.9 0.6 %collective-permute-start = (f32[144,128]{1,0:T(8,128)S(1)}, f32[144,128]{1,0:T(8,128)S(1)}, u32[]{:S(2)}, u32[]{:S(2)}) collective-permute-start(f32[144,128]{1,0:T(8,128)S(1)} %pack.1.after_ref.edges_ref), channel_id=1, source_target_pairs={{0,4},{4,0},{8,12},{12,8},{16,20},{20,16},{24,28},{28,24},{1,5},{5... | collective-permute-start | bytes 221192 | tf_op jit(solution)/shard_map/ppermute | solution.py:398
  1.4 1.0 %columns.1 = (f32[3,128,128]{2,1,0:T(8,128)S(1)}, f32[3,128,128]{2,1,0:T(8,128)S(1)}) custom-call(f32[12,128,128]{2,1,0:T(8,128)} %bitcast.5, f32[144,128]{1,0:T(8,128)S(1)} %pack.1.after_ref.edges_ref), custom_call_target="tpu_custom_call" | custom-call | bytes 1500000 | tf_op jit(solution)/shard_map/columns/pallas_call | solution.py:401
  2.5 3.6 %collective-permute-start.5 = (f32[3,128,128]{2,1,0:T(8,128)S(1)}, f32[3,128,128]{2,1,0:T(8,128)S(1)}, u32[]{:S(2)}, u32[]{:S(2)}) collective-permute-start(f32[3,128,128]{2,1,0:T(8,128)S(1)} %get-tuple-element.19), channel_id=1, source_target_pairs={{0,28},{4,8},{8,4},{12,16},{16,12},{20,24},{24,20},{28,0},{1,29},{... | collective-permute-start | bytes 589832 | tf_op jit(solution)/shard_map/ppermute | solution.py:423
  6.1 0.0 copy-start
  6.1 0.0 collective-permute-start.4
  6.1 0.0 collective-permute-done.other_ref
  6.1 0.7 %collective-permute-start.1 = (f32[184,128]{1,0:T(8,128)S(1)}, f32[184,128]{1,0:T(8,128)S(1)}, u32[]{:S(2)}, u32[]{:S(2)}) collective-permute-start(f32[184,128]{1,0:T(8,128)S(1)} %strip.1.after_ref.own_run_ref), channel_id=1, source_target_pairs={{0,28},{4,8},{8,4},{12,16},{16,12},{20,24},{24,20},{28,0},{1,29},{... | collective-permute-start | bytes 282632 | tf_op jit(solution)/shard_map/ppermute | solution.py:422
  6.8 3.1 %band.1 = (bf16[24,128,256]{2,1,0:T(8,128)(2,1)S(1)}, s32[8,128]{1,0:T(8,128)S(1)}) custom-call(s32[2,8]{1,0:T(2,128)} %owner_ref.1, s32[2,8]{1,0:T(2,128)} %codes_ref.1, f32[12,48,64]{2,1,0:T(8,128)} %bitcast.7, s32[12,4,64]{2,1,0:T(4,128)} %bitcast.8, bf16[104,512]{1,0:T(8,128)(2,1)} %constant.2.clone.matrix_hbm, f32[184,128]{1,0:T(8,128)S(1)} %strip.1.after_ref.own_run_ref), custom_call_target="tpu_custom_call" | custom-call | bytes 9000000 | tf_op jit(solution)/shard_map/band/pallas_call | solution.py:450
  9.9 2.8 %collective-permute-done.1.got_ref.got_run_ref = f32[184,128]{1,0:T(8,128)S(1)} collective-permute-done((f32[184,128]{1,0:T(8,128)S(1)}, f32[184,128]{1,0:T(8,128)S(1)}, u32[]{:S(2)}, u32[]{:S(2)}) %collective-permute-start.1) | collective-permute-done | bytes 94240 | tf_op jit(solution)/shard_map/ppermute | solution.py:422
  12.7 0.1 rows.1
  12.9 1.6 %collective-permute-start.3 = (f32[112,128]{1,0:T(8,128)S(1)}, f32[112,128]{1,0:T(8,128)S(1)}, u32[]{:S(2)}, u32[]{:S(2)}) collective-permute-start(f32[112,128]{1,0:T(8,128)S(1)} %get-tuple-element.18), channel_id=1, source_target_pairs={{0,16},{1,2},{2,1},{3,19},{4,20},{5,6},{6,5},{7,23},{8,24},{9,10},... | collective-permute-start | bytes 172040 | tf_op jit(solution)/shard_map/ppermute | solution.py:480
  14.5 1.8 %collective-permute-start.2 = (f32[112,128]{1,0:T(8,128)S(1)}, f32[112,128]{1,0:T(8,128)S(1)}, u32[]{:S(2)}, u32[]{:S(2)}) collective-permute-start(f32[112,128]{1,0:T(8,128)S(1)} %get-tuple-element.17.after_ref), channel_id=1, source_target_pairs={{0,1},{1,0},{2,3},{3,2},{4,5},{5,4},{6,7},{7,6},{8,9},{9,8},{10,11... | collective-permute-start | bytes 172040 | tf_op jit(solution)/shard_map/ppermute | solution.py:479
  16.3 0.0 collective-permute-done.5.outer_ref
  16.3 0.0 collective-permute-done.4.inner_ref
  16.3 0.0 copy-done
  16.3 1.1 %middle.1 = (f32[12,128,128]{2,1,0:T(8,128)}, f32[18,152,128]{2,1,0:T(8,128)S(1)}) custom-call(f32[12,128,128]{2,1,0:T(8,128)S(1)} %bitcast.6, f32[3,128,128]{2,1,0:T(8,128)S(1)} %collective-permute-done.4.inner_ref, f32[3,128,128]{2,1,0:T(8,128)S(1)} %collective-permute-done.5.outer_ref, bf16[24,128,256]{2,1,0:T(8,128)(2,1)S(1)} %get-tuple-element.16.after_ref.band_ref, ...), custom_call_target="tpu_custom_call" | custom-call | bytes 6000000 | tf_op jit(solution)/shard_map/middle/pallas_call | solution.py:486
  17.5 0.0 collective-permute-done.3.second_ref
  17.5 1.2 %collective-permute-done.2.first_ref = f32[112,128]{1,0:T(8,128)S(1)} collective-permute-done((f32[112,128]{1,0:T(8,128)S(1)}, f32[112,128]{1,0:T(8,128)S(1)}, u32[]{:S(2)}, u32[]{:S(2)}) %collective-permute-start.2) | collective-permute-done | bytes 57376 | tf_op jit(solution)/shard_map/ppermute | solution.py:479
  18.7 1.2 %edge.1 = (f32[18,152,128]{2,1,0:T(8,128)S(1)}, f32[12,128,128]{2,1,0:T(8,128)}) custom-call(s32[8,128]{1,0:T(8,128)S(1)} %get-tuple-element.15.table_ref, f32[112,128]{1,0:T(8,128)S(1)} %collective-permute-done.2.first_ref, f32[112,128]{1,0:T(8,128)S(1)} %collective-permute-done.3.second_ref, ...), custom_call_target="tpu_custom_call", output_to_operand_aliasing={{0}: (6, {}), {1}: (7, {})} | custom-call | bytes 6000000 | tf_op jit(solution)/shard_map/edge/pallas_call | solution.py:499
  (1 shorter events, 0.0 us)
Async XLA Ops:
  0.9 5.2 %collective-permute-start = (f32[144,128]{1,0:T(8,128)S(1)}, f32[144,128]{1,0:T(8,128)S(1)}, u32[]{:S(2)}, u32[]{:S(2)}) collective-permute-start(f32[144,128]{1,0:T(8,128)S(1)} %pack.1.after_ref.edges_ref), channel_id=1, source_target_pairs={{0,4},{4,0},{8,12},{12,8},{16,20},{20,16},{24,28},{28,24},{1,5},{5... | collective-permute-start | bytes 221192 | tf_op jit(solution)/shard_map/ppermute | solution.py:398
  2.5 13.8 %collective-permute-start.5 = (f32[3,128,128]{2,1,0:T(8,128)S(1)}, f32[3,128,128]{2,1,0:T(8,128)S(1)}, u32[]{:S(2)}, u32[]{:S(2)}) collective-permute-start(f32[3,128,128]{2,1,0:T(8,128)S(1)} %get-tuple-element.19), channel_id=1, source_target_pairs={{0,28},{4,8},{8,4},{12,16},{16,12},{20,24},{24,20},{28,0},{1,29},{... | collective-permute-start | bytes 589832 | tf_op jit(solution)/shard_map/ppermute | solution.py:423
  6.1 10.2 %copy-start = (f32[12,64,2,128]{3,2,1,0:T(2,128)S(1)}, f32[12,64,2,128]{3,2,1,0:T(2,128)}, u32[]{:S(2)}) copy-start(f32[12,64,2,128]{3,2,1,0:T(2,128)} %param.6) | copy-start | bytes 2359300
  6.1 10.2 %collective-permute-start.4 = (f32[3,128,128]{2,1,0:T(8,128)S(1)}, f32[3,128,128]{2,1,0:T(8,128)S(1)}, u32[]{:S(2)}, u32[]{:S(2)}) collective-permute-start(f32[3,128,128]{2,1,0:T(8,128)S(1)} %get-tuple-element.14.after_ref), channel_id=1, source_target_pairs={{0,4},{4,0},{8,12},{12,8},{16,20},{20,16},{24,28},{28,24},{1,5},{5... | collective-permute-start | bytes 589832 | tf_op jit(solution)/shard_map/ppermute | solution.py:424
  6.1 6.6 %collective-permute-start.1 = (f32[184,128]{1,0:T(8,128)S(1)}, f32[184,128]{1,0:T(8,128)S(1)}, u32[]{:S(2)}, u32[]{:S(2)}) collective-permute-start(f32[184,128]{1,0:T(8,128)S(1)} %strip.1.after_ref.own_run_ref), channel_id=1, source_target_pairs={{0,28},{4,8},{8,4},{12,16},{16,12},{20,24},{24,20},{28,0},{1,29},{... | collective-permute-start | bytes 282632 | tf_op jit(solution)/shard_map/ppermute | solution.py:422
  12.9 4.6 %collective-permute-start.3 = (f32[112,128]{1,0:T(8,128)S(1)}, f32[112,128]{1,0:T(8,128)S(1)}, u32[]{:S(2)}, u32[]{:S(2)}) collective-permute-start(f32[112,128]{1,0:T(8,128)S(1)} %get-tuple-element.18), channel_id=1, source_target_pairs={{0,16},{1,2},{2,1},{3,19},{4,20},{5,6},{6,5},{7,23},{8,24},{9,10},... | collective-permute-start | bytes 172040 | tf_op jit(solution)/shard_map/ppermute | solution.py:480
  14.5 4.2 %collective-permute-start.2 = (f32[112,128]{1,0:T(8,128)S(1)}, f32[112,128]{1,0:T(8,128)S(1)}, u32[]{:S(2)}, u32[]{:S(2)}) collective-permute-start(f32[112,128]{1,0:T(8,128)S(1)} %get-tuple-element.17.after_ref), channel_id=1, source_target_pairs={{0,1},{1,0},{2,3},{3,2},{4,5},{5,4},{6,7},{7,6},{8,9},{9,8},{10,11... | collective-permute-start | bytes 172040 | tf_op jit(solution)/shard_map/ppermute | solution.py:479

commit v3 on v2

--- a/solution.py
+++ b/solution.py
@@ -46,56 +46,40 @@
     return matrix
 
 
-def columns_kernel(cells_ref, after_ref, inner_ref, outer_ref, sems):
+def load_kernel(count, ends, run, owner_ref, codes_ref, cells_ref, weights_ref, offsets_ref,
+                matrix_ref, after_ref, table_ref, inner_ref, weights_out, offsets_out, matrix_out,
+                owner, codes, sems):
     del after_ref
-    even = lax.axis_index("gx") % 2 == 0
+    index, place = lax.axis_index("gx"), lax.axis_index("gy")
     last = cells_ref.shape[0] - HALO
-    copies = [
-        pltpu.make_async_copy(
-            cells_ref.at[pl.ds(jnp.where(even, last, 0), HALO)], inner_ref, sems.at[0]
-        ),
-        pltpu.make_async_copy(
-            cells_ref.at[pl.ds(jnp.where(even, 0, last), HALO)], outer_ref, sems.at[1]
-        ),
+    pairs = [
+        (owner_ref, owner),
+        (codes_ref, codes),
+        (cells_ref.at[pl.ds(jnp.where(index % 2 == 0, last, 0), HALO)], inner_ref),
+        (weights_ref, weights_out),
+        (offsets_ref, offsets_out),
+        (matrix_ref, matrix_out),
     ]
+    copies = [pltpu.make_async_copy(a, b, sems.at[at]) for at, (a, b) in enumerate(pairs)]
     for copy in copies:
         copy.start()
-    for copy in copies:
-        copy.wait()
-
-
-def band_kernel(levels, rows, count, ends, run, based, owner_ref, codes_ref, weights_hbm, offsets_hbm,
-                matrix_hbm, after_ref, band_ref, table_ref, weights_ref, offsets_ref, matrix_ref, sems):
-    del after_ref
-    cols = weights_ref.shape[0]
-    groups = cols // UNROLL
-
-    def fetch(group):
-        part = pl.ds(group * UNROLL, UNROLL)
-        return pltpu.make_async_copy(weights_hbm.at[part], weights_ref.at[part], sems.at[group])
-
-    others = [
-        pltpu.make_async_copy(offsets_hbm, offsets_ref, sems.at[groups]),
-        pltpu.make_async_copy(matrix_hbm, matrix_ref, sems.at[groups + 1]),
-    ]
-    fetch(0).start()
-    for copy in others:
-        copy.start()
-    for group in range(1, groups):
-        fetch(group).start()
-
-    index, place = lax.axis_index("gx"), lax.axis_index("gy")
+    copies[0].wait()
+    copies[1].wait()
     side = jnp.where(place == 0, 0, 1)
-    window = Window(cols, 0, count, run, based, None, None)
+    window = Window(cells_ref.shape[0], 0, count, run, None)
     target = lax.rem(index + count // 2, count)
     is_end = jnp.logical_or(place == 0, place == ends - 1)
-    code = jnp.where(is_end, codes_ref[side, index], 0)
-    lines = [window.start(owner_ref[side, target]), window.start(owner_ref[side, index]), code]
+    code = jnp.where(is_end, codes[side, index], 0)
+    lines = [window.start(owner[side, target]), window.start(owner[side, index]), code]
     for at, line in enumerate(lines):
         table_ref[at : at + 1] = jnp.full((1, LANES), line, jnp.int32)
-    for copy in others:
+    for copy in copies[2:]:
         copy.wait()
 
+
+def band_kernel(levels, rows, weights_ref, offsets_ref, matrix_ref, after_ref, band_ref):
+    del after_ref
+    groups = weights_ref.shape[0] // UNROLL
     y_blocks = rows // BLOCK_Y
     lane = lax.broadcasted_iota(jnp.int32, (rows, LANES), 1)
     row_in = lax.broadcasted_iota(jnp.int32, (rows, LANES), 0) % BLOCK_Y
@@ -135,7 +119,6 @@
                     band_ref[slot, pl.ds(low, BLOCK_Y), lanes] = jnp.where(keep, rest, 0.0).astype(BF16)
 
     def group_of(group, carry):
-        fetch(group).wait()
         for step in range(UNROLL):
             column(group * UNROLL + step)
         return carry
@@ -143,53 +126,72 @@
     lax.fori_loop(0, groups, group_of, 0)
 
 
-def pack_kernel(cells_ref, edges_ref, low_ref, high_ref, sems):
+def pack_kernel(cells_ref, edges_ref, message_ref, outer_ref, low_ref, high_ref, sems):
     cols, rows, _ = cells_ref.shape
     width = edges_ref.shape[0] // cols // 2
     deep = low_ref.shape[1]
+    even, low = lax.axis_index("gx") % 2 == 0, lax.axis_index("gy") == 0
+    last = cols - HALO
     copies = [
         pltpu.make_async_copy(cells_ref.at[:, pl.ds(0, deep)], low_ref, sems.at[0]),
         pltpu.make_async_copy(cells_ref.at[:, pl.ds(rows - deep, deep)], high_ref, sems.at[1]),
+        pltpu.make_async_copy(
+            cells_ref.at[pl.ds(jnp.where(even, 0, last), HALO)], outer_ref, sems.at[2]
+        ),
     ]
     for copy in copies:
         copy.start()
-    for copy in copies:
+    for copy in copies[:2]:
         copy.wait()
     for col in range(cols):
         at = 2 * width * col
-        edges_ref[at : at + width] = low_ref[col, :width]
-        edges_ref[at + width : at + 2 * width] = high_ref[col, deep - width :]
-
-
-def strip_kernel(cols, width, edges_ref, other_ref, after_ref, message_ref):
+        bottom, top = low_ref[col, :width], high_ref[col, deep - width :]
+        edges_ref[at : at + width] = bottom
+        edges_ref[at + width : at + 2 * width] = top
+        message_ref[width * col : width * (col + 1)] = jnp.where(low, bottom, top)
+    at = width * cols
+    for col in range(HALO):
+        for ref in (low_ref.at[:, :width], high_ref.at[:, deep - width :]):
+            edge = jnp.where(even, ref[col], ref[last + col])
+            message_ref[at : at + width] = edge
+            at += width
+    clear(message_ref, at)
+    copies[2].wait()
+
+
+def clear(ref, at):
+    if at < ref.shape[0]:
+        ref[at:] = jnp.zeros((ref.shape[0] - at, LANES), F32)
+
+
+def relay_kernel(cols, width, edges_ref, message_ref, got_ref, after_ref, relay_ref):
     del after_ref
     even = lax.axis_index("gx") % 2 == 0
-    low = lax.axis_index("gy") == 0
-    for col in range(cols):
-        at = 2 * width * col
-        mine = jnp.where(low, edges_ref[at : at + width], edges_ref[at + width : at + 2 * width])
-        theirs = jnp.where(low, other_ref[at : at + width], other_ref[at + width : at + 2 * width])
-        message_ref[width * col : width * (col + 1)] = jnp.where(even, mine, theirs)
-        to = width * (cols + col)
-        message_ref[to : to + width] = jnp.where(even, theirs, mine)
-    corner = 2 * width * HALO
-    first, last = edges_ref[:corner], edges_ref[2 * width * cols - corner :]
-    at = 2 * width * cols
-    message_ref[at : at + corner] = jnp.where(even, first, last)
-    end = message_ref.shape[0]
-    if end > at + corner:
-        message_ref[at + corner :] = jnp.zeros((end - at - corner, LANES), F32)
+    corner, strip = 2 * width * HALO, width * cols
+    edges = 2 * strip
+    relay_ref[:corner] = jnp.where(even, edges_ref[edges - corner : edges], edges_ref[:corner])
+    relay_ref[corner : corner + strip] = message_ref[:strip]
+    relay_ref[corner + strip : corner + 2 * strip] = got_ref[:strip]
+    clear(relay_ref, corner + 2 * strip)
+
+
+def join_kernel(cols, width, message_ref, got_ref, other_ref, run_ref):
+    even = lax.axis_index("gx") % 2 == 0
+    corner, strip = 2 * width * HALO, width * cols
+    mine, far = message_ref[:strip], got_ref[:strip]
+    near = other_ref[corner : corner + strip]
+    beyond = other_ref[corner + strip : corner + 2 * strip]
+    pairs = ((far, beyond), (mine, near), (near, mine), (beyond, far))
+    for at, (a, b) in enumerate(pairs):
+        run_ref[at * strip : (at + 1) * strip] = jnp.where(even, a, b)
 
 
 class Window:
-    def __init__(self, cols, width, count, run, based, own, got):
+    def __init__(self, cols, width, count, run, held):
         self.cols, self.width, self.total, self.run = cols, width, count * cols, run
-        self.count, self.own, self.got = count, own, got
+        self.held = held
         index = lax.axis_index("gx")
-        even = index % 2 == 0
-        self.half = run * cols // 2
-        self.own_low = jnp.logical_not(even) if based else None
-        self.first = jnp.where(even, index - 2, index - 1)
+        self.first = index - index % 2 - 1
 
     def start(self, owner):
         return lax.rem((owner - self.first) * self.cols - HALO + 2 * self.total, self.total)
@@ -197,38 +199,29 @@
     def column(self, start, step):
         at = start + step
         at = jnp.where(at >= self.total, at - self.total, at)
-        held = at < self.run * self.cols
-        at = jnp.minimum(at, self.run * self.cols - 1)
-        low = at < self.half
-        row = jnp.where(low, at, at - self.half) * self.width
-        own, got = self.own[pl.ds(row, self.width)], self.got[pl.ds(row, self.width)]
-        from_own = low if self.own_low is None else low == self.own_low
-        return held, jnp.where(from_own, own, got)
-
-
-def rows_kernel(cols, width, count, ends, run, based, table_ref, edges_ref, other_ref, got_ref,
-                own_run_ref, got_run_ref, after_ref, first_ref, second_ref):
-    del after_ref
+        row = jnp.minimum(at, self.run * self.cols - 1) * self.width
+        return at < self.run * self.cols, self.held[pl.ds(row, self.width)]
+
+
+def rows_kernel(cols, width, count, ends, run, table_ref, edges_ref, other_ref, got_ref, run_ref,
+                first_ref, second_ref):
     even, place = lax.axis_index("gx") % 2 == 0, lax.axis_index("gy")
     flat_place = place % 2 == 0
-    corner = 2 * width * cols
+    strip = width * cols
 
     def rows(ref, at, top):
         return jnp.where(top, ref[at + width : at + 2 * width], ref[at : at + width])
 
     def column(u, top):
-        if u < HALO:
-            near = rows(other_ref, 2 * width * (cols - HALO + u), top)
-            far = rows(got_ref, corner + 2 * width * u, top)
-            return jnp.where(even, far, near)
-        if u < HALO + cols:
+        if HALO <= u < HALO + cols:
             return rows(edges_ref, 2 * width * (u - HALO), top)
-        near = rows(other_ref, 2 * width * (u - HALO - cols), top)
-        far = rows(got_ref, corner + 2 * width * (u - HALO - cols), top)
-        return jnp.where(even, near, far)
+        col = u if u < HALO else u - HALO - cols
+        near = rows(other_ref, 2 * width * col, top)
+        far = rows(got_ref, strip + 2 * width * col, top)
+        return jnp.where(even == (u < HALO), far, near)
 
     wide = cols + 2 * HALO
-    window = Window(cols, width, count, run, based, own_run_ref, got_run_ref)
+    window = Window(cols, width, count, run, run_ref)
     start = table_ref[0:1, 0:1][0, 0]
     is_end = jnp.logical_or(place == 0, place == ends - 1)
     for u in range(wide):
@@ -236,10 +229,8 @@
         first_ref[to] = column(u, flat_place)
         _, glued = window.column(start, u)
         second_ref[to] = jnp.where(is_end, glued, column(u, jnp.logical_not(flat_place)))
-    end = first_ref.shape[0]
-    if end > wide * width:
-        first_ref[wide * width :] = jnp.zeros((end - wide * width, LANES), F32)
-        second_ref[wide * width :] = jnp.zeros((end - wide * width, LANES), F32)
+    clear(first_ref, wide * width)
+    clear(second_ref, wide * width)
 
 
 def block_sum(field_ref, band_ref, x, y, y_blocks, levels, level):
@@ -301,16 +292,15 @@
     )
 
 
-def edge_kernel(levels, cols, rows, count, ends, run, based, table_ref, first_ref, second_ref,
-                own_run_ref, got_run_ref, band_ref, field_in, out_in, field_ref, out_ref,
-                stage_ref, sems):
+def edge_kernel(levels, cols, rows, count, ends, run, table_ref, first_ref, second_ref, run_ref,
+                band_ref, field_in, out_in, field_ref, out_ref, stage_ref, sems):
     del field_in, out_in
     width = HALO * levels
     lead = LEAD * levels
     place = lax.axis_index("gy")
     flat_place = place % 2 == 0
     wide = cols + 2 * HALO
-    window = Window(cols, width, count, run, based, own_run_ref, got_run_ref)
+    window = Window(cols, width, count, run, run_ref)
     start, code = table_ref[1:2, 0:1][0, 0], table_ref[2:3, 0:1][0, 0]
     is_end = jnp.logical_or(place == 0, place == ends - 1)
     mirrored = code % 2 == 1
@@ -381,103 +371,101 @@
                 second_swap.append((i * ends + j, i * ends + (j + 1 if j % 2 else j - 1)))
 
     deep = eights(width)
-    edges = pl.pallas_call(
+    strip, corner = width * cols, 2 * width * HALO
+    columns = shaped(HALO, rows * levels, lanes)
+    edges, message, outer = pl.pallas_call(
         pack_kernel,
-        out_shape=shaped(2 * width * cols, lanes),
+        out_shape=(shaped(2 * strip, lanes), shaped(eights(strip + corner), lanes), columns),
         in_specs=[HBM],
-        out_specs=VMEM,
+        out_specs=(VMEM, VMEM, VMEM),
         scratch_shapes=[
             pltpu.VMEM((cols, deep, lanes), F32),
             pltpu.VMEM((cols, deep, lanes), F32),
-            pltpu.SemaphoreType.DMA((2,)),
+            pltpu.SemaphoreType.DMA((3,)),
         ],
         name="pack",
         compiler_params=grant(4),
         cost_estimate=takes(1.0),
     )(in_hbm(cells))
-    other = lax.ppermute(edges, "gx", partner)
-
-    columns = shaped(HALO, rows * levels, lanes)
-    inner, outer = pl.pallas_call(
-        columns_kernel,
-        out_shape=(columns, columns),
-        in_specs=[HBM, ANY],
-        out_specs=(VMEM, VMEM),
-        scratch_shapes=[pltpu.SemaphoreType.DMA((2,))],
-        name="columns",
-        compiler_params=grant(4),
-        cost_estimate=takes(0.5),
-    )(in_hbm(cells), edges)
-
-    strip_rows = 2 * width * cols
-    message = pl.pallas_call(
-        functools.partial(strip_kernel, cols, width),
-        out_shape=shaped(eights(strip_rows + 2 * width * HALO), lanes),
-        in_specs=[VMEM, VMEM, ANY],
-        out_specs=VMEM,
-        name="strip",
-        cost_estimate=takes(1.0),
-        compiler_params=grant(4),
-    )(edges, other, inner)
     got = lax.ppermute(message, "gx", across)
     outer_got = lax.ppermute(outer, "gx", across)
-    inner_got = lax.ppermute(inner, "gx", partner)
-
-    run, based = 4, True
-    own_run, got_run = message, got
-    if count // 2 > run:
-        mine, theirs = message[:strip_rows], got[:strip_rows]
-        own_run = jnp.where(
-            lax.axis_index("gx") % 2 == 0,
-            jnp.concatenate([theirs, mine]),
-            jnp.concatenate([mine, theirs]),
-        )
-        based = False
-        while True:
-            shift = run
-            got_run = lax.ppermute(
-                own_run, "gx", [((i + shift) % count, i) for i in range(count)]
-            )
-            run *= 2
-            if run >= count // 2:
-                break
-            own_run = jnp.concatenate([own_run, got_run])
-
+
+    run = 4
+    held = max(run, count // 2)
     weights = jnp.swapaxes(weights, 1, 2)
     offsets = jnp.swapaxes(offsets, 1, 2)
-    y_blocks = rows // BLOCK_Y
-    slots = cols // BLOCK_X * y_blocks * levels
-    band, table = pl.pallas_call(
-        functools.partial(band_kernel, levels, rows, count, ends, run, based),
+    table, inner, weights, offsets, matrix = pl.pallas_call(
+        functools.partial(load_kernel, count, ends, held),
         out_shape=(
-            shaped(slots, 2 * BLOCK_X * BLOCK_Y, 2 * LANES, dtype=BF16),
             shaped(8, lanes, dtype=jnp.int32),
+            columns,
+            shaped(*weights.shape),
+            shaped(*offsets.shape, dtype=jnp.int32),
+            shaped(*matrix.shape, dtype=BF16),
         ),
-        in_specs=[SMEM, SMEM] + [HBM] * 3 + [ANY],
-        out_specs=(VMEM, VMEM),
+        in_specs=[HBM] * 6 + [ANY],
+        out_specs=(VMEM,) * 5,
         scratch_shapes=[
-            pltpu.VMEM(weights.shape, F32),
-            pltpu.VMEM(offsets.shape, jnp.int32),
-            pltpu.VMEM(matrix.shape, BF16),
-            pltpu.SemaphoreType.DMA((cols // UNROLL + 2,)),
+            pltpu.SMEM(owner.shape, jnp.int32),
+            pltpu.SMEM(codes.shape, jnp.int32),
+            pltpu.SemaphoreType.DMA((6,)),
         ],
-        name="band",
-        compiler_params=grant(6),
-        cost_estimate=takes(3.0),
-    )(*[in_hbm(a) for a in (owner, codes, weights, offsets, matrix)], message)
+        name="load",
+        compiler_params=grant(4),
+        cost_estimate=takes(1.0),
+    )(*[in_hbm(a) for a in (owner, codes, cells, weights, offsets, matrix)], message)
+
+    relay = pl.pallas_call(
+        functools.partial(relay_kernel, cols, width),
+        out_shape=shaped(eights(corner + 2 * strip), lanes),
+        in_specs=[VMEM] * 3 + [ANY],
+        out_specs=VMEM,
+        name="relay",
+        compiler_params=grant(2),
+        cost_estimate=takes(0.5),
+    )(edges, message, got, table)
+    other = lax.ppermute(relay, "gx", partner)
+    inner_got = lax.ppermute(inner, "gx", partner)
+
+    ring = pl.pallas_call(
+        functools.partial(join_kernel, cols, width),
+        out_shape=shaped(run * strip, lanes),
+        in_specs=[VMEM] * 3,
+        out_specs=VMEM,
+        name="join",
+        compiler_params=grant(2),
+        cost_estimate=takes(0.5),
+    )(message, got, other)
+    while run < held:
+        shift = run
+        more = lax.ppermute(ring, "gx", [((i + shift) % count, i) for i in range(count)])
+        ring = jnp.concatenate([ring, more])
+        run *= 2
 
     z_rows = eights(width * (cols + 2 * HALO))
     first, second = pl.pallas_call(
-        functools.partial(rows_kernel, cols, width, count, ends, run, based),
+        functools.partial(rows_kernel, cols, width, count, ends, run),
         out_shape=(shaped(z_rows, lanes), shaped(z_rows, lanes)),
-        in_specs=[VMEM] * 6 + [ANY],
+        in_specs=[VMEM] * 5,
         out_specs=(VMEM, VMEM),
         name="rows",
         cost_estimate=takes(1.0),
-        compiler_params=grant(2),
-    )(table, edges, other, got, own_run, got_run, band)
+        compiler_params=grant(2 * pl.cdiv(run, 8)),
+    )(table, edges, other, got, ring)
     first_got = lax.ppermute(first, axes, first_swap)
     second_got = lax.ppermute(second, axes, second_swap)
+
+    y_blocks = rows // BLOCK_Y
+    slots = cols // BLOCK_X * y_blocks * levels
+    band = pl.pallas_call(
+        functools.partial(band_kernel, levels, rows),
+        out_shape=shaped(slots, 2 * BLOCK_X * BLOCK_Y, 2 * LANES, dtype=BF16),
+        in_specs=[VMEM] * 3 + [ANY],
+        out_specs=VMEM,
+        name="band",
+        compiler_params=grant(6),
+        cost_estimate=takes(1.5),
+    )(weights, offsets, matrix, first)
 
     field_rows = eights((LEAD + rows + HALO + PITCH - BLOCK_Y - 2 * HALO) * levels)
     field_shape = shaped(cols + 2 * HALO, field_rows, lanes)
@@ -497,16 +485,16 @@
         compiler_params=grant(6),
     )(cells, inner_got, outer_got, band, first)
     _, updated = pl.pallas_call(
-        functools.partial(edge_kernel, levels, cols, rows * levels, count, ends, run, based),
+        functools.partial(edge_kernel, levels, cols, rows * levels, count, ends, run),
         out_shape=(field_shape, out_shape),
-        in_specs=[VMEM] * 7 + [HBM],
+        in_specs=[VMEM] * 6 + [HBM],
         out_specs=(VMEM, HBM),
         scratch_shapes=[pltpu.VMEM((2, *stage), F32), pltpu.SemaphoreType.DMA((2,))],
-        input_output_aliases={6: 0, 7: 1},
+        input_output_aliases={5: 0, 6: 1},
         name="edge",
         cost_estimate=takes(2.0),
         compiler_params=grant(6),
-    )(table, first_got, second_got, own_run, got_run, band, field, partial)
+    )(table, first_got, second_got, ring, band, field, partial)
     return updated.reshape(cols, rows, levels, lanes)
 
 

time: 20.1 us -> 16.2 us (0.81)
  waiting for transfers between devices: 4.01 us -> 2.28 us
  Pallas kernels: 7.49 us -> 5.96 us
  starting transfers between devices: 8.31 us -> 7.69 us
    ppermute x1, starting transfers between devices: 3.61 us -> 0.08 us  [on_device(): outer_got = lax.ppermute(outer, 'gx', across)]
    ppermute x1, starting transfers between devices: 0.71 us -> 3.43 us  [on_device(): got = lax.ppermute(message, 'gx', across)]
    ppermute x1, waiting for transfers between devices: 2.82 us -> 0.99 us  [on_device(): got = lax.ppermute(message, 'gx', across)]
    pallas_call x4 -> x5, Pallas kernels: 4.99 us -> 3.57 us  [the longest x1 1.36 us: on_device(): pl.pallas_call(functools.partial(band_kernel, levels, rows), out_shape=sh...]
    ppermute x1, waiting for transfers between devices: 0.01 us -> 1.28 us  [on_device(): other = lax.ppermute(relay, 'gx', partner)]
    ppermute x1, waiting for transfers between devices: 1.18 us -> 0.01 us  [on_device(): first_got = lax.ppermute(first, axes, first_swap)]
    ppermute x1, starting transfers between devices: 0.56 us -> 0.07 us  [on_device(): other = lax.ppermute(relay, 'gx', partner)]
    ppermute x1, starting transfers between devices: 1.82 us -> 2.14 us  [on_device(): first_got = lax.ppermute(first, axes, first_swap)]
  transfers between devices with their start and end apart: 6 -> 6, of which waited for: 2 -> 2; matrix products, arithmetic and copies ran while one was open for 0% -> 0% of each run, Pallas kernels for 27% -> 23%
where the time goes in v3:
time: 16.2 us; the launch traced here: 16.1 us
  starting transfers between devices  7.69 us (47%)
  Pallas kernels  5.96 us (37%)
  waiting for transfers between devices  2.28 us (14%)
    ppermute x1, starting transfers between devices, on_device(): got = lax.ppermute(message, 'gx', across)  3.43 us
    ppermute x1, starting transfers between devices, on_device(): first_got = lax.ppermute(first, axes, first_swap)  2.14 us
    ppermute x1, starting transfers between devices, on_device(): second_got = lax.ppermute(second, axes, second_swap)  1.9 us
    pallas_call x1, Pallas kernels, on_device(): pl.pallas_call(functools.partial(band_kernel, levels, rows), out_shape=sh...  1.36 us
    ppermute x1, waiting for transfers between devices, on_device(): other = lax.ppermute(relay, 'gx', partner)  1.28 us
    pallas_call x1, Pallas kernels, on_device(): pl.pallas_call(functools.partial(edge_kernel, levels, cols, rows * levels...  1.17 us
    pallas_call x1, Pallas kernels, on_device(): pl.pallas_call(functools.partial(load_kernel, count, ends, held), out_sha...  1.15 us
    pallas_call x1, Pallas kernels, on_device(): pl.pallas_call(functools.partial(middle_kernel, levels), out_shape=(out_s...  1.14 us
  transfers between devices with their start and end apart: 6, of which 2 were waited for; matrix products, arithmetic and copies ran while one was open for 0% of the time, Pallas kernels for 23%

profile of v3, /device:TPU:0, one launch (start us, length us, event | category | flops | bytes accessed | tf_op | source)
XLA Modules:
  0.0 16.1 jit_solution(8576930186787338669)
XLA Ops:
  0.0 1.0 %pack.1 = (f32[144,128]{1,0:T(8,128)S(1)}, f32[112,128]{1,0:T(8,128)S(1)}, f32[3,128,128]{2,1,0:T(8,128)S(1)}) custom-call(f32[12,128,128]{2,1,0:T(8,128)} %bitcast.4), custom_call_target="tpu_custom_call" | custom-call | bytes 3000000 | tf_op jit(solution)/shard_map/pack/pallas_call | solution.py:376
  1.0 3.4 %collective-permute-start = (f32[112,128]{1,0:T(8,128)S(1)}, f32[112,128]{1,0:T(8,128)S(1)}, u32[]{:S(2)}, u32[]{:S(2)}) collective-permute-start(f32[112,128]{1,0:T(8,128)S(1)} %get-tuple-element.18.after_ref.message_ref), channel_id=1, source_target_pairs={{0,28},{4,8},{8,4},{12,16},{16,12},{20,24},{24,20},{28,0},{1,29},{... | collective-permute-start | bytes 172040 | tf_op jit(solution)/shard_map/ppermute | solution.py:390
  4.5 0.1 collective-permute-start.5
  4.6 1.1 %load.1 = (s32[8,128]{1,0:T(8,128)S(1)}, f32[3,128,128]{2,1,0:T(8,128)S(1)}, f32[12,48,64]{2,1,0:T(8,128)S(1)}, s32[12,4,64]{2,1,0:T(4,128)S(1)}, bf16[104,512]{1,0:T(8,128)(2,1)S(1)}) custom-call(s32[2,8]{1,0:T(2,128)} %owner_ref.1, s32[2,8]{1,0:T(2,128)} %codes_ref.1, f32[12,128,128]{2,1,0:T(8,128)} %bitcast.5, f32[12,48,64]{2,1,0:T(8,128)} %bitcast.7, ...), custom_call_target="tpu_custom_call" | custom-call | bytes 3000000 | tf_op jit(solution)/shard_map/load/pallas_call | solution.py:397
  5.7 0.1 collective-permute-start.4
  5.8 1.0 %collective-permute-done.got_ref = f32[112,128]{1,0:T(8,128)S(1)} collective-permute-done((f32[112,128]{1,0:T(8,128)S(1)}, f32[112,128]{1,0:T(8,128)S(1)}, u32[]{:S(2)}, u32[]{:S(2)}) %collective-permute-start) | collective-permute-done | bytes 57376 | tf_op jit(solution)/shard_map/ppermute | solution.py:390
  6.8 0.0 copy-start
  6.8 0.1 collective-permute-start.1
  6.9 1.3 %collective-permute-done.1.other_ref = f32[184,128]{1,0:T(8,128)S(1)} collective-permute-done((f32[184,128]{1,0:T(8,128)S(1)}, f32[184,128]{1,0:T(8,128)S(1)}, u32[]{:S(2)}, u32[]{:S(2)}) %collective-permute-start.1) | collective-permute-done | bytes 94240 | tf_op jit(solution)/shard_map/ppermute | solution.py:427
  8.2 0.1 rows.1
  8.3 1.9 %collective-permute-start.3 = (f32[112,128]{1,0:T(8,128)S(1)}, f32[112,128]{1,0:T(8,128)S(1)}, u32[]{:S(2)}, u32[]{:S(2)}) collective-permute-start(f32[112,128]{1,0:T(8,128)S(1)} %get-tuple-element.22), channel_id=1, source_target_pairs={{0,16},{1,2},{2,1},{3,19},{4,20},{5,6},{6,5},{7,23},{8,24},{9,10},... | collective-permute-start | bytes 172040 | tf_op jit(solution)/shard_map/ppermute | solution.py:456
  10.2 2.1 %collective-permute-start.2 = (f32[112,128]{1,0:T(8,128)S(1)}, f32[112,128]{1,0:T(8,128)S(1)}, u32[]{:S(2)}, u32[]{:S(2)}) collective-permute-start(f32[112,128]{1,0:T(8,128)S(1)} %get-tuple-element.21.after_ref), channel_id=1, source_target_pairs={{0,1},{1,0},{2,3},{3,2},{4,5},{5,4},{6,7},{7,6},{8,9},{9,8},{10,11... | collective-permute-start | bytes 172040 | tf_op jit(solution)/shard_map/ppermute | solution.py:455
  12.3 1.4 %band.1.band_ref = bf16[24,128,256]{2,1,0:T(8,128)(2,1)S(1)} custom-call(f32[12,48,64]{2,1,0:T(8,128)S(1)} %get-tuple-element.23.weights_ref, s32[12,4,64]{2,1,0:T(4,128)S(1)} %get-tuple-element.24.offsets_ref, bf16[104,512]{1,0:T(8,128)(2,1)S(1)} %get-tuple-element.25.matrix_ref, f32[112,128]{1,0:T(8,128)S(1)} %get-tuple-element.21.after_ref), custom_call_target="tpu_custom_call" | custom-call | bytes 4500000 | tf_op jit(solution)/shard_map/band/pallas_call | solution.py:460
  13.7 0.0 collective-permute-done.5.outer_ref
  13.7 0.0 collective-permute-done.4.inner_ref
  13.7 0.0 copy-done
  13.7 1.1 %middle.1 = (f32[12,128,128]{2,1,0:T(8,128)}, f32[18,152,128]{2,1,0:T(8,128)S(1)}) custom-call(f32[12,128,128]{2,1,0:T(8,128)S(1)} %bitcast.6, f32[3,128,128]{2,1,0:T(8,128)S(1)} %collective-permute-done.4.inner_ref, f32[3,128,128]{2,1,0:T(8,128)S(1)} %collective-permute-done.5.outer_ref, bf16[24,128,256]{2,1,0:T(8,128)(2,1)S(1)} %band.1.band_ref, ...), custom_call_target="tpu_custom_call" | custom-call | bytes 6000000 | tf_op jit(solution)/shard_map/middle/pallas_call | solution.py:474
  14.9 0.0 collective-permute-done.3.second_ref
  14.9 0.0 collective-permute-done.2.first_ref
  14.9 1.2 %edge.1 = (f32[18,152,128]{2,1,0:T(8,128)S(1)}, f32[12,128,128]{2,1,0:T(8,128)}) custom-call(s32[8,128]{1,0:T(8,128)S(1)} %get-tuple-element.19.after_ref.table_ref, f32[112,128]{1,0:T(8,128)S(1)} %collective-permute-done.2.first_ref, f32[112,128]{1,0:T(8,128)S(1)} %collective-permute-done.3.second_ref, ...), custom_call_target="tpu_custom_call", output_to_operand_aliasing={{0}: (5, {}), {1}: (6, {})} | custom-call | bytes 6000000 | tf_op jit(solution)/shard_map/edge/pallas_call | solution.py:487
  (2 shorter events, 0.0 us)
Async XLA Ops:
  1.0 5.7 %collective-permute-start = (f32[112,128]{1,0:T(8,128)S(1)}, f32[112,128]{1,0:T(8,128)S(1)}, u32[]{:S(2)}, u32[]{:S(2)}) collective-permute-start(f32[112,128]{1,0:T(8,128)S(1)} %get-tuple-element.18.after_ref.message_ref), channel_id=1, source_target_pairs={{0,28},{4,8},{8,4},{12,16},{16,12},{20,24},{24,20},{28,0},{1,29},{... | collective-permute-start | bytes 172040 | tf_op jit(solution)/shard_map/ppermute | solution.py:390
  4.5 9.2 %collective-permute-start.5 = (f32[3,128,128]{2,1,0:T(8,128)S(1)}, f32[3,128,128]{2,1,0:T(8,128)S(1)}, u32[]{:S(2)}, u32[]{:S(2)}) collective-permute-start(f32[3,128,128]{2,1,0:T(8,128)S(1)} %get-tuple-element.27), channel_id=1, source_target_pairs={{0,28},{4,8},{8,4},{12,16},{16,12},{20,24},{24,20},{28,0},{1,29},{... | collective-permute-start | bytes 589832 | tf_op jit(solution)/shard_map/ppermute | solution.py:391
  5.7 8.0 %collective-permute-start.4 = (f32[3,128,128]{2,1,0:T(8,128)S(1)}, f32[3,128,128]{2,1,0:T(8,128)S(1)}, u32[]{:S(2)}, u32[]{:S(2)}) collective-permute-start(f32[3,128,128]{2,1,0:T(8,128)S(1)} %get-tuple-element.26), channel_id=1, source_target_pairs={{0,4},{4,0},{8,12},{12,8},{16,20},{20,16},{24,28},{28,24},{1,5},{5... | collective-permute-start | bytes 589832 | tf_op jit(solution)/shard_map/ppermute | solution.py:428
  6.8 6.9 %copy-start = (f32[12,64,2,128]{3,2,1,0:T(2,128)S(1)}, f32[12,64,2,128]{3,2,1,0:T(2,128)}, u32[]{:S(2)}) copy-start(f32[12,64,2,128]{3,2,1,0:T(2,128)} %param.6) | copy-start | bytes 2359300
  6.8 1.4 %collective-permute-start.1 = (f32[184,128]{1,0:T(8,128)S(1)}, f32[184,128]{1,0:T(8,128)S(1)}, u32[]{:S(2)}, u32[]{:S(2)}) collective-permute-start(f32[184,128]{1,0:T(8,128)S(1)} %relay.1), channel_id=1, source_target_pairs={{0,4},{4,0},{8,12},{12,8},{16,20},{20,16},{24,28},{28,24},{1,5},{5... | collective-permute-start | bytes 282632 | tf_op jit(solution)/shard_map/ppermute | solution.py:427
  8.3 6.6 %collective-permute-start.3 = (f32[112,128]{1,0:T(8,128)S(1)}, f32[112,128]{1,0:T(8,128)S(1)}, u32[]{:S(2)}, u32[]{:S(2)}) collective-permute-start(f32[112,128]{1,0:T(8,128)S(1)} %get-tuple-element.22), channel_id=1, source_target_pairs={{0,16},{1,2},{2,1},{3,19},{4,20},{5,6},{6,5},{7,23},{8,24},{9,10},... | collective-permute-start | bytes 172040 | tf_op jit(solution)/shard_map/ppermute | solution.py:456
  10.2 4.7 %collective-permute-start.2 = (f32[112,128]{1,0:T(8,128)S(1)}, f32[112,128]{1,0:T(8,128)S(1)}, u32[]{:S(2)}, u32[]{:S(2)}) collective-permute-start(f32[112,128]{1,0:T(8,128)S(1)} %get-tuple-element.21.after_ref), channel_id=1, source_target_pairs={{0,1},{1,0},{2,3},{3,2},{4,5},{5,4},{6,7},{7,6},{8,9},{9,8},{10,11... | collective-permute-start | bytes 172040 | tf_op jit(solution)/shard_map/ppermute | solution.py:455

commit v4 on v3

--- a/solution.py
+++ b/solution.py
@@ -14,7 +14,6 @@
 PITCH = 24
 LANES = 128
 LEAD = 4
-UNROLL = 4
 BF16 = jnp.bfloat16
 F32 = jnp.float32
 
@@ -77,9 +76,8 @@
         copy.wait()
 
 
-def band_kernel(levels, rows, weights_ref, offsets_ref, matrix_ref, after_ref, band_ref):
+def band_kernel(levels, rows, block, weights_ref, offsets_ref, matrix_ref, after_ref, band_ref):
     del after_ref
-    groups = weights_ref.shape[0] // UNROLL
     y_blocks = rows // BLOCK_Y
     lane = lax.broadcasted_iota(jnp.int32, (rows, LANES), 1)
     row_in = lax.broadcasted_iota(jnp.int32, (rows, LANES), 0) % BLOCK_Y
@@ -95,9 +93,9 @@
         spread = lax.dot_general(
             stacked, matrix_ref[...], (((0,), (0,)), ((), ())), preferred_element_type=F32
         )
-        block, inner = x // BLOCK_X, x % BLOCK_X
-        at = pl.multiple_of(inner * BLOCK_Y, BLOCK_Y)
-        low = pl.multiple_of(at + BLOCK_X * BLOCK_Y, BLOCK_Y)
+        inner = x % BLOCK_X
+        at = inner * BLOCK_Y
+        low = at + BLOCK_X * BLOCK_Y
         for level in range(levels):
             points = spread[:, level * LANES : (level + 1) * LANES]
             first = (levels + level) * LANES
@@ -111,19 +109,15 @@
                 top = picked.astype(BF16).astype(F32)
                 rest = picked - top
                 here = index >= 0
-                slot = (block * y_blocks + y) * levels + level
+                slot = y * levels + level
                 for part in range(2):
                     lanes = slice(part * LANES, (part + 1) * LANES)
                     keep = here if part == 0 else jnp.logical_not(here)
-                    band_ref[slot, pl.ds(at, BLOCK_Y), lanes] = jnp.where(keep, top, 0.0).astype(BF16)
-                    band_ref[slot, pl.ds(low, BLOCK_Y), lanes] = jnp.where(keep, rest, 0.0).astype(BF16)
-
-    def group_of(group, carry):
-        for step in range(UNROLL):
-            column(group * UNROLL + step)
-        return carry
-
-    lax.fori_loop(0, groups, group_of, 0)
+                    band_ref[slot, at : at + BLOCK_Y, lanes] = jnp.where(keep, top, 0.0).astype(BF16)
+                    band_ref[slot, low : low + BLOCK_Y, lanes] = jnp.where(keep, rest, 0.0).astype(BF16)
+
+    for step in range(BLOCK_X):
+        column(block * BLOCK_X + step)
 
 
 def pack_kernel(cells_ref, edges_ref, message_ref, outer_ref, low_ref, high_ref, sems):
@@ -175,7 +169,8 @@
     clear(relay_ref, corner + 2 * strip)
 
 
-def join_kernel(cols, width, message_ref, got_ref, other_ref, run_ref):
+def join_kernel(cols, width, message_ref, got_ref, other_ref, after_ref, run_ref):
+    del after_ref
     even = lax.axis_index("gx") % 2 == 0
     corner, strip = 2 * width * HALO, width * cols
     mine, far = message_ref[:strip], got_ref[:strip]
@@ -233,7 +228,7 @@
     clear(second_ref, wide * width)
 
 
-def block_sum(field_ref, band_ref, x, y, y_blocks, levels, level):
+def block_sum(field_ref, bands, x, y, levels, level):
     size = BLOCK_X * BLOCK_Y
     reach = BLOCK_X + 2 * HALO
     begin = (y * BLOCK_Y + LEAD - HALO) * levels + level
@@ -247,19 +242,19 @@
     )
     top = points.astype(BF16)
     rest = (points - top.astype(F32)).astype(BF16)
-    band = band_ref[(x * y_blocks + y) * levels + level]
+    band = bands[x][y * levels + level]
     product = jnp.dot(band, jnp.concatenate([top, rest], axis=1), preferred_element_type=F32)
     return product[:size, :LANES] + (product[:size, LANES:] + product[size:, :LANES])
 
 
-def remap_rows(field_ref, band_ref, stage_ref, out_ref, sems, levels, y_blocks, which):
+def remap_rows(field_ref, bands, stage_ref, out_ref, sems, levels, which):
     x_blocks = stage_ref.shape[1] // BLOCK_X
     deep = BLOCK_Y * levels
     copies = []
     for at, y in enumerate(which):
         for level in range(levels):
             for x in range(x_blocks):
-                total = block_sum(field_ref, band_ref, x, y, y_blocks, levels, level)
+                total = block_sum(field_ref, bands, x, y, levels, level)
                 for c in range(BLOCK_X):
                     stage_ref[at, x * BLOCK_X + c, pl.ds(level, BLOCK_Y, stride=levels), :] = total[
                         c * BLOCK_Y : (c + 1) * BLOCK_Y
@@ -274,9 +269,9 @@
         copy.wait()
 
 
-def middle_kernel(levels, cells_ref, inner_ref, outer_ref, band_ref, after_ref, out_ref, field_ref,
-                  stage_ref, sems):
+def middle_kernel(levels, cells_ref, inner_ref, outer_ref, after_ref, *refs):
     del after_ref
+    *bands, out_ref, field_ref, stage_ref, sems = refs
     cols, rows, _ = cells_ref.shape
     lead = LEAD * levels
     even = lax.axis_index("gx") % 2 == 0
@@ -287,14 +282,13 @@
         field_ref[col, lead : lead + rows] = jnp.where(even, outer, inner)
         field_ref[HALO + cols + col, lead : lead + rows] = jnp.where(even, inner, outer)
     y_blocks = rows // levels // BLOCK_Y
-    remap_rows(
-        field_ref, band_ref, stage_ref, out_ref, sems, levels, y_blocks, range(1, y_blocks - 1)
-    )
+    remap_rows(field_ref, bands, stage_ref, out_ref, sems, levels, range(1, y_blocks - 1))
 
 
 def edge_kernel(levels, cols, rows, count, ends, run, table_ref, first_ref, second_ref, run_ref,
-                band_ref, field_in, out_in, field_ref, out_ref, stage_ref, sems):
+                field_in, out_in, *refs):
     del field_in, out_in
+    *bands, field_ref, out_ref, stage_ref, sems = refs
     width = HALO * levels
     lead = LEAD * levels
     place = lax.axis_index("gy")
@@ -320,9 +314,7 @@
         field_ref[u, lead + rows : lead + rows + width] = jnp.where(flat_place, plain, strip)
         field_ref[u, lead + rows + width :] = jnp.zeros((tail, LANES), F32)
     y_blocks = rows // levels // BLOCK_Y
-    remap_rows(
-        field_ref, band_ref, stage_ref, out_ref, sems, levels, y_blocks, (0, y_blocks - 1)
-    )
+    remap_rows(field_ref, bands, stage_ref, out_ref, sems, levels, (0, y_blocks - 1))
 
 
 def grant(mebibytes):
@@ -415,6 +407,20 @@
         cost_estimate=takes(1.0),
     )(*[in_hbm(a) for a in (owner, codes, cells, weights, offsets, matrix)], message)
 
+    x_blocks, y_blocks = cols // BLOCK_X, rows // BLOCK_Y
+
+    def band_of(block, after):
+        return pl.pallas_call(
+            functools.partial(band_kernel, levels, rows, block),
+            out_shape=shaped(y_blocks * levels, 2 * BLOCK_X * BLOCK_Y, 2 * LANES, dtype=BF16),
+            in_specs=[VMEM] * 3 + [ANY],
+            out_specs=VMEM,
+            name="band",
+            compiler_params=grant(4),
+            cost_estimate=takes(0.5),
+        )(weights, offsets, matrix, after)
+
+    bands = [band_of(0, table)]
     relay = pl.pallas_call(
         functools.partial(relay_kernel, cols, width),
         out_shape=shaped(eights(corner + 2 * strip), lanes),
@@ -423,19 +429,20 @@
         name="relay",
         compiler_params=grant(2),
         cost_estimate=takes(0.5),
-    )(edges, message, got, table)
+    )(edges, message, got, bands[0])
     other = lax.ppermute(relay, "gx", partner)
     inner_got = lax.ppermute(inner, "gx", partner)
 
+    bands.append(band_of(1, relay))
     ring = pl.pallas_call(
         functools.partial(join_kernel, cols, width),
         out_shape=shaped(run * strip, lanes),
-        in_specs=[VMEM] * 3,
+        in_specs=[VMEM] * 3 + [ANY],
         out_specs=VMEM,
         name="join",
         compiler_params=grant(2),
         cost_estimate=takes(0.5),
-    )(message, got, other)
+    )(message, got, other, bands[1])
     while run < held:
         shift = run
         more = lax.ppermute(ring, "gx", [((i + shift) % count, i) for i in range(count)])
@@ -455,17 +462,7 @@
     first_got = lax.ppermute(first, axes, first_swap)
     second_got = lax.ppermute(second, axes, second_swap)
 
-    y_blocks = rows // BLOCK_Y
-    slots = cols // BLOCK_X * y_blocks * levels
-    band = pl.pallas_call(
-        functools.partial(band_kernel, levels, rows),
-        out_shape=shaped(slots, 2 * BLOCK_X * BLOCK_Y, 2 * LANES, dtype=BF16),
-        in_specs=[VMEM] * 3 + [ANY],
-        out_specs=VMEM,
-        name="band",
-        compiler_params=grant(6),
-        cost_estimate=takes(1.5),
-    )(weights, offsets, matrix, first)
+    bands.extend(band_of(block, second) for block in range(2, x_blocks))
 
     field_rows = eights((LEAD + rows + HALO + PITCH - BLOCK_Y - 2 * HALO) * levels)
     field_shape = shaped(cols + 2 * HALO, field_rows, lanes)
@@ -474,7 +471,7 @@
     partial, field = pl.pallas_call(
         functools.partial(middle_kernel, levels),
         out_shape=(out_shape, field_shape),
-        in_specs=[VMEM] * 4 + [ANY],
+        in_specs=[VMEM] * 3 + [ANY] + [VMEM] * x_blocks,
         out_specs=(HBM, VMEM),
         scratch_shapes=[
             pltpu.VMEM((y_blocks - 2, *stage), F32),
@@ -483,18 +480,18 @@
         name="middle",
         cost_estimate=takes(2.0),
         compiler_params=grant(6),
-    )(cells, inner_got, outer_got, band, first)
+    )(cells, inner_got, outer_got, second, *bands)
     _, updated = pl.pallas_call(
         functools.partial(edge_kernel, levels, cols, rows * levels, count, ends, run),
         out_shape=(field_shape, out_shape),
-        in_specs=[VMEM] * 6 + [HBM],
+        in_specs=[VMEM] * 5 + [HBM] + [VMEM] * x_blocks,
         out_specs=(VMEM, HBM),
         scratch_shapes=[pltpu.VMEM((2, *stage), F32), pltpu.SemaphoreType.DMA((2,))],
-        input_output_aliases={5: 0, 6: 1},
+        input_output_aliases={4: 0, 5: 1},
         name="edge",
         cost_estimate=takes(2.0),
         compiler_params=grant(6),
-    )(table, first_got, second_got, ring, band, field, partial)
+    )(table, first_got, second_got, ring, field, partial, *bands)
     return updated.reshape(cols, rows, levels, lanes)
 
 

time: 16.2 us -> 16.2 us (level)
  waiting for transfers between devices: 2.28 us -> 2.95 us
  starting transfers between devices: 7.69 us -> 7.13 us
    ppermute x1, waiting for transfers between devices: 0.01 us -> 1.24 us  [on_device(): second_got = lax.ppermute(second, axes, second_swap)]
    ppermute x1, starting transfers between devices: 1.9 us -> 1.01 us  [on_device(): second_got = lax.ppermute(second, axes, second_swap)]
    ppermute x1, waiting for transfers between devices: 0.99 us -> 0.54 us  [on_device(): got = lax.ppermute(message, 'gx', across)]
    ppermute x1, waiting for transfers between devices: 1.28 us -> 0.83 us  [on_device(): other = lax.ppermute(relay, 'gx', partner)]
    ppermute x1, starting transfers between devices: 2.14 us -> 2.47 us  [on_device(): first_got = lax.ppermute(first, axes, first_swap)]
    ppermute x1, waiting for transfers between devices: 0.01 us -> 0.33 us  [on_device(): outer_got = lax.ppermute(outer, 'gx', across)]
    pallas_call x1 -> x3, Pallas kernels: 1.36 us -> 1.34 us  [band_of(): pl.pallas_call(functools.partial(band_kernel, levels, rows, block), out_s...]
  transfers between devices with their start and end apart: 6 -> 6, of which waited for: 2 -> 4; matrix products, arithmetic and copies ran while one was open for 0% -> 0% of each run, Pallas kernels for 23% -> 23%
where the time goes in v4:
time: 16.2 us; the launch traced here: 16.1 us
  starting transfers between devices  7.13 us (44%)
  Pallas kernels  5.93 us (37%)
  waiting for transfers between devices  2.95 us (18%)
    ppermute x1, starting transfers between devices, on_device(): got = lax.ppermute(message, 'gx', across)  3.43 us
    ppermute x1, starting transfers between devices, on_device(): first_got = lax.ppermute(first, axes, first_swap)  2.47 us
    pallas_call x3, Pallas kernels, band_of(): pl.pallas_call(functools.partial(band_kernel, levels, rows, block), out_s...  1.34 us
    ppermute x1, waiting for transfers between devices, on_device(): second_got = lax.ppermute(second, axes, second_swap)  1.24 us
    pallas_call x1, Pallas kernels, on_device(): pl.pallas_call(functools.partial(edge_kernel, levels, cols, rows * levels...  1.17 us
    pallas_call x1, Pallas kernels, on_device(): pl.pallas_call(functools.partial(load_kernel, count, ends, held), out_sha...  1.15 us
    pallas_call x1, Pallas kernels, on_device(): pl.pallas_call(functools.partial(middle_kernel, levels), out_shape=(out_s...  1.13 us
    pallas_call x1, Pallas kernels, on_device(): pl.pallas_call(pack_kernel, out_shape=(shaped(2 * strip, lanes), shaped(e...  1.04 us
  transfers between devices with their start and end apart: 6, of which 4 were waited for; matrix products, arithmetic and copies ran while one was open for 0% of the time, Pallas kernels for 23%

profile of v4, /device:TPU:0, one launch (start us, length us, event | category | flops | bytes accessed | tf_op | source)
XLA Modules:
  0.0 16.1 jit_solution(5919817168748931507)
XLA Ops:
  0.0 1.0 %pack.1 = (f32[144,128]{1,0:T(8,128)S(1)}, f32[112,128]{1,0:T(8,128)S(1)}, f32[3,128,128]{2,1,0:T(8,128)S(1)}) custom-call(f32[12,128,128]{2,1,0:T(8,128)} %bitcast.4), custom_call_target="tpu_custom_call" | custom-call | bytes 3000000 | tf_op jit(solution)/shard_map/pack/pallas_call | solution.py:368
  1.0 3.4 %collective-permute-start = (f32[112,128]{1,0:T(8,128)S(1)}, f32[112,128]{1,0:T(8,128)S(1)}, u32[]{:S(2)}, u32[]{:S(2)}) collective-permute-start(f32[112,128]{1,0:T(8,128)S(1)} %get-tuple-element.18.after_ref.message_ref), channel_id=1, source_target_pairs={{0,28},{4,8},{8,4},{12,16},{16,12},{20,24},{24,20},{28,0},{1,29},{... | collective-permute-start | bytes 172040 | tf_op jit(solution)/shard_map/ppermute | solution.py:382
  4.5 0.1 collective-permute-start.5
  4.6 1.1 %load.1 = (s32[8,128]{1,0:T(8,128)S(1)}, f32[3,128,128]{2,1,0:T(8,128)S(1)}, f32[12,48,64]{2,1,0:T(8,128)S(1)}, s32[12,4,64]{2,1,0:T(4,128)S(1)}, bf16[104,512]{1,0:T(8,128)(2,1)S(1)}) custom-call(s32[2,8]{1,0:T(2,128)} %owner_ref.1, s32[2,8]{1,0:T(2,128)} %codes_ref.1, f32[12,128,128]{2,1,0:T(8,128)} %bitcast.5, f32[12,48,64]{2,1,0:T(8,128)} %bitcast.7, ...), custom_call_target="tpu_custom_call" | custom-call | bytes 3000000 | tf_op jit(solution)/shard_map/load/pallas_call | solution.py:389
  5.7 0.1 collective-permute-start.4
  5.8 0.4 %band.3.after_ref.refs_0_ = bf16[8,128,256]{2,1,0:T(8,128)(2,1)S(1)} custom-call(f32[12,48,64]{2,1,0:T(8,128)S(1)} %get-tuple-element.21.weights_ref, s32[12,4,64]{2,1,0:T(4,128)S(1)} %get-tuple-element.22.offsets_ref, bf16[104,512]{1,0:T(8,128)(2,1)S(1)} %get-tuple-element.23.matrix_ref, s32[8,128]{1,0:T(8,128)S(1)} %get-tuple-element.19.after_ref.table_ref), custom_call_target="tpu_custom_call" | custom-call | bytes 1500000 | tf_op jit(solution)/shard_map/band/pallas_call | solution.py:413
  6.2 0.5 %collective-permute-done.got_ref = f32[112,128]{1,0:T(8,128)S(1)} collective-permute-done((f32[112,128]{1,0:T(8,128)S(1)}, f32[112,128]{1,0:T(8,128)S(1)}, u32[]{:S(2)}, u32[]{:S(2)}) %collective-permute-start) | collective-permute-done | bytes 57376 | tf_op jit(solution)/shard_map/ppermute | solution.py:382
  6.8 0.0 copy-start
  6.8 0.1 collective-permute-start.1
  6.9 0.4 %band.4.after_ref.refs_1_ = bf16[8,128,256]{2,1,0:T(8,128)(2,1)S(1)} custom-call(f32[12,48,64]{2,1,0:T(8,128)S(1)} %get-tuple-element.21.weights_ref, s32[12,4,64]{2,1,0:T(4,128)S(1)} %get-tuple-element.22.offsets_ref, bf16[104,512]{1,0:T(8,128)(2,1)S(1)} %get-tuple-element.23.matrix_ref, f32[184,128]{1,0:T(8,128)S(1)} %relay.1.after_ref), custom_call_target="tpu_custom_call" | custom-call | bytes 1500000 | tf_op jit(solution)/shard_map/band/pallas_call | solution.py:413
  7.3 0.8 %collective-permute-done.1.other_ref = f32[184,128]{1,0:T(8,128)S(1)} collective-permute-done((f32[184,128]{1,0:T(8,128)S(1)}, f32[184,128]{1,0:T(8,128)S(1)}, u32[]{:S(2)}, u32[]{:S(2)}) %collective-permute-start.1) | collective-permute-done | bytes 94240 | tf_op jit(solution)/shard_map/ppermute | solution.py:433
  8.2 0.1 rows.1
  8.3 2.5 %collective-permute-start.2 = (f32[112,128]{1,0:T(8,128)S(1)}, f32[112,128]{1,0:T(8,128)S(1)}, u32[]{:S(2)}, u32[]{:S(2)}) collective-permute-start(f32[112,128]{1,0:T(8,128)S(1)} %get-tuple-element.24), channel_id=1, source_target_pairs={{0,1},{1,0},{2,3},{3,2},{4,5},{5,4},{6,7},{7,6},{8,9},{9,8},{10,11... | collective-permute-start | bytes 172040 | tf_op jit(solution)/shard_map/ppermute | solution.py:462
  10.7 1.0 %collective-permute-start.3 = (f32[112,128]{1,0:T(8,128)S(1)}, f32[112,128]{1,0:T(8,128)S(1)}, u32[]{:S(2)}, u32[]{:S(2)}) collective-permute-start(f32[112,128]{1,0:T(8,128)S(1)} %get-tuple-element.25.after_ref), channel_id=1, source_target_pairs={{0,16},{1,2},{2,1},{3,19},{4,20},{5,6},{6,5},{7,23},{8,24},{9,10},... | collective-permute-start | bytes 172040 | tf_op jit(solution)/shard_map/ppermute | solution.py:463
  11.8 0.4 %band.5.refs_2_ = bf16[8,128,256]{2,1,0:T(8,128)(2,1)S(1)} custom-call(f32[12,48,64]{2,1,0:T(8,128)S(1)} %get-tuple-element.21.weights_ref, s32[12,4,64]{2,1,0:T(4,128)S(1)} %get-tuple-element.22.offsets_ref, bf16[104,512]{1,0:T(8,128)(2,1)S(1)} %get-tuple-element.23.matrix_ref, f32[112,128]{1,0:T(8,128)S(1)} %get-tuple-element.25.after_ref), custom_call_target="tpu_custom_call" | custom-call | bytes 1500000 | tf_op jit(solution)/shard_map/band/pallas_call | solution.py:413
  12.2 0.3 %collective-permute-done.5.outer_ref = f32[3,128,128]{2,1,0:T(8,128)S(1)} collective-permute-done((f32[3,128,128]{2,1,0:T(8,128)S(1)}, f32[3,128,128]{2,1,0:T(8,128)S(1)}, u32[]{:S(2)}, u32[]{:S(2)}) %collective-permute-start.5) | collective-permute-done | bytes 196640 | tf_op jit(solution)/shard_map/ppermute | solution.py:383
  12.5 0.0 collective-permute-done.4.inner_ref
  12.5 0.0 copy-done
  12.5 1.1 %middle.1 = (f32[12,128,128]{2,1,0:T(8,128)}, f32[18,152,128]{2,1,0:T(8,128)S(1)}) custom-call(f32[12,128,128]{2,1,0:T(8,128)S(1)} %bitcast.6, f32[3,128,128]{2,1,0:T(8,128)S(1)} %collective-permute-done.4.inner_ref, f32[3,128,128]{2,1,0:T(8,128)S(1)} %collective-permute-done.5.outer_ref, f32[112,128]{1,0:T(8,128)S(1)} %get-tuple-element.25.after_ref, ...), custom_call_target="tpu_custom_call" | custom-call | bytes 6000000 | tf_op jit(solution)/shard_map/middle/pallas_call | solution.py:471
  13.7 0.0 collective-permute-done.2.first_ref
  13.7 1.2 %collective-permute-done.3.second_ref = f32[112,128]{1,0:T(8,128)S(1)} collective-permute-done((f32[112,128]{1,0:T(8,128)S(1)}, f32[112,128]{1,0:T(8,128)S(1)}, u32[]{:S(2)}, u32[]{:S(2)}) %collective-permute-start.3) | collective-permute-done | bytes 57376 | tf_op jit(solution)/shard_map/ppermute | solution.py:463
  14.9 1.2 %edge.1 = (f32[18,152,128]{2,1,0:T(8,128)S(1)}, f32[12,128,128]{2,1,0:T(8,128)}) custom-call(s32[8,128]{1,0:T(8,128)S(1)} %get-tuple-element.19.after_ref.table_ref, f32[112,128]{1,0:T(8,128)S(1)} %collective-permute-done.2.first_ref, f32[112,128]{1,0:T(8,128)S(1)} %collective-permute-done.3.second_ref, ...), custom_call_target="tpu_custom_call", output_to_operand_aliasing={{0}: (4, {}), {1}: (5, {})} | custom-call | bytes 6000000 | tf_op jit(solution)/shard_map/edge/pallas_call | solution.py:484
  (2 shorter events, 0.0 us)
Async XLA Ops:
  1.0 5.7 %collective-permute-start = (f32[112,128]{1,0:T(8,128)S(1)}, f32[112,128]{1,0:T(8,128)S(1)}, u32[]{:S(2)}, u32[]{:S(2)}) collective-permute-start(f32[112,128]{1,0:T(8,128)S(1)} %get-tuple-element.18.after_ref.message_ref), channel_id=1, source_target_pairs={{0,28},{4,8},{8,4},{12,16},{16,12},{20,24},{24,20},{28,0},{1,29},{... | collective-permute-start | bytes 172040 | tf_op jit(solution)/shard_map/ppermute | solution.py:382
  4.5 8.1 %collective-permute-start.5 = (f32[3,128,128]{2,1,0:T(8,128)S(1)}, f32[3,128,128]{2,1,0:T(8,128)S(1)}, u32[]{:S(2)}, u32[]{:S(2)}) collective-permute-start(f32[3,128,128]{2,1,0:T(8,128)S(1)} %get-tuple-element.27), channel_id=1, source_target_pairs={{0,28},{4,8},{8,4},{12,16},{16,12},{20,24},{24,20},{28,0},{1,29},{... | collective-permute-start | bytes 589832 | tf_op jit(solution)/shard_map/ppermute | solution.py:383
  5.7 6.8 %collective-permute-start.4 = (f32[3,128,128]{2,1,0:T(8,128)S(1)}, f32[3,128,128]{2,1,0:T(8,128)S(1)}, u32[]{:S(2)}, u32[]{:S(2)}) collective-permute-start(f32[3,128,128]{2,1,0:T(8,128)S(1)} %get-tuple-element.26), channel_id=1, source_target_pairs={{0,4},{4,0},{8,12},{12,8},{16,20},{20,16},{24,28},{28,24},{1,5},{5... | collective-permute-start | bytes 589832 | tf_op jit(solution)/shard_map/ppermute | solution.py:434
  6.8 5.7 %copy-start = (f32[12,64,2,128]{3,2,1,0:T(2,128)S(1)}, f32[12,64,2,128]{3,2,1,0:T(2,128)}, u32[]{:S(2)}) copy-start(f32[12,64,2,128]{3,2,1,0:T(2,128)} %param.6) | copy-start | bytes 2359300
  6.8 1.4 %collective-permute-start.1 = (f32[184,128]{1,0:T(8,128)S(1)}, f32[184,128]{1,0:T(8,128)S(1)}, u32[]{:S(2)}, u32[]{:S(2)}) collective-permute-start(f32[184,128]{1,0:T(8,128)S(1)} %relay.1.after_ref), channel_id=1, source_target_pairs={{0,4},{4,0},{8,12},{12,8},{16,20},{20,16},{24,28},{28,24},{1,5},{5... | collective-permute-start | bytes 282632 | tf_op jit(solution)/shard_map/ppermute | solution.py:433
  8.3 5.4 %collective-permute-start.2 = (f32[112,128]{1,0:T(8,128)S(1)}, f32[112,128]{1,0:T(8,128)S(1)}, u32[]{:S(2)}, u32[]{:S(2)}) collective-permute-start(f32[112,128]{1,0:T(8,128)S(1)} %get-tuple-element.24), channel_id=1, source_target_pairs={{0,1},{1,0},{2,3},{3,2},{4,5},{5,4},{6,7},{7,6},{8,9},{9,8},{10,11... | collective-permute-start | bytes 172040 | tf_op jit(solution)/shard_map/ppermute | solution.py:462
  10.7 4.2 %collective-permute-start.3 = (f32[112,128]{1,0:T(8,128)S(1)}, f32[112,128]{1,0:T(8,128)S(1)}, u32[]{:S(2)}, u32[]{:S(2)}) collective-permute-start(f32[112,128]{1,0:T(8,128)S(1)} %get-tuple-element.25.after_ref), channel_id=1, source_target_pairs={{0,16},{1,2},{2,1},{3,19},{4,20},{5,6},{6,5},{7,23},{8,24},{9,10},... | collective-permute-start | bytes 172040 | tf_op jit(solution)/shard_map/ppermute | solution.py:463

commit v5 on v4

--- a/solution.py
+++ b/solution.py
@@ -47,10 +47,12 @@
 
 def load_kernel(count, ends, run, owner_ref, codes_ref, cells_ref, weights_ref, offsets_ref,
                 matrix_ref, after_ref, table_ref, inner_ref, weights_out, offsets_out, matrix_out,
-                owner, codes, sems):
+                field_ref, owner, codes, sems):
     del after_ref
     index, place = lax.axis_index("gx"), lax.axis_index("gy")
-    last = cells_ref.shape[0] - HALO
+    cols, rows, _ = cells_ref.shape
+    lead = LEAD * (weights_ref.shape[1] // 24)
+    last = cols - HALO
     pairs = [
         (owner_ref, owner),
         (codes_ref, codes),
@@ -59,6 +61,9 @@
         (offsets_ref, offsets_out),
         (matrix_ref, matrix_out),
     ]
+    for col in range(0, cols, BLOCK_X):
+        to = field_ref.at[pl.ds(HALO + col, BLOCK_X), pl.ds(lead, rows)]
+        pairs.append((cells_ref.at[pl.ds(col, BLOCK_X)], to))
     copies = [pltpu.make_async_copy(a, b, sems.at[at]) for at, (a, b) in enumerate(pairs)]
     for copy in copies:
         copy.start()
@@ -158,15 +163,32 @@
         ref[at:] = jnp.zeros((ref.shape[0] - at, LANES), F32)
 
 
-def relay_kernel(cols, width, edges_ref, message_ref, got_ref, after_ref, relay_ref):
+def relay_kernel(cols, width, edges_ref, message_ref, got_ref, after_ref, relay_ref, first_ref):
     del after_ref
     even = lax.axis_index("gx") % 2 == 0
+    up = lax.axis_index("gy") % 2 == 0
     corner, strip = 2 * width * HALO, width * cols
     edges = 2 * strip
     relay_ref[:corner] = jnp.where(even, edges_ref[edges - corner : edges], edges_ref[:corner])
     relay_ref[corner : corner + strip] = message_ref[:strip]
     relay_ref[corner + strip : corner + 2 * strip] = got_ref[:strip]
     clear(relay_ref, corner + 2 * strip)
+    for u in range(HALO + cols):
+        ref, at = (got_ref, strip) if u < HALO else (edges_ref, -corner)
+        at += 2 * width * u
+        first_ref[u * width : (u + 1) * width] = jnp.where(
+            up, ref[at + width : at + 2 * width], ref[at : at + width]
+        )
+    clear(first_ref, (HALO + cols) * width)
+
+
+def turn_kernel(cols, width, first_ref, *refs):
+    corner_ref = refs[-1]
+    even = lax.axis_index("gx") % 2 == 0
+    size = HALO * width
+    last = (HALO + cols) * width
+    corner_ref[:size] = jnp.where(even, first_ref[last - size : last], first_ref[size : 2 * size])
+    clear(corner_ref, size)
 
 
 def join_kernel(cols, width, message_ref, got_ref, other_ref, after_ref, run_ref):
@@ -199,9 +221,9 @@
 
 
 def rows_kernel(cols, width, count, ends, run, table_ref, edges_ref, other_ref, got_ref, run_ref,
-                first_ref, second_ref):
+                second_ref):
     even, place = lax.axis_index("gx") % 2 == 0, lax.axis_index("gy")
-    flat_place = place % 2 == 0
+    top = place % 2 == 1
     strip = width * cols
 
     def rows(ref, at, top):
@@ -221,10 +243,8 @@
     is_end = jnp.logical_or(place == 0, place == ends - 1)
     for u in range(wide):
         to = slice(u * width, (u + 1) * width)
-        first_ref[to] = column(u, flat_place)
         _, glued = window.column(start, u)
-        second_ref[to] = jnp.where(is_end, glued, column(u, jnp.logical_not(flat_place)))
-    clear(first_ref, wide * width)
+        second_ref[to] = jnp.where(is_end, glued, column(u, top))
     clear(second_ref, wide * width)
 
 
@@ -247,51 +267,48 @@
     return product[:size, :LANES] + (product[:size, LANES:] + product[size:, :LANES])
 
 
-def remap_rows(field_ref, bands, stage_ref, out_ref, sems, levels, which):
-    x_blocks = stage_ref.shape[1] // BLOCK_X
-    deep = BLOCK_Y * levels
-    copies = []
-    for at, y in enumerate(which):
+def remap_blocks(field_ref, bands, stage_ref, levels, blocks, ready=None):
+    for at, (x, y) in enumerate(blocks):
         for level in range(levels):
-            for x in range(x_blocks):
-                total = block_sum(field_ref, bands, x, y, levels, level)
-                for c in range(BLOCK_X):
-                    stage_ref[at, x * BLOCK_X + c, pl.ds(level, BLOCK_Y, stride=levels), :] = total[
-                        c * BLOCK_Y : (c + 1) * BLOCK_Y
-                    ]
-        copies.append(
-            pltpu.make_async_copy(
-                stage_ref.at[at], out_ref.at[:, pl.ds(y * deep, deep)], sems.at[at]
-            )
-        )
-        copies[-1].start()
-    for copy in copies:
-        copy.wait()
-
-
-def middle_kernel(levels, cells_ref, inner_ref, outer_ref, after_ref, *refs):
-    del after_ref
-    *bands, out_ref, field_ref, stage_ref, sems = refs
-    cols, rows, _ = cells_ref.shape
+            total = block_sum(field_ref, bands, x, y, levels, level)
+            for c in range(BLOCK_X):
+                stage_ref[at, c, pl.ds(level, BLOCK_Y, stride=levels), :] = total[
+                    c * BLOCK_Y : (c + 1) * BLOCK_Y
+                ]
+        if ready is not None:
+            ready(at, x, y)
+
+
+def middle_kernel(levels, blocks, inner_ref, outer_ref, after_ref, field_in, *refs):
+    del after_ref, field_in
+    *bands, field_ref, stage_ref = refs
+    rows, wide = inner_ref.shape[1], field_ref.shape[0]
     lead = LEAD * levels
     even = lax.axis_index("gx") % 2 == 0
-    for col in range(cols):
-        field_ref[HALO + col, lead : lead + rows] = cells_ref[col]
     for col in range(HALO):
         inner, outer = inner_ref[col], outer_ref[col]
         field_ref[col, lead : lead + rows] = jnp.where(even, outer, inner)
-        field_ref[HALO + cols + col, lead : lead + rows] = jnp.where(even, inner, outer)
-    y_blocks = rows // levels // BLOCK_Y
-    remap_rows(field_ref, bands, stage_ref, out_ref, sems, levels, range(1, y_blocks - 1))
-
-
-def edge_kernel(levels, cols, rows, count, ends, run, table_ref, first_ref, second_ref, run_ref,
-                field_in, out_in, *refs):
-    del field_in, out_in
+        field_ref[wide - HALO + col, lead : lead + rows] = jnp.where(even, inner, outer)
+    remap_blocks(field_ref, bands, stage_ref, levels, blocks)
+
+
+def edge_kernel(levels, cols, rows, count, ends, run, blocks, done, table_ref, first_ref, corner_ref,
+                second_ref, run_ref, done_ref, field_in, *refs):
+    del field_in
     *bands, field_ref, out_ref, stage_ref, sems = refs
+    deep = BLOCK_Y * levels
+    copies = []
+
+    def put(source, x, y):
+        to = out_ref.at[pl.ds(x * BLOCK_X, BLOCK_X), pl.ds(y * deep, deep)]
+        copies.append(pltpu.make_async_copy(source, to, sems.at[len(copies)]))
+        copies[-1].start()
+
+    for at, (x, y) in enumerate(done):
+        put(done_ref.at[at], x, y)
     width = HALO * levels
     lead = LEAD * levels
-    place = lax.axis_index("gy")
+    even, place = lax.axis_index("gx") % 2 == 0, lax.axis_index("gy")
     flat_place = place % 2 == 0
     wide = cols + 2 * HALO
     window = Window(cols, width, count, run, run_ref)
@@ -301,7 +318,13 @@
     flipped = code // 2 % 2 == 1
     tail = field_ref.shape[1] - lead - rows - width
     for u in range(wide):
-        plain = first_ref[u * width : (u + 1) * width]
+        if HALO <= u < HALO + cols:
+            plain = first_ref[u * width : (u + 1) * width]
+        else:
+            col = u if u < HALO else u - HALO - cols
+            far = first_ref[col * width : (col + 1) * width]
+            near = corner_ref[col * width : (col + 1) * width]
+            plain = jnp.where(even == (u < HALO), far, near)
         step = jnp.where(mirrored, wide - 1 - u, u)
         held, glued = window.column(start, step)
         come = second_ref[pl.ds(step * width, width)]
@@ -313,8 +336,12 @@
         field_ref[u, lead - width : lead] = jnp.where(flat_place, strip, plain)
         field_ref[u, lead + rows : lead + rows + width] = jnp.where(flat_place, plain, strip)
         field_ref[u, lead + rows + width :] = jnp.zeros((tail, LANES), F32)
-    y_blocks = rows // levels // BLOCK_Y
-    remap_rows(field_ref, bands, stage_ref, out_ref, sems, levels, (0, y_blocks - 1))
+    remap_blocks(
+        field_ref, bands, stage_ref, levels, blocks,
+        lambda at, x, y: put(stage_ref.at[at], x, y),
+    )
+    for copy in copies:
+        copy.wait()
 
 
 def grant(mebibytes):
@@ -382,11 +409,13 @@
     got = lax.ppermute(message, "gx", across)
     outer_got = lax.ppermute(outer, "gx", across)
 
+    field_rows = eights((LEAD + rows + HALO + PITCH - BLOCK_Y - 2 * HALO) * levels)
+    field_shape = shaped(cols + 2 * HALO, field_rows, lanes)
     run = 4
     held = max(run, count // 2)
     weights = jnp.swapaxes(weights, 1, 2)
     offsets = jnp.swapaxes(offsets, 1, 2)
-    table, inner, weights, offsets, matrix = pl.pallas_call(
+    load = pl.pallas_call(
         functools.partial(load_kernel, count, ends, held),
         out_shape=(
             shaped(8, lanes, dtype=jnp.int32),
@@ -394,18 +423,22 @@
             shaped(*weights.shape),
             shaped(*offsets.shape, dtype=jnp.int32),
             shaped(*matrix.shape, dtype=BF16),
+            field_shape,
         ),
         in_specs=[HBM] * 6 + [ANY],
-        out_specs=(VMEM,) * 5,
+        out_specs=(VMEM,) * 6,
         scratch_shapes=[
             pltpu.SMEM(owner.shape, jnp.int32),
             pltpu.SMEM(codes.shape, jnp.int32),
-            pltpu.SemaphoreType.DMA((6,)),
+            pltpu.SemaphoreType.DMA((6 + cols // BLOCK_X,)),
         ],
         name="load",
         compiler_params=grant(4),
         cost_estimate=takes(1.0),
-    )(*[in_hbm(a) for a in (owner, codes, cells, weights, offsets, matrix)], message)
+    )
+    table, inner, weights, offsets, matrix, field = load(
+        *[in_hbm(a) for a in (owner, codes, cells, weights, offsets, matrix)], message
+    )
 
     x_blocks, y_blocks = cols // BLOCK_X, rows // BLOCK_Y
 
@@ -420,20 +453,22 @@
             cost_estimate=takes(0.5),
         )(weights, offsets, matrix, after)
 
-    bands = [band_of(0, table)]
-    relay = pl.pallas_call(
+    relay, first = pl.pallas_call(
         functools.partial(relay_kernel, cols, width),
-        out_shape=shaped(eights(corner + 2 * strip), lanes),
+        out_shape=(
+            shaped(eights(corner + 2 * strip), lanes),
+            shaped(eights(width * (cols + HALO)), lanes),
+        ),
         in_specs=[VMEM] * 3 + [ANY],
-        out_specs=VMEM,
+        out_specs=(VMEM, VMEM),
         name="relay",
         compiler_params=grant(2),
         cost_estimate=takes(0.5),
-    )(edges, message, got, bands[0])
+    )(edges, message, got, table)
     other = lax.ppermute(relay, "gx", partner)
+    first_got = lax.ppermute(first, axes, first_swap)
     inner_got = lax.ppermute(inner, "gx", partner)
 
-    bands.append(band_of(1, relay))
     ring = pl.pallas_call(
         functools.partial(join_kernel, cols, width),
         out_shape=shaped(run * strip, lanes),
@@ -442,7 +477,7 @@
         name="join",
         compiler_params=grant(2),
         cost_estimate=takes(0.5),
-    )(message, got, other, bands[1])
+    )(message, got, other, relay)
     while run < held:
         shift = run
         more = lax.ppermute(ring, "gx", [((i + shift) % count, i) for i in range(count)])
@@ -450,48 +485,59 @@
         run *= 2
 
     z_rows = eights(width * (cols + 2 * HALO))
-    first, second = pl.pallas_call(
+    second = pl.pallas_call(
         functools.partial(rows_kernel, cols, width, count, ends, run),
-        out_shape=(shaped(z_rows, lanes), shaped(z_rows, lanes)),
+        out_shape=shaped(z_rows, lanes),
         in_specs=[VMEM] * 5,
-        out_specs=(VMEM, VMEM),
+        out_specs=VMEM,
         name="rows",
         cost_estimate=takes(1.0),
         compiler_params=grant(2 * pl.cdiv(run, 8)),
     )(table, edges, other, got, ring)
-    first_got = lax.ppermute(first, axes, first_swap)
     second_got = lax.ppermute(second, axes, second_swap)
 
-    bands.extend(band_of(block, second) for block in range(2, x_blocks))
-
-    field_rows = eights((LEAD + rows + HALO + PITCH - BLOCK_Y - 2 * HALO) * levels)
-    field_shape = shaped(cols + 2 * HALO, field_rows, lanes)
-    out_shape = shaped(cols, rows * levels, lanes)
-    stage = (cols, BLOCK_Y * levels, lanes)
-    partial, field = pl.pallas_call(
-        functools.partial(middle_kernel, levels),
-        out_shape=(out_shape, field_shape),
-        in_specs=[VMEM] * 3 + [ANY] + [VMEM] * x_blocks,
-        out_specs=(HBM, VMEM),
+    bands = [band_of(block, second) for block in range(x_blocks)]
+
+    turned = pl.pallas_call(
+        functools.partial(turn_kernel, cols, width),
+        out_shape=shaped(eights(width * HALO), lanes),
+        in_specs=[VMEM] + [ANY] * x_blocks,
+        out_specs=VMEM,
+        name="turn",
+        compiler_params=grant(2),
+        cost_estimate=takes(0.1),
+    )(first_got, *bands)
+    turned_got = lax.ppermute(turned, "gx", partner)
+    inside = [(x, y) for y in range(1, y_blocks - 1) for x in range(x_blocks)]
+    edge = [(x, y) for y in (0, y_blocks - 1) for x in range(x_blocks)]
+    block_shape = (BLOCK_X, BLOCK_Y * levels, lanes)
+    middle = pl.pallas_call(
+        functools.partial(middle_kernel, levels, inside),
+        out_shape=(field_shape, shaped(len(inside), *block_shape)),
+        in_specs=[VMEM, VMEM, ANY] + [VMEM] * (1 + x_blocks),
+        out_specs=(VMEM, VMEM),
+        input_output_aliases={3: 0},
+        name="middle",
+        cost_estimate=takes(0.7),
+        compiler_params=grant(6),
+    )
+    field, done = middle(inner_got, outer_got, second, field, *bands)
+    _, updated = pl.pallas_call(
+        functools.partial(
+            edge_kernel, levels, cols, rows * levels, count, ends, run, edge, inside
+        ),
+        out_shape=(field_shape, shaped(cols, rows * levels, lanes)),
+        in_specs=[VMEM] * (7 + x_blocks),
+        out_specs=(VMEM, HBM),
         scratch_shapes=[
-            pltpu.VMEM((y_blocks - 2, *stage), F32),
-            pltpu.SemaphoreType.DMA((y_blocks - 2,)),
+            pltpu.VMEM((len(edge), *block_shape), F32),
+            pltpu.SemaphoreType.DMA((len(edge) + len(inside),)),
         ],
-        name="middle",
-        cost_estimate=takes(2.0),
+        input_output_aliases={6: 0},
+        name="edge",
+        cost_estimate=takes(1.0),
         compiler_params=grant(6),
-    )(cells, inner_got, outer_got, second, *bands)
-    _, updated = pl.pallas_call(
-        functools.partial(edge_kernel, levels, cols, rows * levels, count, ends, run),
-        out_shape=(field_shape, out_shape),
-        in_specs=[VMEM] * 5 + [HBM] + [VMEM] * x_blocks,
-        out_specs=(VMEM, HBM),
-        scratch_shapes=[pltpu.VMEM((2, *stage), F32), pltpu.SemaphoreType.DMA((2,))],
-        input_output_aliases={4: 0, 5: 1},
-        name="edge",
-        cost_estimate=takes(2.0),
-        compiler_params=grant(6),
-    )(table, first_got, second_got, ring, field, partial, *bands)
+    )(table, first_got, turned_got, second_got, ring, done, field, *bands)
     return updated.reshape(cols, rows, levels, lanes)
 
 

time: 16.2 us -> 15.1 us (0.932)
  waiting for transfers between devices: 2.95 us -> 1.87 us
  Pallas kernels: 5.93 us -> 5.6 us
  starting transfers between devices: 7.13 us -> 7.35 us
    ppermute x1, waiting for transfers between devices: 0.83 us -> 0.01 us  [on_device(): other = lax.ppermute(relay, 'gx', partner)]
    ppermute x1, waiting for transfers between devices: 1.24 us -> 0.44 us  [on_device(): second_got = lax.ppermute(second, axes, second_swap)]
    pallas_call x3 -> x4, Pallas kernels: 2.29 us -> 1.92 us  [the longest x1 1.45 us: on_device(): load(*[in_hbm(a) for a in (owner, codes, cells, weights, offsets, matrix)...]
    ppermute x1, waiting for transfers between devices: 0.33 us -> 0.53 us  [on_device(): outer_got = lax.ppermute(outer, 'gx', across)]
    ppermute x0 -> x1, waiting for transfers between devices: none -> 0.2 us  [on_device(): turned_got = lax.ppermute(turned, 'gx', partner)]
    ppermute x1, starting transfers between devices: 1.01 us -> 1.17 us  [on_device(): second_got = lax.ppermute(second, axes, second_swap)]
  transfers between devices with their start and end apart: 6 -> 7, of which waited for: 4 -> 4; matrix products, arithmetic and copies ran while one was open for 0% -> 0% of each run, Pallas kernels for 23% -> 23%
where the time goes in v5:
time: 15.1 us; the launch traced here: 14.9 us
  starting transfers between devices  7.35 us (49%)
  Pallas kernels  5.6 us (37%)
  waiting for transfers between devices  1.87 us (12%)
    ppermute x1, starting transfers between devices, on_device(): got = lax.ppermute(message, 'gx', across)  3.43 us
    ppermute x1, starting transfers between devices, on_device(): first_got = lax.ppermute(first, axes, first_swap)  2.46 us
    pallas_call x1, Pallas kernels, on_device(): load(*[in_hbm(a) for a in (owner, codes, cells, weights, offsets, matrix)...  1.45 us
    pallas_call x3, Pallas kernels, band_of(): pl.pallas_call(functools.partial(band_kernel, levels, rows, block), out_s...  1.34 us
    pallas_call x1, Pallas kernels, on_device(): pl.pallas_call(functools.partial(edge_kernel, levels, cols, rows * levels...  1.21 us
    ppermute x1, starting transfers between devices, on_device(): second_got = lax.ppermute(second, axes, second_swap)  1.17 us
    pallas_call x1, Pallas kernels, on_device(): pl.pallas_call(pack_kernel, out_shape=(shaped(2 * strip, lanes), shaped(e...  1.04 us
    ppermute x1, waiting for transfers between devices, on_device(): got = lax.ppermute(message, 'gx', across)  0.7 us
  transfers between devices with their start and end apart: 7, of which 4 were waited for; matrix products, arithmetic and copies ran while one was open for 0% of the time, Pallas kernels for 23%

profile of v5, /device:TPU:0, one launch (start us, length us, event | category | flops | bytes accessed | tf_op | source)
XLA Modules:
  0.0 14.9 jit_solution(8489791923535530506)
XLA Ops:
  0.0 1.0 %pack.1 = (f32[144,128]{1,0:T(8,128)S(1)}, f32[112,128]{1,0:T(8,128)S(1)}, f32[3,128,128]{2,1,0:T(8,128)S(1)}) custom-call(f32[12,128,128]{2,1,0:T(8,128)} %bitcast.4), custom_call_target="tpu_custom_call" | custom-call | bytes 3000000 | tf_op jit(solution)/shard_map/pack/pallas_call | solution.py:395
  1.0 3.4 %collective-permute-start = (f32[112,128]{1,0:T(8,128)S(1)}, f32[112,128]{1,0:T(8,128)S(1)}, u32[]{:S(2)}, u32[]{:S(2)}) collective-permute-start(f32[112,128]{1,0:T(8,128)S(1)} %get-tuple-element.19.after_ref.message_ref), channel_id=1, source_target_pairs={{0,28},{4,8},{8,4},{12,16},{16,12},{20,24},{24,20},{28,0},{1,29},{... | collective-permute-start | bytes 172040 | tf_op jit(solution)/shard_map/ppermute | solution.py:409
  4.5 0.1 collective-permute-start.6
  4.6 1.4 %load.1 = (s32[8,128]{1,0:T(8,128)S(1)}, f32[3,128,128]{2,1,0:T(8,128)S(1)}, f32[12,48,64]{2,1,0:T(8,128)S(1)}, s32[12,4,64]{2,1,0:T(4,128)S(1)}, bf16[104,512]{...) custom-call(s32[2,8]{1,0:T(2,128)} %owner_ref.1, s32[2,8]{1,0:T(2,128)} %codes_ref.1, f32[12,128,128]{2,1,0:T(8,128)} %bitcast.5, ...), custom_call_target="tpu_custom_call" | custom-call | bytes 3000000 | tf_op jit(solution)/shard_map/load/pallas_call | solution.py:439
  6.0 0.1 collective-permute-start.5
  6.1 0.7 %collective-permute-done.got_ref = f32[112,128]{1,0:T(8,128)S(1)} collective-permute-done((f32[112,128]{1,0:T(8,128)S(1)}, f32[112,128]{1,0:T(8,128)S(1)}, u32[]{:S(2)}, u32[]{:S(2)}) %collective-permute-start) | collective-permute-done | bytes 57376 | tf_op jit(solution)/shard_map/ppermute | solution.py:409
  6.8 0.1 collective-permute-start.2
  6.9 2.5 %collective-permute-start.1 = (f32[96,128]{1,0:T(8,128)S(1)}, f32[96,128]{1,0:T(8,128)S(1)}, u32[]{:S(2)}, u32[]{:S(2)}) collective-permute-start(f32[96,128]{1,0:T(8,128)S(1)} %get-tuple-element.22), channel_id=1, source_target_pairs={{0,1},{1,0},{2,3},{3,2},{4,5},{5,4},{6,7},{7,6},{8,9},{9,8},{10,11... | collective-permute-start | bytes 147464 | tf_op jit(solution)/shard_map/ppermute | solution.py:469
  9.3 0.0 collective-permute-done.2.other_ref
  9.4 0.1 rows.1.after_ref
  9.5 1.2 %collective-permute-start.4 = (f32[112,128]{1,0:T(8,128)S(1)}, f32[112,128]{1,0:T(8,128)S(1)}, u32[]{:S(2)}, u32[]{:S(2)}) collective-permute-start(f32[112,128]{1,0:T(8,128)S(1)} %rows.1.after_ref), channel_id=1, source_target_pairs={{0,16},{1,2},{2,1},{3,19},{4,20},{5,6},{6,5},{7,23},{8,24},{9,10},... | collective-permute-start | bytes 172040 | tf_op jit(solution)/shard_map/ppermute | solution.py:497
  10.6 0.4 %band.5.refs_2_ = bf16[8,128,256]{2,1,0:T(8,128)(2,1)S(1)} custom-call(f32[12,48,64]{2,1,0:T(8,128)S(1)} %get-tuple-element.23.weights_ref, s32[12,4,64]{2,1,0:T(4,128)S(1)} %get-tuple-element.24.offsets_ref, bf16[104,512]{1,0:T(8,128)(2,1)S(1)} %get-tuple-element.25.matrix_ref, f32[112,128]{1,0:T(8,128)S(1)} %rows.1.after_ref), custom_call_target="tpu_custom_call" | custom-call | bytes 1500000 | tf_op jit(solution)/shard_map/band/pallas_call | solution.py:446
  11.1 0.4 %band.4.refs_1_ = bf16[8,128,256]{2,1,0:T(8,128)(2,1)S(1)} custom-call(f32[12,48,64]{2,1,0:T(8,128)S(1)} %get-tuple-element.23.weights_ref, s32[12,4,64]{2,1,0:T(4,128)S(1)} %get-tuple-element.24.offsets_ref, bf16[104,512]{1,0:T(8,128)(2,1)S(1)} %get-tuple-element.25.matrix_ref, f32[112,128]{1,0:T(8,128)S(1)} %rows.1.after_ref), custom_call_target="tpu_custom_call" | custom-call | bytes 1500000 | tf_op jit(solution)/shard_map/band/pallas_call | solution.py:446
  11.5 0.4 %band.3.refs_0_ = bf16[8,128,256]{2,1,0:T(8,128)(2,1)S(1)} custom-call(f32[12,48,64]{2,1,0:T(8,128)S(1)} %get-tuple-element.23.weights_ref, s32[12,4,64]{2,1,0:T(4,128)S(1)} %get-tuple-element.24.offsets_ref, bf16[104,512]{1,0:T(8,128)(2,1)S(1)} %get-tuple-element.25.matrix_ref, f32[112,128]{1,0:T(8,128)S(1)} %rows.1.after_ref), custom_call_target="tpu_custom_call" | custom-call | bytes 1500000 | tf_op jit(solution)/shard_map/band/pallas_call | solution.py:446
  12.0 0.0 collective-permute-done.1.first_ref
  12.0 0.1 collective-permute-start.3
  12.1 0.5 %collective-permute-done.6.outer_ref = f32[3,128,128]{2,1,0:T(8,128)S(1)} collective-permute-done((f32[3,128,128]{2,1,0:T(8,128)S(1)}, f32[3,128,128]{2,1,0:T(8,128)S(1)}, u32[]{:S(2)}, u32[]{:S(2)}) %collective-permute-start.6) | collective-permute-done | bytes 196640 | tf_op jit(solution)/shard_map/ppermute | solution.py:410
  12.6 0.0 collective-permute-done.5.inner_ref
  12.6 0.4 %middle.1 = (f32[18,152,128]{2,1,0:T(8,128)S(1)}, f32[6,4,32,128]{3,2,1,0:T(8,128)S(1)}) custom-call(f32[3,128,128]{2,1,0:T(8,128)S(1)} %collective-permute-done.5.inner_ref, f32[3,128,128]{2,1,0:T(8,128)S(1)} %collective-permute-done.6.outer_ref, f32[112,128]{1,0:T(8,128)S(1)} %rows.1.after_ref, ...), custom_call_target="tpu_custom_call", output_to_operand_aliasing={{0}: (3, {})} | custom-call | bytes 2100000 | tf_op jit(solution)/shard_map/middle/pallas_call | solution.py:524
  13.1 0.2 %collective-permute-done.3.corner_ref = f32[24,128]{1,0:T(8,128)S(1)} collective-permute-done((f32[24,128]{1,0:T(8,128)S(1)}, f32[24,128]{1,0:T(8,128)S(1)}, u32[]{:S(2)}, u32[]{:S(2)}) %collective-permute-start.3) | collective-permute-done | bytes 12320 | tf_op jit(solution)/shard_map/ppermute | solution.py:510
  13.3 0.4 %collective-permute-done.4.second_ref = f32[112,128]{1,0:T(8,128)S(1)} collective-permute-done((f32[112,128]{1,0:T(8,128)S(1)}, f32[112,128]{1,0:T(8,128)S(1)}, u32[]{:S(2)}, u32[]{:S(2)}) %collective-permute-start.4) | collective-permute-done | bytes 57376 | tf_op jit(solution)/shard_map/ppermute | solution.py:497
  13.7 1.2 %edge.1 = (f32[18,152,128]{2,1,0:T(8,128)S(1)}, f32[12,128,128]{2,1,0:T(8,128)}) custom-call(s32[8,128]{1,0:T(8,128)S(1)} %get-tuple-element.20.after_ref.table_ref, f32[96,128]{1,0:T(8,128)S(1)} %collective-permute-done.1.first_ref, f32[24,128]{1,0:T(8,128)S(1)} %collective-permute-done.3.corner_ref, ...), custom_call_target="tpu_custom_call", output_to_operand_aliasing={{0}: (6, {})} | custom-call | bytes 3000000 | tf_op jit(solution)/shard_map/edge/pallas_call | solution.py:525
  (3 shorter events, 0.1 us)
Async XLA Ops:
  1.0 5.7 %collective-permute-start = (f32[112,128]{1,0:T(8,128)S(1)}, f32[112,128]{1,0:T(8,128)S(1)}, u32[]{:S(2)}, u32[]{:S(2)}) collective-permute-start(f32[112,128]{1,0:T(8,128)S(1)} %get-tuple-element.19.after_ref.message_ref), channel_id=1, source_target_pairs={{0,28},{4,8},{8,4},{12,16},{16,12},{20,24},{24,20},{28,0},{1,29},{... | collective-permute-start | bytes 172040 | tf_op jit(solution)/shard_map/ppermute | solution.py:409
  4.5 8.2 %collective-permute-start.6 = (f32[3,128,128]{2,1,0:T(8,128)S(1)}, f32[3,128,128]{2,1,0:T(8,128)S(1)}, u32[]{:S(2)}, u32[]{:S(2)}) collective-permute-start(f32[3,128,128]{2,1,0:T(8,128)S(1)} %get-tuple-element.28), channel_id=1, source_target_pairs={{0,28},{4,8},{8,4},{12,16},{16,12},{20,24},{24,20},{28,0},{1,29},{... | collective-permute-start | bytes 589832 | tf_op jit(solution)/shard_map/ppermute | solution.py:410
  6.0 6.6 %collective-permute-start.5 = (f32[3,128,128]{2,1,0:T(8,128)S(1)}, f32[3,128,128]{2,1,0:T(8,128)S(1)}, u32[]{:S(2)}, u32[]{:S(2)}) collective-permute-start(f32[3,128,128]{2,1,0:T(8,128)S(1)} %get-tuple-element.27), channel_id=1, source_target_pairs={{0,4},{4,0},{8,12},{12,8},{16,20},{20,16},{24,28},{28,24},{1,5},{5... | collective-permute-start | bytes 589832 | tf_op jit(solution)/shard_map/ppermute | solution.py:470
  6.8 2.5 %collective-permute-start.2 = (f32[184,128]{1,0:T(8,128)S(1)}, f32[184,128]{1,0:T(8,128)S(1)}, u32[]{:S(2)}, u32[]{:S(2)}) collective-permute-start(f32[184,128]{1,0:T(8,128)S(1)} %get-tuple-element.26.after_ref), channel_id=1, source_target_pairs={{0,4},{4,0},{8,12},{12,8},{16,20},{20,16},{24,28},{28,24},{1,5},{5... | collective-permute-start | bytes 282632 | tf_op jit(solution)/shard_map/ppermute | solution.py:468
  6.9 5.1 %collective-permute-start.1 = (f32[96,128]{1,0:T(8,128)S(1)}, f32[96,128]{1,0:T(8,128)S(1)}, u32[]{:S(2)}, u32[]{:S(2)}) collective-permute-start(f32[96,128]{1,0:T(8,128)S(1)} %get-tuple-element.22), channel_id=1, source_target_pairs={{0,1},{1,0},{2,3},{3,2},{4,5},{5,4},{6,7},{7,6},{8,9},{9,8},{10,11... | collective-permute-start | bytes 147464 | tf_op jit(solution)/shard_map/ppermute | solution.py:469
  9.5 4.2 %collective-permute-start.4 = (f32[112,128]{1,0:T(8,128)S(1)}, f32[112,128]{1,0:T(8,128)S(1)}, u32[]{:S(2)}, u32[]{:S(2)}) collective-permute-start(f32[112,128]{1,0:T(8,128)S(1)} %rows.1.after_ref), channel_id=1, source_target_pairs={{0,16},{1,2},{2,1},{3,19},{4,20},{5,6},{6,5},{7,23},{8,24},{9,10},... | collective-permute-start | bytes 172040 | tf_op jit(solution)/shard_map/ppermute | solution.py:497
  12.0 1.2 %collective-permute-start.3 = (f32[24,128]{1,0:T(8,128)S(1)}, f32[24,128]{1,0:T(8,128)S(1)}, u32[]{:S(2)}, u32[]{:S(2)}) collective-permute-start(f32[24,128]{1,0:T(8,128)S(1)} %turn.1), channel_id=1, source_target_pairs={{0,4},{4,0},{8,12},{12,8},{16,20},{20,16},{24,28},{28,24},{1,5},{5... | collective-permute-start | bytes 36872 | tf_op jit(solution)/shard_map/ppermute | solution.py:510

commit v6 on v5

--- a/solution.py
+++ b/solution.py
@@ -125,11 +125,13 @@
         column(block * BLOCK_X + step)
 
 
-def pack_kernel(cells_ref, edges_ref, message_ref, outer_ref, low_ref, high_ref, sems):
+def pack_kernel(ends, cells_ref, edges_ref, message_ref, outer_ref, low_ref, high_ref, sems):
     cols, rows, _ = cells_ref.shape
     width = edges_ref.shape[0] // cols // 2
     deep = low_ref.shape[1]
-    even, low = lax.axis_index("gx") % 2 == 0, lax.axis_index("gy") == 0
+    even, place = lax.axis_index("gx") % 2 == 0, lax.axis_index("gy")
+    low, up = place == 0, place % 2 == 0
+    is_end = jnp.logical_or(low, place == ends - 1)
     last = cols - HALO
     copies = [
         pltpu.make_async_copy(cells_ref.at[:, pl.ds(0, deep)], low_ref, sems.at[0]),
@@ -147,14 +149,15 @@
         bottom, top = low_ref[col, :width], high_ref[col, deep - width :]
         edges_ref[at : at + width] = bottom
         edges_ref[at + width : at + 2 * width] = top
-        message_ref[width * col : width * (col + 1)] = jnp.where(low, bottom, top)
-    at = width * cols
-    for col in range(HALO):
-        for ref in (low_ref.at[:, :width], high_ref.at[:, deep - width :]):
-            edge = jnp.where(even, ref[col], ref[last + col])
-            message_ref[at : at + width] = edge
-            at += width
-    clear(message_ref, at)
+        strip = jnp.where(low, bottom, top)
+        if col < HALO:
+            bottom = jnp.where(even, bottom, low_ref[last + col, :width])
+            top = jnp.where(even, top, high_ref[last + col, deep - width :])
+            message_ref[width * col : width * (col + 1)] = jnp.where(up, top, bottom)
+            strip = jnp.where(is_end, strip, jnp.where(up, bottom, top))
+        to = width * (HALO + col)
+        message_ref[to : to + width] = strip
+    clear(message_ref, width * (HALO + cols))
     copies[2].wait()
 
 
@@ -163,41 +166,68 @@
         ref[at:] = jnp.zeros((ref.shape[0] - at, LANES), F32)
 
 
-def relay_kernel(cols, width, edges_ref, message_ref, got_ref, after_ref, relay_ref, first_ref):
+def relay_kernel(cols, width, ends, edges_ref, message_ref, got_ref, after_ref, relay_ref,
+                 first_ref):
     del after_ref
-    even = lax.axis_index("gx") % 2 == 0
-    up = lax.axis_index("gy") % 2 == 0
-    corner, strip = 2 * width * HALO, width * cols
-    edges = 2 * strip
-    relay_ref[:corner] = jnp.where(even, edges_ref[edges - corner : edges], edges_ref[:corner])
-    relay_ref[corner : corner + strip] = message_ref[:strip]
-    relay_ref[corner + strip : corner + 2 * strip] = got_ref[:strip]
-    clear(relay_ref, corner + 2 * strip)
-    for u in range(HALO + cols):
-        ref, at = (got_ref, strip) if u < HALO else (edges_ref, -corner)
-        at += 2 * width * u
-        first_ref[u * width : (u + 1) * width] = jnp.where(
-            up, ref[at + width : at + 2 * width], ref[at : at + width]
+    even, place = lax.axis_index("gx") % 2 == 0, lax.axis_index("gy")
+    up = place % 2 == 0
+    is_end = jnp.logical_or(place == 0, place == ends - 1)
+    corner, strip = width * HALO, width * cols
+    relay_ref[:strip] = message_ref[corner : corner + strip]
+    relay_ref[strip : 2 * strip] = got_ref[corner : corner + strip]
+    for col in range(HALO):
+        left, right = 2 * width * col, 2 * width * (cols - HALO + col)
+        low = jnp.where(even, edges_ref[right : right + width], edges_ref[left : left + width])
+        left, right = left + width, right + width
+        high = jnp.where(even, edges_ref[right : right + width], edges_ref[left : left + width])
+        to = slice(width * col, width * (col + 1))
+        relay_ref[to] = jnp.where(is_end, relay_ref[to], jnp.where(up, low, high))
+    clear(relay_ref, 2 * strip)
+    first_ref[:corner] = got_ref[:corner]
+    for col in range(cols):
+        at = 2 * width * col
+        to = corner + width * col
+        first_ref[to : to + width] = jnp.where(
+            up, edges_ref[at + width : at + 2 * width], edges_ref[at : at + width]
         )
-    clear(first_ref, (HALO + cols) * width)
-
-
-def turn_kernel(cols, width, first_ref, *refs):
-    corner_ref = refs[-1]
-    even = lax.axis_index("gx") % 2 == 0
+    clear(first_ref, corner + strip)
+
+
+def turn_kernel(levels, cols, width, count, ends, run, first_ref, *refs):
+    run_ref, table_ref, corner_ref, glued_ref, mask_ref = refs[-5:]
+    even, place = lax.axis_index("gx") % 2 == 0, lax.axis_index("gy")
     size = HALO * width
     last = (HALO + cols) * width
     corner_ref[:size] = jnp.where(even, first_ref[last - size : last], first_ref[size : 2 * size])
     clear(corner_ref, size)
+    wide = cols + 2 * HALO
+    window = Window(cols, width, count, run, run_ref)
+    start, code = table_ref[1:2, 0:1][0, 0], table_ref[2:3, 0:1][0, 0]
+    is_end = jnp.logical_or(place == 0, place == ends - 1)
+    mirrored, flipped = code % 2 == 1, code // 2 % 2 == 1
+    for u in range(wide):
+        to = slice(width * u, width * (u + 1))
+        held, strip = window.column(start, jnp.where(mirrored, wide - 1 - u, u))
+        glued_ref[to] = jnp.where(flipped, turn_rows(strip, levels), strip)
+        mask_ref[to] = jnp.full(
+            (width, LANES), jnp.where(jnp.logical_and(is_end, held), 1.0, 0.0), F32
+        )
+    clear(glued_ref, wide * width)
+    clear(mask_ref, wide * width)
+
+
+def turn_rows(strip, levels):
+    return jnp.concatenate(
+        [strip[levels * r : levels * (r + 1)] for r in reversed(range(HALO))], axis=0
+    )
 
 
 def join_kernel(cols, width, message_ref, got_ref, other_ref, after_ref, run_ref):
     del after_ref
     even = lax.axis_index("gx") % 2 == 0
-    corner, strip = 2 * width * HALO, width * cols
-    mine, far = message_ref[:strip], got_ref[:strip]
-    near = other_ref[corner : corner + strip]
-    beyond = other_ref[corner + strip : corner + 2 * strip]
+    corner, strip = width * HALO, width * cols
+    mine, far = message_ref[corner : corner + strip], got_ref[corner : corner + strip]
+    near, beyond = other_ref[:strip], other_ref[strip : 2 * strip]
     pairs = ((far, beyond), (mine, near), (near, mine), (beyond, far))
     for at, (a, b) in enumerate(pairs):
         run_ref[at * strip : (at + 1) * strip] = jnp.where(even, a, b)
@@ -224,17 +254,16 @@
                 second_ref):
     even, place = lax.axis_index("gx") % 2 == 0, lax.axis_index("gy")
     top = place % 2 == 1
-    strip = width * cols
-
-    def rows(ref, at, top):
-        return jnp.where(top, ref[at + width : at + 2 * width], ref[at : at + width])
-
-    def column(u, top):
+
+    def column(u):
         if HALO <= u < HALO + cols:
-            return rows(edges_ref, 2 * width * (u - HALO), top)
+            at = 2 * width * (u - HALO)
+            return jnp.where(
+                top, edges_ref[at + width : at + 2 * width], edges_ref[at : at + width]
+            )
         col = u if u < HALO else u - HALO - cols
-        near = rows(other_ref, 2 * width * col, top)
-        far = rows(got_ref, strip + 2 * width * col, top)
+        near = other_ref[width * col : width * (col + 1)]
+        far = got_ref[width * (HALO + col) : width * (HALO + col + 1)]
         return jnp.where(even == (u < HALO), far, near)
 
     wide = cols + 2 * HALO
@@ -244,7 +273,7 @@
     for u in range(wide):
         to = slice(u * width, (u + 1) * width)
         _, glued = window.column(start, u)
-        second_ref[to] = jnp.where(is_end, glued, column(u, top))
+        second_ref[to] = jnp.where(is_end, glued, column(u))
     clear(second_ref, wide * width)
 
 
@@ -292,54 +321,66 @@
     remap_blocks(field_ref, bands, stage_ref, levels, blocks)
 
 
-def edge_kernel(levels, cols, rows, count, ends, run, blocks, done, table_ref, first_ref, corner_ref,
-                second_ref, run_ref, done_ref, field_in, *refs):
+def put_block(source, out_ref, sem, x, y):
+    _, deep, _ = source.shape
+    to = out_ref.at[pl.ds(x * BLOCK_X, BLOCK_X), pl.ds(pl.multiple_of(y * deep, deep), deep)]
+    copy = pltpu.make_async_copy(source, to, sem)
+    copy.start()
+    return copy
+
+
+def near_kernel(levels, cols, rows, first_ref, corner_ref, field_in, *refs):
     del field_in
-    *bands, field_ref, out_ref, stage_ref, sems = refs
-    deep = BLOCK_Y * levels
-    copies = []
-
-    def put(source, x, y):
-        to = out_ref.at[pl.ds(x * BLOCK_X, BLOCK_X), pl.ds(y * deep, deep)]
-        copies.append(pltpu.make_async_copy(source, to, sems.at[len(copies)]))
-        copies[-1].start()
-
-    for at, (x, y) in enumerate(done):
-        put(done_ref.at[at], x, y)
-    width = HALO * levels
-    lead = LEAD * levels
-    even, place = lax.axis_index("gx") % 2 == 0, lax.axis_index("gy")
-    flat_place = place % 2 == 0
-    wide = cols + 2 * HALO
-    window = Window(cols, width, count, run, run_ref)
-    start, code = table_ref[1:2, 0:1][0, 0], table_ref[2:3, 0:1][0, 0]
-    is_end = jnp.logical_or(place == 0, place == ends - 1)
-    mirrored = code % 2 == 1
-    flipped = code // 2 % 2 == 1
+    *bands, field_ref, stage_ref = refs
+    width, lead = HALO * levels, LEAD * levels
+    even, up = lax.axis_index("gx") % 2 == 0, lax.axis_index("gy") % 2 == 0
     tail = field_ref.shape[1] - lead - rows - width
-    for u in range(wide):
+    for u in range(cols + 2 * HALO):
         if HALO <= u < HALO + cols:
-            plain = first_ref[u * width : (u + 1) * width]
+            strip = first_ref[u * width : (u + 1) * width]
         else:
             col = u if u < HALO else u - HALO - cols
             far = first_ref[col * width : (col + 1) * width]
             near = corner_ref[col * width : (col + 1) * width]
-            plain = jnp.where(even == (u < HALO), far, near)
-        step = jnp.where(mirrored, wide - 1 - u, u)
-        held, glued = window.column(start, step)
-        come = second_ref[pl.ds(step * width, width)]
-        strip = jnp.where(jnp.logical_and(is_end, held), glued, come)
-        turned = jnp.concatenate(
-            [strip[levels * r : levels * (r + 1)] for r in reversed(range(HALO))], axis=0
-        )
-        strip = jnp.where(flipped, turned, strip)
-        field_ref[u, lead - width : lead] = jnp.where(flat_place, strip, plain)
-        field_ref[u, lead + rows : lead + rows + width] = jnp.where(flat_place, plain, strip)
+            strip = jnp.where(even == (u < HALO), far, near)
+        field_ref[u, lead - width : lead] = strip
+        field_ref[u, lead + rows : lead + rows + width] = strip
         field_ref[u, lead + rows + width :] = jnp.zeros((tail, LANES), F32)
-    remap_blocks(
-        field_ref, bands, stage_ref, levels, blocks,
-        lambda at, x, y: put(stage_ref.at[at], x, y),
-    )
+    last = rows // levels // BLOCK_Y - 1
+    blocks = [(x, jnp.where(up, last, 0)) for x in range(cols // BLOCK_X)]
+    remap_blocks(field_ref, bands, stage_ref, levels, blocks)
+
+
+def edge_kernel(levels, cols, rows, done, table_ref, second_ref, glued_ref, mask_ref, near_ref,
+                done_ref, field_in, *refs):
+    del field_in
+    *bands, field_ref, out_ref, stage_ref, sems = refs
+    last = rows // levels // BLOCK_Y - 1
+    up = lax.axis_index("gy") % 2 == 0
+    blocks = [(x, jnp.where(up, 0, last)) for x in range(cols // BLOCK_X)]
+    copies = []
+    ready = [(done_ref.at[at], x, y) for at, (x, y) in enumerate(done)]
+    ready += [(near_ref.at[x], x, last - y) for x, y in blocks]
+    for source, x, y in ready:
+        copies.append(put_block(source, out_ref, sems.at[len(copies)], x, y))
+
+    def put(at, x, y):
+        copies.append(put_block(stage_ref.at[at], out_ref, sems.at[len(copies)], x, y))
+
+    width, lead = HALO * levels, LEAD * levels
+    wide = cols + 2 * HALO
+    code = table_ref[2:3, 0:1][0, 0]
+    mirrored, flipped = code % 2 == 1, code // 2 % 2 == 1
+    for u in range(wide):
+        to = slice(width * u, width * (u + 1))
+        back = slice(width * (wide - 1 - u), width * (wide - u))
+        come = jnp.where(mirrored, second_ref[back], second_ref[to])
+        come = jnp.where(flipped, turn_rows(come, levels), come)
+        strip = jnp.where(mask_ref[to] > 0, glued_ref[to], come)
+        for at, mine in ((lead - width, up), (lead + rows, jnp.logical_not(up))):
+            old = field_ref[u, at : at + width]
+            field_ref[u, at : at + width] = jnp.where(mine, strip, old)
+    remap_blocks(field_ref, bands, stage_ref, levels, blocks, put)
     for copy in copies:
         copy.wait()
 
@@ -390,10 +431,10 @@
                 second_swap.append((i * ends + j, i * ends + (j + 1 if j % 2 else j - 1)))
 
     deep = eights(width)
-    strip, corner = width * cols, 2 * width * HALO
+    strip, corner = width * cols, width * HALO
     columns = shaped(HALO, rows * levels, lanes)
     edges, message, outer = pl.pallas_call(
-        pack_kernel,
+        functools.partial(pack_kernel, ends),
         out_shape=(shaped(2 * strip, lanes), shaped(eights(strip + corner), lanes), columns),
         in_specs=[HBM],
         out_specs=(VMEM, VMEM, VMEM),
@@ -453,10 +494,11 @@
             cost_estimate=takes(0.5),
         )(weights, offsets, matrix, after)
 
+    bands = [band_of(0, table)]
     relay, first = pl.pallas_call(
-        functools.partial(relay_kernel, cols, width),
+        functools.partial(relay_kernel, cols, width, ends),
         out_shape=(
-            shaped(eights(corner + 2 * strip), lanes),
+            shaped(eights(2 * strip), lanes),
             shaped(eights(width * (cols + HALO)), lanes),
         ),
         in_specs=[VMEM] * 3 + [ANY],
@@ -464,7 +506,7 @@
         name="relay",
         compiler_params=grant(2),
         cost_estimate=takes(0.5),
-    )(edges, message, got, table)
+    )(edges, message, got, bands[0])
     other = lax.ppermute(relay, "gx", partner)
     first_got = lax.ppermute(first, axes, first_swap)
     inner_got = lax.ppermute(inner, "gx", partner)
@@ -496,20 +538,19 @@
     )(table, edges, other, got, ring)
     second_got = lax.ppermute(second, axes, second_swap)
 
-    bands = [band_of(block, second) for block in range(x_blocks)]
-
-    turned = pl.pallas_call(
-        functools.partial(turn_kernel, cols, width),
-        out_shape=shaped(eights(width * HALO), lanes),
-        in_specs=[VMEM] + [ANY] * x_blocks,
-        out_specs=VMEM,
+    bands.extend(band_of(block, second) for block in range(1, x_blocks))
+
+    turned, glued, mask = pl.pallas_call(
+        functools.partial(turn_kernel, levels, cols, width, count, ends, run),
+        out_shape=(shaped(eights(width * HALO), lanes), shaped(z_rows, lanes), shaped(z_rows, lanes)),
+        in_specs=[VMEM] + [ANY] * x_blocks + [VMEM] * 2,
+        out_specs=(VMEM, VMEM, VMEM),
         name="turn",
         compiler_params=grant(2),
         cost_estimate=takes(0.1),
-    )(first_got, *bands)
+    )(first_got, *bands, ring, table)
     turned_got = lax.ppermute(turned, "gx", partner)
     inside = [(x, y) for y in range(1, y_blocks - 1) for x in range(x_blocks)]
-    edge = [(x, y) for y in (0, y_blocks - 1) for x in range(x_blocks)]
     block_shape = (BLOCK_X, BLOCK_Y * levels, lanes)
     middle = pl.pallas_call(
         functools.partial(middle_kernel, levels, inside),
@@ -522,22 +563,31 @@
         compiler_params=grant(6),
     )
     field, done = middle(inner_got, outer_got, second, field, *bands)
+    out_shape = shaped(cols, rows * levels, lanes)
+    field, near = pl.pallas_call(
+        functools.partial(near_kernel, levels, cols, rows * levels),
+        out_shape=(field_shape, shaped(x_blocks, *block_shape)),
+        in_specs=[VMEM] * (3 + x_blocks),
+        out_specs=(VMEM, VMEM),
+        input_output_aliases={2: 0},
+        name="near",
+        cost_estimate=takes(0.5),
+        compiler_params=grant(6),
+    )(first_got, turned_got, field, *bands)
     _, updated = pl.pallas_call(
-        functools.partial(
-            edge_kernel, levels, cols, rows * levels, count, ends, run, edge, inside
-        ),
-        out_shape=(field_shape, shaped(cols, rows * levels, lanes)),
+        functools.partial(edge_kernel, levels, cols, rows * levels, inside),
+        out_shape=(field_shape, out_shape),
         in_specs=[VMEM] * (7 + x_blocks),
         out_specs=(VMEM, HBM),
         scratch_shapes=[
-            pltpu.VMEM((len(edge), *block_shape), F32),
-            pltpu.SemaphoreType.DMA((len(edge) + len(inside),)),
+            pltpu.VMEM((x_blocks, *block_shape), F32),
+            pltpu.SemaphoreType.DMA((2 * x_blocks + len(inside),)),
         ],
         input_output_aliases={6: 0},
         name="edge",
         cost_estimate=takes(1.0),
         compiler_params=grant(6),
-    )(table, first_got, turned_got, second_got, ring, done, field, *bands)
+    )(table, second_got, glued, mask, near, done, field, *bands)
     return updated.reshape(cols, rows, levels, lanes)
 
 

time: 15.1 us -> 19 us (1.26)
  waiting for transfers between devices: 1.87 us -> 5.43 us
  Pallas kernels: 5.6 us -> 5.93 us
    ppermute x1, starting transfers between devices: 0.08 us -> 3.43 us  [on_device(): outer_got = lax.ppermute(outer, 'gx', across)]
    ppermute x1, waiting for transfers between devices: 0.7 us -> 3.84 us  [on_device(): got = lax.ppermute(message, 'gx', across)]
    ppermute x1, starting transfers between devices: 3.43 us -> 0.7 us  [on_device(): got = lax.ppermute(message, 'gx', across)]
    ppermute x1, waiting for transfers between devices: 0.01 us -> 0.54 us  [on_device(): first_got = lax.ppermute(first, axes, first_swap)]
    ppermute x1, waiting for transfers between devices: 0.53 us -> 0.01 us  [on_device(): outer_got = lax.ppermute(outer, 'gx', across)]
    ppermute x1, waiting for transfers between devices: 0.2 us -> 0.7 us  [on_device(): turned_got = lax.ppermute(turned, 'gx', partner)]
    pallas_call x3 -> x4, Pallas kernels: 1.08 us -> 1.48 us  [the longest x1 1.04 us: on_device(): pl.pallas_call(functools.partial(pack_kernel, ends), out_shape=(shaped(2...]
    ppermute x1, starting transfers between devices: 1.17 us -> 0.78 us  [on_device(): second_got = lax.ppermute(second, axes, second_swap)]
  transfers between devices with their start and end apart: 7 -> 7, of which waited for: 4 -> 4; matrix products, arithmetic and copies ran while one was open for 0% -> 0% of each run, Pallas kernels for 23% -> 20%
where the time goes in v6:
time: 19 us; the launch traced here: 18.9 us
  starting transfers between devices  7.41 us (39%)
  Pallas kernels  5.93 us (31%)
  waiting for transfers between devices  5.43 us (29%)
    ppermute x1, waiting for transfers between devices, on_device(): got = lax.ppermute(message, 'gx', across)  3.84 us
    ppermute x1, starting transfers between devices, on_device(): outer_got = lax.ppermute(outer, 'gx', across)  3.43 us
    ppermute x1, starting transfers between devices, on_device(): first_got = lax.ppermute(first, axes, first_swap)  2.29 us
    pallas_call x1, Pallas kernels, on_device(): load(*[in_hbm(a) for a in (owner, codes, cells, weights, offsets, matrix)...  1.45 us
    pallas_call x3, Pallas kernels, band_of(): pl.pallas_call(functools.partial(band_kernel, levels, rows, block), out_s...  1.33 us
    pallas_call x1, Pallas kernels, on_device(): pl.pallas_call(functools.partial(edge_kernel, levels, cols, rows * levels...  1.14 us
    pallas_call x1, Pallas kernels, on_device(): pl.pallas_call(functools.partial(pack_kernel, ends), out_shape=(shaped(2...  1.04 us
    ppermute x1, starting transfers between devices, on_device(): second_got = lax.ppermute(second, axes, second_swap)  0.78 us
  transfers between devices with their start and end apart: 7, of which 4 were waited for; matrix products, arithmetic and copies ran while one was open for 0% of the time, Pallas kernels for 20%

profile of v6, /device:TPU:0, one launch (start us, length us, event | category | flops | bytes accessed | tf_op | source)
XLA Modules:
  0.0 18.9 jit_solution(1997954525067738434)
XLA Ops:
  0.0 1.0 %pack.1 = (f32[144,128]{1,0:T(8,128)S(1)}, f32[96,128]{1,0:T(8,128)S(1)}, f32[3,128,128]{2,1,0:T(8,128)S(1)}) custom-call(f32[12,128,128]{2,1,0:T(8,128)} %bitcast.4), custom_call_target="tpu_custom_call" | custom-call | bytes 3000000 | tf_op jit(solution)/shard_map/pack/pallas_call | solution.py:436
  1.0 3.4 %collective-permute-start.6 = (f32[3,128,128]{2,1,0:T(8,128)S(1)}, f32[3,128,128]{2,1,0:T(8,128)S(1)}, u32[]{:S(2)}, u32[]{:S(2)}) collective-permute-start(f32[3,128,128]{2,1,0:T(8,128)S(1)} %get-tuple-element.36), channel_id=1, source_target_pairs={{0,28},{4,8},{8,4},{12,16},{16,12},{20,24},{24,20},{28,0},{1,29},{... | collective-permute-start | bytes 589832 | tf_op jit(solution)/shard_map/ppermute | solution.py:451
  4.5 1.4 %load.1 = (s32[8,128]{1,0:T(8,128)S(1)}, f32[3,128,128]{2,1,0:T(8,128)S(1)}, f32[12,48,64]{2,1,0:T(8,128)S(1)}, s32[12,4,64]{2,1,0:T(4,128)S(1)}, bf16[104,512]{...) custom-call(s32[2,8]{1,0:T(2,128)} %owner_ref.1, s32[2,8]{1,0:T(2,128)} %codes_ref.1, f32[12,128,128]{2,1,0:T(8,128)} %bitcast.5, ...), custom_call_target="tpu_custom_call" | custom-call | bytes 3000000 | tf_op jit(solution)/shard_map/load/pallas_call | solution.py:480
  5.9 0.1 collective-permute-start.5
  6.0 0.7 %collective-permute-start = (f32[96,128]{1,0:T(8,128)S(1)}, f32[96,128]{1,0:T(8,128)S(1)}, u32[]{:S(2)}, u32[]{:S(2)}) collective-permute-start(f32[96,128]{1,0:T(8,128)S(1)} %get-tuple-element.24.after_ref.message_ref), channel_id=1, source_target_pairs={{0,28},{4,8},{8,4},{12,16},{16,12},{20,24},{24,20},{28,0},{1,29},{... | collective-permute-start | bytes 147464 | tf_op jit(solution)/shard_map/ppermute | solution.py:450
  6.7 0.4 %band.3.after_ref.refs_0_ = bf16[8,128,256]{2,1,0:T(8,128)(2,1)S(1)} custom-call(f32[12,48,64]{2,1,0:T(8,128)S(1)} %get-tuple-element.27.weights_ref, s32[12,4,64]{2,1,0:T(4,128)S(1)} %get-tuple-element.28.offsets_ref, bf16[104,512]{1,0:T(8,128)(2,1)S(1)} %get-tuple-element.29.matrix_ref, s32[8,128]{1,0:T(8,128)S(1)} %get-tuple-element.25.after_ref.table_ref.refs_4_), custom_call_target="tpu_custom_call" | custom-call | bytes 1500000 | tf_op jit(solution)/shard_map/band/pallas_call | solution.py:487
  7.2 3.8 %collective-permute-done.got_ref = f32[96,128]{1,0:T(8,128)S(1)} collective-permute-done((f32[96,128]{1,0:T(8,128)S(1)}, f32[96,128]{1,0:T(8,128)S(1)}, u32[]{:S(2)}, u32[]{:S(2)}) %collective-permute-start) | collective-permute-done | bytes 49184 | tf_op jit(solution)/shard_map/ppermute | solution.py:450
  11.0 0.1 collective-permute-start.1
  11.1 2.3 %collective-permute-start.3 = (f32[96,128]{1,0:T(8,128)S(1)}, f32[96,128]{1,0:T(8,128)S(1)}, u32[]{:S(2)}, u32[]{:S(2)}) collective-permute-start(f32[96,128]{1,0:T(8,128)S(1)} %get-tuple-element.31), channel_id=1, source_target_pairs={{0,1},{1,0},{2,3},{3,2},{4,5},{5,4},{6,7},{7,6},{8,9},{9,8},{10,11... | collective-permute-start | bytes 147464 | tf_op jit(solution)/shard_map/ppermute | solution.py:511
  13.4 0.0 collective-permute-done.1.other_ref
  13.4 0.1 rows.1.after_ref
  13.5 0.8 %collective-permute-start.2 = (f32[112,128]{1,0:T(8,128)S(1)}, f32[112,128]{1,0:T(8,128)S(1)}, u32[]{:S(2)}, u32[]{:S(2)}) collective-permute-start(f32[112,128]{1,0:T(8,128)S(1)} %rows.1.after_ref), channel_id=1, source_target_pairs={{0,16},{1,2},{2,1},{3,19},{4,20},{5,6},{6,5},{7,23},{8,24},{9,10},... | collective-permute-start | bytes 172040 | tf_op jit(solution)/shard_map/ppermute | solution.py:539
  14.3 0.4 %band.5.refs_2_ = bf16[8,128,256]{2,1,0:T(8,128)(2,1)S(1)} custom-call(f32[12,48,64]{2,1,0:T(8,128)S(1)} %get-tuple-element.27.weights_ref, s32[12,4,64]{2,1,0:T(4,128)S(1)} %get-tuple-element.28.offsets_ref, bf16[104,512]{1,0:T(8,128)(2,1)S(1)} %get-tuple-element.29.matrix_ref, f32[112,128]{1,0:T(8,128)S(1)} %rows.1.after_ref), custom_call_target="tpu_custom_call" | custom-call | bytes 1500000 | tf_op jit(solution)/shard_map/band/pallas_call | solution.py:487
  14.7 0.4 %band.4.refs_1_ = bf16[8,128,256]{2,1,0:T(8,128)(2,1)S(1)} custom-call(f32[12,48,64]{2,1,0:T(8,128)S(1)} %get-tuple-element.27.weights_ref, s32[12,4,64]{2,1,0:T(4,128)S(1)} %get-tuple-element.28.offsets_ref, bf16[104,512]{1,0:T(8,128)(2,1)S(1)} %get-tuple-element.29.matrix_ref, f32[112,128]{1,0:T(8,128)S(1)} %rows.1.after_ref), custom_call_target="tpu_custom_call" | custom-call | bytes 1500000 | tf_op jit(solution)/shard_map/band/pallas_call | solution.py:487
  15.2 0.5 %collective-permute-done.3.first_ref = f32[96,128]{1,0:T(8,128)S(1)} collective-permute-done((f32[96,128]{1,0:T(8,128)S(1)}, f32[96,128]{1,0:T(8,128)S(1)}, u32[]{:S(2)}, u32[]{:S(2)}) %collective-permute-start.3) | collective-permute-done | bytes 49184 | tf_op jit(solution)/shard_map/ppermute | solution.py:511
  15.7 0.1 turn.1
  15.9 0.1 collective-permute-start.4
  15.9 0.0 collective-permute-done.6.outer_ref
  15.9 0.0 collective-permute-done.5.inner_ref
  16.0 0.4 %middle.1 = (f32[18,152,128]{2,1,0:T(8,128)S(1)}, f32[6,4,32,128]{3,2,1,0:T(8,128)S(1)}) custom-call(f32[3,128,128]{2,1,0:T(8,128)S(1)} %collective-permute-done.5.inner_ref, f32[3,128,128]{2,1,0:T(8,128)S(1)} %collective-permute-done.6.outer_ref, f32[112,128]{1,0:T(8,128)S(1)} %rows.1.after_ref, ...), custom_call_target="tpu_custom_call", output_to_operand_aliasing={{0}: (3, {})} | custom-call | bytes 2100000 | tf_op jit(solution)/shard_map/middle/pallas_call | solution.py:565
  16.4 0.7 %collective-permute-done.4.corner_ref = f32[24,128]{1,0:T(8,128)S(1)} collective-permute-done((f32[24,128]{1,0:T(8,128)S(1)}, f32[24,128]{1,0:T(8,128)S(1)}, u32[]{:S(2)}, u32[]{:S(2)}) %collective-permute-start.4) | collective-permute-done | bytes 12320 | tf_op jit(solution)/shard_map/ppermute | solution.py:552
  17.1 0.3 %near.1 = (f32[18,152,128]{2,1,0:T(8,128)S(1)}, f32[3,4,32,128]{3,2,1,0:T(8,128)S(1)}) custom-call(f32[96,128]{1,0:T(8,128)S(1)} %collective-permute-done.3.first_ref, f32[24,128]{1,0:T(8,128)S(1)} %collective-permute-done.4.corner_ref, f32[18,152,128]{2,1,0:T(8,128)S(1)} %get-tuple-element.38.field_in, ...), custom_call_target="tpu_custom_call", output_to_operand_aliasing={{0}: (2, {})} | custom-call | bytes 1500000 | tf_op jit(solution)/shard_map/near/pallas_call | solution.py:567
  17.4 0.3 %collective-permute-done.2.second_ref = f32[112,128]{1,0:T(8,128)S(1)} collective-permute-done((f32[112,128]{1,0:T(8,128)S(1)}, f32[112,128]{1,0:T(8,128)S(1)}, u32[]{:S(2)}, u32[]{:S(2)}) %collective-permute-start.2) | collective-permute-done | bytes 57376 | tf_op jit(solution)/shard_map/ppermute | solution.py:539
  17.7 1.1 %edge.1 = (f32[18,152,128]{2,1,0:T(8,128)S(1)}, f32[12,128,128]{2,1,0:T(8,128)}) custom-call(s32[8,128]{1,0:T(8,128)S(1)} %get-tuple-element.25.after_ref.table_ref.refs_4_, f32[112,128]{1,0:T(8,128)S(1)} %collective-permute-done.2.second_ref, f32[112,128]{1,0:T(8,128)S(1)} %get-tuple-element.32.glued_ref, ...), custom_call_target="tpu_custom_call", output_to_operand_aliasing={{0}: (6, {})} | custom-call | bytes 3000000 | tf_op jit(solution)/shard_map/edge/pallas_call | solution.py:577
  (2 shorter events, 0.0 us)
Async XLA Ops:
  1.0 14.9 %collective-permute-start.6 = (f32[3,128,128]{2,1,0:T(8,128)S(1)}, f32[3,128,128]{2,1,0:T(8,128)S(1)}, u32[]{:S(2)}, u32[]{:S(2)}) collective-permute-start(f32[3,128,128]{2,1,0:T(8,128)S(1)} %get-tuple-element.36), channel_id=1, source_target_pairs={{0,28},{4,8},{8,4},{12,16},{16,12},{20,24},{24,20},{28,0},{1,29},{... | collective-permute-start | bytes 589832 | tf_op jit(solution)/shard_map/ppermute | solution.py:451
  5.9 10.0 %collective-permute-start.5 = (f32[3,128,128]{2,1,0:T(8,128)S(1)}, f32[3,128,128]{2,1,0:T(8,128)S(1)}, u32[]{:S(2)}, u32[]{:S(2)}) collective-permute-start(f32[3,128,128]{2,1,0:T(8,128)S(1)} %get-tuple-element.35), channel_id=1, source_target_pairs={{0,4},{4,0},{8,12},{12,8},{16,20},{20,16},{24,28},{28,24},{1,5},{5... | collective-permute-start | bytes 589832 | tf_op jit(solution)/shard_map/ppermute | solution.py:512
  6.0 5.0 %collective-permute-start = (f32[96,128]{1,0:T(8,128)S(1)}, f32[96,128]{1,0:T(8,128)S(1)}, u32[]{:S(2)}, u32[]{:S(2)}) collective-permute-start(f32[96,128]{1,0:T(8,128)S(1)} %get-tuple-element.24.after_ref.message_ref), channel_id=1, source_target_pairs={{0,28},{4,8},{8,4},{12,16},{16,12},{20,24},{24,20},{28,0},{1,29},{... | collective-permute-start | bytes 147464 | tf_op jit(solution)/shard_map/ppermute | solution.py:450
  11.0 2.4 %collective-permute-start.1 = (f32[144,128]{1,0:T(8,128)S(1)}, f32[144,128]{1,0:T(8,128)S(1)}, u32[]{:S(2)}, u32[]{:S(2)}) collective-permute-start(f32[144,128]{1,0:T(8,128)S(1)} %get-tuple-element.30.after_ref), channel_id=1, source_target_pairs={{0,4},{4,0},{8,12},{12,8},{16,20},{20,16},{24,28},{28,24},{1,5},{5... | collective-permute-start | bytes 221192 | tf_op jit(solution)/shard_map/ppermute | solution.py:510
  11.1 4.6 %collective-permute-start.3 = (f32[96,128]{1,0:T(8,128)S(1)}, f32[96,128]{1,0:T(8,128)S(1)}, u32[]{:S(2)}, u32[]{:S(2)}) collective-permute-start(f32[96,128]{1,0:T(8,128)S(1)} %get-tuple-element.31), channel_id=1, source_target_pairs={{0,1},{1,0},{2,3},{3,2},{4,5},{5,4},{6,7},{7,6},{8,9},{9,8},{10,11... | collective-permute-start | bytes 147464 | tf_op jit(solution)/shard_map/ppermute | solution.py:511
  13.5 4.2 %collective-permute-start.2 = (f32[112,128]{1,0:T(8,128)S(1)}, f32[112,128]{1,0:T(8,128)S(1)}, u32[]{:S(2)}, u32[]{:S(2)}) collective-permute-start(f32[112,128]{1,0:T(8,128)S(1)} %rows.1.after_ref), channel_id=1, source_target_pairs={{0,16},{1,2},{2,1},{3,19},{4,20},{5,6},{6,5},{7,23},{8,24},{9,10},... | collective-permute-start | bytes 172040 | tf_op jit(solution)/shard_map/ppermute | solution.py:539
  15.9 1.2 %collective-permute-start.4 = (f32[24,128]{1,0:T(8,128)S(1)}, f32[24,128]{1,0:T(8,128)S(1)}, u32[]{:S(2)}, u32[]{:S(2)}) collective-permute-start(f32[24,128]{1,0:T(8,128)S(1)} %get-tuple-element.34), channel_id=1, source_target_pairs={{0,4},{4,0},{8,12},{12,8},{16,20},{20,16},{24,28},{28,24},{1,5},{5... | collective-permute-start | bytes 36872 | tf_op jit(solution)/shard_map/ppermute | solution.py:552
